TPU v7x, 32 devices: a whole 2x2x4 slice. The times are simulated.
32 devices in a mesh: groups: 2 (over y), col: 4 (over z), row: 2 (over x), head: 2 (over core).
Axes of the slice: x: 2, y: 2, z: 4, core: 2. Of those that a mesh axis runs over, the one named last changes fastest.
Arguments:
- pair: bfloat16 [4, 512, 128], P(('groups', 'row'), 'col'), parts along dimension 0, may hold values from -24 to 24
- out_grad: bfloat16 [4, 512, 128], P(('groups', 'row'), 'col'), parts along dimension 0, may hold values from -400 to 400
- pair_bias: bfloat16 [1024, 4, 512], P(('groups', 'col'), 'head'), parts along dimension 0, may hold values from -6 to 256
- w_query: bfloat16 [128, 128], P(None, 'head'), may hold values from -0.5 to 0.5
- w_key: bfloat16 [128, 128], P(None, 'head'), may hold values from -0.5 to 0.5
- w_value: bfloat16 [128, 128], P(None, 'head'), may hold values from -0.5 to 0.5
- w_gate: bfloat16 [128, 128], P(None, 'head'), may hold values from -0.5 to 0.5
- w_out: bfloat16 [128, 128], P('head'), may hold values from -0.5 to 0.5
- tile_mask: int32 [8, 4], P('groups'), parts along dimension 0, may hold values from 0 to 1, as said below
- chain_ids: int32 [1024], P('groups'), parts along dimension 0, may hold values from 0 to 7, never falling along the last dimension, each value on 1 to 128 neighbouring positions
Outputs:
- pair_grad: bfloat16 [4, 512, 128], P(('groups', 'row'), ('col', 'head')), parts along dimension 0
- query_weight_grad: float32 [256, 128], P('groups', 'head'), parts along dimension 0
- key_weight_grad: float32 [256, 128], P('groups', 'head'), parts along dimension 0
- value_weight_grad: float32 [256, 128], P('groups', 'head'), parts along dimension 0
- gate_weight_grad: float32 [256, 128], P('groups', 'head'), parts along dimension 0
- out_weight_grad: float32 [256, 128], P(('groups', 'head')), parts along dimension 0
There are 2 independent parts, one for each index of `groups`. A program takes and returns all parts, laid end to end along the dimension named above; an argument that names none is the same for every part. Nothing has to cross between parts.
Inputs may be any that keep to these rules, and one draw needn't show every extreme that they name: `tile_mask`: 1 where the residues of a query tile and a key tile, each of 128 residues, may attend to each other.
All inputs are finite; a program needn't handle non-finite values.
Results may differ from a plain program's by a relative error of at most 0.03.
The roundings to bfloat16 on the way count: a program that leaves them out, or rounds other values in their place, can miss the bound.
Values may be sent and summed in bfloat16 or wider, within the bound.
No kernel may reach another device: no remote copies, remote signals or barrier semaphores. Data moves between devices by JAX's collectives and lax.ppermute only.
A program may use at most 64 MiB of HBM per device.

v0:
```python
import math

import jax
import jax.numpy as jnp
from jax import lax
from jax.sharding import PartitionSpec as P

C = 128
H = 4
HD = 32
TILE = 128


NEG_FILL = -1e30


def shifted(value, axis, steps):
    count = lax.axis_size(axis)
    pairs = [(source, (source + steps) % count) for source in range(count)]
    return lax.ppermute(value, axis, pairs)


def allowed_between(tile_mask, chain_ids, query_start, query_count, key_start, key_count):
    tile_ids = jnp.arange(tile_mask.shape[0], dtype=jnp.int32)
    query_pos = query_start + jnp.arange(query_count, dtype=jnp.int32)
    key_pos = key_start + jnp.arange(key_count, dtype=jnp.int32)
    query_tiles = (query_pos[:, None] // TILE == tile_ids[None, :]).astype(jnp.float32)
    key_tiles = (key_pos[:, None] // TILE == tile_ids[None, :]).astype(jnp.float32)
    marks = jnp.dot(jnp.dot(query_tiles, tile_mask.astype(jnp.float32)), key_tiles.T)
    query_chain = lax.dynamic_slice_in_dim(chain_ids, query_start, query_count)
    key_chain = lax.dynamic_slice_in_dim(chain_ids, key_start, key_count)
    return (marks > 0.5) | (query_chain[:, None] == key_chain[None, :])


def score_block(query_four, key_four, bias_block, allowed):
    scores = jnp.einsum("rjhd,rkhd->rjhk", query_four, key_four, preferred_element_type=jnp.float32)
    scores = scores + bias_block[None].astype(jnp.float32)
    return jnp.where(allowed[None, :, None, :], scores, NEG_FILL)


def prob_and_grad(
    query_four, grad_four, log_total, delta_sum, key_four, value_four, bias_block, allowed
):
    scores = score_block(query_four, key_four, bias_block, allowed)
    prob = jnp.where(allowed[None, :, None, :], jnp.exp(scores - log_total[..., None]), 0.0)
    grad_prob = jnp.einsum(
        "rjhd,rkhd->rjhk", grad_four, value_four, preferred_element_type=jnp.float32
    )
    grad_score = (prob * (grad_prob - delta_sum[..., None])).astype(jnp.bfloat16)
    return (prob.astype(jnp.bfloat16), grad_score)


def per_device(
    pair, out_grad, pair_bias, w_query, w_key, w_value, w_gate, w_out, tile_mask, chain_ids
):
    rows_dev, cols_dev, channels = pair.shape
    heads_dev = pair_bias.shape[1]
    head_width = w_query.shape[1]
    head_size = head_width // heads_dev
    hd_scale = head_size ** (-0.5)
    col_count = lax.axis_size("col")
    col_index = lax.axis_index("col")
    col_start = col_index * cols_dev
    shape_four = (rows_dev, cols_dev, heads_dev, head_size)
    stat_shape = (rows_dev, cols_dev, heads_dev)
    flat_pair = pair.reshape(rows_dev * cols_dev, channels)
    flat_grad = out_grad.reshape(rows_dev * cols_dev, channels)
    w_joined = jnp.concatenate([w_query, w_key, w_value, w_gate], axis=1)
    projected = jnp.dot(flat_pair, w_joined, preferred_element_type=jnp.float32)
    query_flat = (projected[:, :head_width] * hd_scale).astype(jnp.bfloat16)
    key_grid = (
        projected[:, head_width : 2 * head_width]
        .astype(jnp.bfloat16)
        .reshape(rows_dev, cols_dev, head_width)
    )
    value_grid = (
        projected[:, 2 * head_width : 3 * head_width]
        .astype(jnp.bfloat16)
        .reshape(rows_dev, cols_dev, head_width)
    )
    gate_value = jax.nn.sigmoid(projected[:, 3 * head_width :])
    query_four = query_flat.reshape(shape_four)
    key_piece = lax.all_gather(key_grid, "col", axis=1, tiled=True)
    value_piece = lax.all_gather(value_grid, "col", axis=1, tiled=True)
    key_count = key_piece.shape[1]
    allowed = allowed_between(tile_mask, chain_ids, col_start, cols_dev, jnp.int32(0), key_count)
    bias_block = pair_bias
    run_max = jnp.full(stat_shape, NEG_FILL, jnp.float32)
    key_four = key_piece.reshape(rows_dev, key_count, heads_dev, head_size)
    value_four = value_piece.reshape(rows_dev, key_count, heads_dev, head_size)
    scores = score_block(query_four, key_four, bias_block, allowed)
    new_max = jnp.maximum(run_max, jnp.max(scores, axis=3))
    weights = jnp.where(allowed[None, :, None, :], jnp.exp(scores - new_max[..., None]), 0.0)
    new_sum = jnp.sum(weights, axis=3)
    added = jnp.einsum(
        "rjhk,rkhd->rjhd",
        weights.astype(jnp.bfloat16),
        value_four,
        preferred_element_type=jnp.float32,
    )
    attended = (added / new_sum[..., None]).reshape(rows_dev * cols_dev, head_width)
    log_total = new_max + jnp.log(new_sum)
    gated = (gate_value * attended).astype(jnp.bfloat16)
    grad_gated = jnp.dot(flat_grad, w_out.T, preferred_element_type=jnp.float32)
    grad_att = (grad_gated * gate_value).astype(jnp.bfloat16)
    grad_gate_logit = (grad_gated * attended * gate_value * (1.0 - gate_value)).astype(jnp.bfloat16)
    delta_sum = jnp.sum((grad_att.astype(jnp.float32) * attended).reshape(shape_four), axis=3)
    grad_four = grad_att.reshape(shape_four)

    def back_turn(turn_index, loop_state):
        travel_keys, travel_grads, query_acc = loop_state
        owner_col = jnp.mod(col_index - turn_index, col_count)
        key_start = owner_col * cols_dev
        allowed = allowed_between(tile_mask, chain_ids, col_start, cols_dev, key_start, cols_dev)
        bias_block = lax.dynamic_slice_in_dim(pair_bias, key_start, cols_dev, 2)
        grads_in = travel_grads
        query_in = query_acc
        key_four = travel_keys[0].reshape(shape_four)
        value_four = travel_keys[1].reshape(shape_four)
        prob_bf, grad_score = prob_and_grad(
            query_four, grad_four, log_total, delta_sum, key_four, value_four, bias_block, allowed
        )
        query_more = jnp.einsum(
            "rjhk,rkhd->rjhd", grad_score, key_four, preferred_element_type=jnp.float32
        )
        key_more = jnp.einsum(
            "rjhk,rjhd->rkhd", grad_score, query_four, preferred_element_type=jnp.float32
        )
        value_more = jnp.einsum(
            "rjhk,rjhd->rkhd", prob_bf, grad_four, preferred_element_type=jnp.float32
        )
        travel_grads = grads_in + jnp.stack([key_more, value_more]).reshape(grads_in.shape)
        query_acc = query_in + query_more
        travel_keys = shifted(travel_keys, "col", 1)
        travel_grads = shifted(travel_grads.astype(jnp.bfloat16), "col", 1).astype(
            travel_grads.dtype
        )
        return (travel_keys, travel_grads, query_acc)

    def back_pair(pair_index, loop_state):
        for half_turn in range(2):
            loop_state = back_turn(2 * pair_index + half_turn, loop_state)
        return loop_state

    loop_start = (
        jnp.stack([key_grid, value_grid]),
        jnp.zeros((2, rows_dev, cols_dev, head_width), jnp.float32),
        jnp.zeros(shape_four, jnp.float32),
    )
    travel_keys, key_value_acc, query_acc = lax.fori_loop(0, col_count // 2, back_pair, loop_start)
    query_grad = (
        (query_acc * hd_scale).astype(jnp.bfloat16).reshape(rows_dev * cols_dev, head_width)
    )
    key_grad = key_value_acc[0].astype(jnp.bfloat16).reshape(rows_dev * cols_dev, head_width)
    value_grad = key_value_acc[1].astype(jnp.bfloat16).reshape(rows_dev * cols_dev, head_width)
    grad_joined = jnp.concatenate([query_grad, key_grad, value_grad, grad_gate_logit], axis=1)
    partial_pair = jnp.dot(grad_joined, w_joined.T, preferred_element_type=jnp.float32).reshape(
        rows_dev, cols_dev, channels
    )
    pair_grad = lax.psum_scatter(
        partial_pair.astype(jnp.bfloat16), "head", scatter_dimension=1, tiled=True
    )
    raw_four = jnp.dot(flat_pair.T, grad_joined, preferred_element_type=jnp.float32)
    raw_out = jnp.dot(gated.T, flat_grad, preferred_element_type=jnp.float32)
    summed_four, summed_out = lax.psum((raw_four, raw_out), ("col", "row"))
    local_squares = jnp.sum(summed_four * summed_four) + jnp.sum(summed_out * summed_out)
    squares = lax.psum(local_squares, "head")
    clip = jnp.minimum(1.0, 0.5 * math.sqrt(5.0 * C * H * HD) / jnp.sqrt(squares + 1e-06))
    return (
        pair_grad,
        summed_four[:, :head_width] * clip,
        summed_four[:, head_width : 2 * head_width] * clip,
        summed_four[:, 2 * head_width : 3 * head_width] * clip,
        summed_four[:, 3 * head_width :] * clip,
        summed_out * clip,
    )


def solution(mesh):
    return jax.shard_map(
        per_device,
        mesh=mesh,
        in_specs=(
            P(("groups", "row"), "col", None),
            P(("groups", "row"), "col", None),
            P(("groups", "col"), "head", None),
            P(None, "head"),
            P(None, "head"),
            P(None, "head"),
            P(None, "head"),
            P("head", None),
            P("groups", None),
            P("groups"),
        ),
        out_specs=(
            P(("groups", "row"), ("col", "head"), None),
            P("groups", "head"),
            P("groups", "head"),
            P("groups", "head"),
            P("groups", "head"),
            P(("groups", "head"), None),
        ),
        check_vma=False,
    )
```

profile of v0, /device:TPU:0, one launch (start us, length us, event | category | flops | bytes accessed | tf_op | source)
XLA Modules:
  0.0 155.0 jit_solution(3555819905112902982)
XLA Ops:
  8.1 0.7 copy-done.9
  8.8 0.7 copy-done.8
  10.6 0.7 copy-done.5
  11.4 0.7 copy-done.6
  12.1 0.7 copy-done.7
  13.0 13.7 %all-gather = bf16[512,64]{0,1:T(8,128)(2,1)S(1)} all-gather(bf16[128,64]{0,1:T(8,128)(2,1)S(1)} %get-tuple-element.488), channel_id=2, replica_groups=mesh['groups'=2,'col'=4,'row'=2,'head'=2] {'col'}, dimensions={0}, use_global_device_ids=true | all-gather | bytes 81920 | tf_op jit(solution)/shard_map/all_gather | solution.py:83
  27.2 12.0 %all-gather.1 = bf16[512,64]{0,1:T(8,128)(2,1)S(1)} all-gather(bf16[128,64]{0,1:T(8,128)(2,1)S(1)} %get-tuple-element.487), channel_id=3, replica_groups=mesh['groups'=2,'col'=4,'row'=2,'head'=2] {'col'}, dimensions={0}, use_global_device_ids=true | all-gather | bytes 81920 | tf_op jit(solution)/shard_map/all_gather | solution.py:84
  40.3 27.4 %while.21 = (s32[]{:T(128)}, bf16[2,1,128,64]{2,3,1,0:T(8,128)(2,1)S(1)}, f32[2,1,128,64]{2,3,1,0:T(8,128)S(1)}, f32[1,128,2,32]{1,3,2,0:T(8,128)S(1)}, s32[]{:T...) while((s32[]{:T(128)}, ...), condition=%wide.region_4.5_spmd.clone, body=%wide.region_3.4_spmd.clone.sunk | while | flops 22105636 | bytes 2997002 | solution.py:150
  42.4 1.0 collective-permute-start.2
  43.9 2.3 %collective-permute-done = bf16[2,1,128,64]{2,3,1,0:T(8,128)(2,1)S(1)} collective-permute-done((bf16[2,1,128,64]{2,3,1,0:T(8,128)(2,1)S(1)}, bf16[2,1,128,64]{2,3,1,0:T(8,128)(2,1)S(1)}, u32[]{:S(2)}, u32[]{:S(2)}) %collective-permute-start) | collective-permute-done | bytes 32800 | tf_op jit(solution)/shard_map/while/body/eval_jaxpr/ppermute | solution.py:20
  46.9 1.2 collective-permute-done.2
  48.7 5.3 %collective-permute-done.3 = bf16[2,1,128,64]{2,3,1,0:T(8,128)(2,1)S(1)} collective-permute-done((bf16[2,1,128,64]{2,3,1,0:T(8,128)(2,1)S(1)}, bf16[2,1,128,64]{2,3,1,0:T(8,128)(2,1)S(1)}, u32[]{:S(2)}, u32[]{:S(2)}) %collective-permute-start.3) | collective-permute-done | bytes 32800 | tf_op jit(solution)/shard_map/while/body/eval_jaxpr/ppermute | solution.py:20
  56.9 3.1 %collective-permute-done = bf16[2,1,128,64]{2,3,1,0:T(8,128)(2,1)S(1)} collective-permute-done((bf16[2,1,128,64]{2,3,1,0:T(8,128)(2,1)S(1)}, bf16[2,1,128,64]{2,3,1,0:T(8,128)(2,1)S(1)}, u32[]{:S(2)}, u32[]{:S(2)}) %collective-permute-start) | collective-permute-done | bytes 32800 | tf_op jit(solution)/shard_map/while/body/eval_jaxpr/ppermute | solution.py:20
  60.8 0.8 collective-permute-done.2
  61.7 1.0 collective-permute-start.1
  62.8 4.6 %collective-permute-done.3 = bf16[2,1,128,64]{2,3,1,0:T(8,128)(2,1)S(1)} collective-permute-done((bf16[2,1,128,64]{2,3,1,0:T(8,128)(2,1)S(1)}, bf16[2,1,128,64]{2,3,1,0:T(8,128)(2,1)S(1)}, u32[]{:S(2)}, u32[]{:S(2)}) %collective-permute-start.3) | collective-permute-done | bytes 32800 | tf_op jit(solution)/shard_map/while/body/eval_jaxpr/ppermute | solution.py:20
  67.7 0.8 convolution_bitcast_fusion.7
  68.8 35.6 %psum.22 = f32[64,128]{1,0:T(8,128)S(1)} all-reduce(f32[64,128]{1,0:T(8,128)S(1)} %fusion.69), channel_id=1, replica_groups=mesh['groups'=2,'col'=4,'row'=2,'head'=2] {'col','row'}, use_global_device_ids=true, to_apply=%region_8.9 | all-reduce | flops 8192 | bytes 65536 | tf_op jit(solution)/shard_map/psum | solution.py:165
  104.9 0.8 fusion.51
  105.7 32.1 %all-reduce.2.cloned.1.call-done = f32[128,256]{0,1:T(8,128)} async-done(((f32[128,256]{0,1:T(8,128)}), f32[128,256]{0,1:T(8,128)}) %all-reduce.2.cloned.1.call-update) | async-done | bytes 131088 | tf_op jit(solution)/shard_map/psum | solution.py:165
  137.8 1.6 %multiply_reduce_fusion = f32[]{:T(128)} fusion(f32[128,256]{0,1:T(8,128)} %all-reduce.2.cloned.1.call-done), kind=kLoop, calls=%fused_computation.89 | loop fusion | flops 65535 | bytes 131076 | tf_op jit(solution)/shard_map/reduce_sum | solution.py:166
  140.8 3.0 %psum.23 = f32[]{:T(128)} all-reduce(f32[]{:T(128)S(6)} %add.317), channel_id=1, replica_groups=mesh['groups'=2,'col'=4,'row'=2,'head'=2] {'head'}, use_global_device_ids=true, to_apply=%region_10.11 | all-reduce | flops 1 | bytes 8 | tf_op jit(solution)/shard_map/psum | solution.py:167
  144.4 0.7 slice_multiply_fusion
  145.7 1.8 %reduce-scatter.2.cloned.1.call-done = bf16[1,64,128]{2,1,0:T(8,128)(2,1)} async-done(((bf16[1,128,128]{2,1,0:T(8,128)(2,1)}), bf16[1,64,128]{2,1,0:T(8,128)(2,1)}) %reduce-scatter.2.cloned.1.call-update) | async-done | bytes 16400 | tf_op jit(solution)/shard_map/reduce_scatter | solution.py:160
  (103 shorter events, 12.4 us)
Async XLA Ops:
  8.0 4.8 %copy-start = (bf16[1,128,128]{2,1,0:T(8,128)(2,1)S(1)}, bf16[1,128,128]{2,1,0:T(8,128)(2,1)}, u32[]{:S(2)}) copy-start(bf16[1,128,128]{2,1,0:T(8,128)(2,1)} %param.12) | copy-start | bytes 98308
  8.0 129.8 %all-reduce.2.cloned.1.call-start = ((), (), s32[]{:S(2)}) async-start(), calls=%async_computation.2 | async-start | bytes 262144 | tf_op jit(solution)/shard_map/psum | solution.py:165
  8.1 0.7 copy-start.9
  8.8 0.7 copy-start.8
  9.9 0.7 copy-start.4
  10.6 0.7 copy-start.5
  11.4 0.7 copy-start.6
  12.1 0.7 copy-start.7
  12.8 13.9 %copy-start.2 = (bf16[128,2,512]{2,1,0:T(2,128)(2,1)S(1)}, bf16[128,2,512]{2,1,0:T(2,128)(2,1)}, u32[]{:S(2)}) copy-start(bf16[128,2,512]{2,1,0:T(2,128)(2,1)} %param.14) | copy-start | bytes 786436
  39.3 0.8 copy-start.3
  39.3 0.8 copy-start.10
  40.3 5.9 %collective-permute-start = (bf16[2,1,128,64]{2,3,1,0:T(8,128)(2,1)S(1)}, bf16[2,1,128,64]{2,3,1,0:T(8,128)(2,1)S(1)}, u32[]{:S(2)}, u32[]{:S(2)}) collective-permute-start(bf16[2,1,128,64]{2,3,1,0:T(8,128)(2,1)S(1)} %get-tuple-element.621), channel_id=1, source_target_pairs={{0,4},{4,8},{8,12},{12,0},{1,5},{5,9},{9,13},{13,1},{2,6},{6,10},{... | collective-permute-start | bytes 98312 | tf_op jit(solution)/shard_map/while/body/eval_jaxpr/ppermute | solution.py:20
  42.4 5.8 %collective-permute-start.2 = (bf16[2,1,128,64]{2,3,1,0:T(8,128)(2,1)S(1)}, bf16[2,1,128,64]{2,3,1,0:T(8,128)(2,1)S(1)}, u32[]{:S(2)}, u32[]{:S(2)}) collective-permute-start(bf16[2,1,128,64]{2,3,1,0:T(8,128)(2,1)S(1)} %fusion.188), channel_id=1, source_target_pairs={{0,4},{4,8},{8,12},{12,0},{1,5},{5,9},{9,13},{13,1},{2,6},{6,10},{... | collective-permute-start | bytes 98312 | tf_op jit(solution)/shard_map/while/body/eval_jaxpr/ppermute | solution.py:20
  48.2 5.8 %collective-permute-start.3 = (bf16[2,1,128,64]{2,3,1,0:T(8,128)(2,1)S(1)}, bf16[2,1,128,64]{2,3,1,0:T(8,128)(2,1)S(1)}, u32[]{:S(2)}, u32[]{:S(2)}) collective-permute-start(bf16[2,1,128,64]{2,3,1,0:T(8,128)(2,1)S(1)} %fusion.189), channel_id=1, source_target_pairs={{0,4},{4,8},{8,12},{12,0},{1,5},{5,9},{9,13},{13,1},{2,6},{6,10},{... | collective-permute-start | bytes 98312 | tf_op jit(solution)/shard_map/while/body/eval_jaxpr/ppermute | solution.py:20
  48.2 6.0 %collective-permute-start.1 = (bf16[2,1,128,64]{2,3,1,0:T(8,128)(2,1)S(1)}, bf16[2,1,128,64]{2,3,1,0:T(8,128)(2,1)S(1)}, u32[]{:S(2)}, u32[]{:S(2)}) collective-permute-start(bf16[2,1,128,64]{2,3,1,0:T(8,128)(2,1)S(1)} %collective-permute-done), channel_id=1, source_target_pairs={{0,4},{4,8},{8,12},{12,0},{1,5},{5,9},{9,13},{13,1},{2,6},{6,10},{... | collective-permute-start | bytes 98312 | tf_op jit(solution)/shard_map/while/body/eval_jaxpr/ppermute | solution.py:20
  54.3 5.7 %collective-permute-start = (bf16[2,1,128,64]{2,3,1,0:T(8,128)(2,1)S(1)}, bf16[2,1,128,64]{2,3,1,0:T(8,128)(2,1)S(1)}, u32[]{:S(2)}, u32[]{:S(2)}) collective-permute-start(bf16[2,1,128,64]{2,3,1,0:T(8,128)(2,1)S(1)} %get-tuple-element.621), channel_id=1, source_target_pairs={{0,4},{4,8},{8,12},{12,0},{1,5},{5,9},{9,13},{13,1},{2,6},{6,10},{... | collective-permute-start | bytes 98312 | tf_op jit(solution)/shard_map/while/body/eval_jaxpr/ppermute | solution.py:20
  55.8 5.8 %collective-permute-start.2 = (bf16[2,1,128,64]{2,3,1,0:T(8,128)(2,1)S(1)}, bf16[2,1,128,64]{2,3,1,0:T(8,128)(2,1)S(1)}, u32[]{:S(2)}, u32[]{:S(2)}) collective-permute-start(bf16[2,1,128,64]{2,3,1,0:T(8,128)(2,1)S(1)} %fusion.188), channel_id=1, source_target_pairs={{0,4},{4,8},{8,12},{12,0},{1,5},{5,9},{9,13},{13,1},{2,6},{6,10},{... | collective-permute-start | bytes 98312 | tf_op jit(solution)/shard_map/while/body/eval_jaxpr/ppermute | solution.py:20
  61.6 5.8 %collective-permute-start.3 = (bf16[2,1,128,64]{2,3,1,0:T(8,128)(2,1)S(1)}, bf16[2,1,128,64]{2,3,1,0:T(8,128)(2,1)S(1)}, u32[]{:S(2)}, u32[]{:S(2)}) collective-permute-start(bf16[2,1,128,64]{2,3,1,0:T(8,128)(2,1)S(1)} %fusion.189), channel_id=1, source_target_pairs={{0,4},{4,8},{8,12},{12,0},{1,5},{5,9},{9,13},{13,1},{2,6},{6,10},{... | collective-permute-start | bytes 98312 | tf_op jit(solution)/shard_map/while/body/eval_jaxpr/ppermute | solution.py:20
  61.7 6.0 %collective-permute-start.1 = (bf16[2,1,128,64]{2,3,1,0:T(8,128)(2,1)S(1)}, bf16[2,1,128,64]{2,3,1,0:T(8,128)(2,1)S(1)}, u32[]{:S(2)}, u32[]{:S(2)}) collective-permute-start(bf16[2,1,128,64]{2,3,1,0:T(8,128)(2,1)S(1)} %collective-permute-done), channel_id=1, source_target_pairs={{0,4},{4,8},{8,12},{12,0},{1,5},{5,9},{9,13},{13,1},{2,6},{6,10},{... | collective-permute-start | bytes 98312 | tf_op jit(solution)/shard_map/while/body/eval_jaxpr/ppermute | solution.py:20
  68.6 79.0 %reduce-scatter.2.cloned.1.call-start = ((), (), s32[]{:S(2)}) async-start(), calls=%async_computation.1 | async-start | bytes 49152 | tf_op jit(solution)/shard_map/reduce_scatter | solution.py:160
  137.8 6.6 %copy-start.1 = (f32[128,256]{0,1:T(8,128)S(1)}, f32[128,256]{0,1:T(8,128)}, u32[]{:S(2)}) copy-start(f32[128,256]{0,1:T(8,128)} %all-reduce.2.cloned.1.call-done) | copy-start | bytes 393220
Sparse Core Ops, SparseCore 0:
  68.7 69.0 all-reduce.1
Sparse Core Ops, SparseCore 1:
  140.8 6.6 reduce-scatter.1
where the time goes:
time: 156 us; the launch traced here: 155 us
  blocking collectives  64.2 us (41%)
  waiting for transfers between devices  51.9 us (33%)
  between operations  17.7 us (11%)
  matrix products  7.86 us (5%)
  local copies, waits for them, and re-layouts  5.54 us (4%)
  other arithmetic  3.99 us (3%)
  starting transfers between devices  3.59 us (2%)
    psum x1, blocking collectives, per_device(): summed_four, summed_out = lax.psum((raw_four, raw_out), ('col', 'row'))  35.6 us
    psum x1, waiting for transfers between devices, per_device(): summed_four, summed_out = lax.psum((raw_four, raw_out), ('col', 'row'))  32.1 us
    ppermute x8, waiting for transfers between devices, shifted(): return lax.ppermute(value, axis, pairs)  18 us
    all_gather x1, blocking collectives, per_device(): key_piece = lax.all_gather(key_grid, 'col', axis=1, tiled=True)  13.7 us
    all_gather x1, blocking collectives, per_device(): value_piece = lax.all_gather(value_grid, 'col', axis=1, tiled=True)  12 us
    unnamed x26, local copies, waits for them, and re-layouts  4.79 us
    ppermute x8, starting transfers between devices, shifted(): return lax.ppermute(value, axis, pairs)  3.5 us
  transfers between devices with their start and end apart: 10, of which 10 were waited for; matrix products, arithmetic and copies ran while one was open for 5% of the time, Pallas kernels for 0%

commit v1 on v0

--- a/solution.py
+++ b/solution.py
@@ -3,6 +3,8 @@
 import jax
 import jax.numpy as jnp
 from jax import lax
+from jax.experimental import pallas as pl
+from jax.experimental.pallas import tpu as pltpu
 from jax.sharding import PartitionSpec as P
 
 C = 128
@@ -12,7 +14,9 @@
 
 
 NEG_FILL = -1e30
-
+F32 = jnp.float32
+BF16 = jnp.bfloat16
+CLIP_NORM = 0.5 * math.sqrt(5.0 * C * H * HD)
 
 def shifted(value, axis, steps):
     count = lax.axis_size(axis)
@@ -50,7 +54,7 @@
     return (prob.astype(jnp.bfloat16), grad_score)
 
 
-def per_device(
+def any_cols(
     pair, out_grad, pair_bias, w_query, w_key, w_value, w_gate, w_out, tile_mask, chain_ids
 ):
     rows_dev, cols_dev, channels = pair.shape
@@ -176,6 +180,216 @@
     )
 
 
+def crossed(value, axis, bits):
+    count = lax.axis_size(axis)
+    return lax.ppermute(value, axis, [(source, source ^ bits) for source in range(count)])
+
+
+def dot_nn(left, right):
+    return jnp.dot(left, right, preferred_element_type=F32)
+
+
+def dot_nt(left, right):
+    return lax.dot_general(left, right, (((1,), (1,)), ((), ())), preferred_element_type=F32)
+
+
+def split_rows(flat):
+    first = lax.broadcasted_iota(jnp.int32, flat.shape, 0) < HD
+    zero = jnp.zeros_like(flat)
+    return jnp.concatenate([jnp.where(first, flat, zero), jnp.where(first, zero, flat)], axis=1)
+
+
+def join_rows(wide):
+    count = wide.shape[1] // 2
+    first = lax.broadcasted_iota(jnp.int32, (wide.shape[0], count), 0) < HD
+    return jnp.where(first, wide[:, :count], wide[:, count:])
+
+
+def split_cols(flat):
+    first = lax.broadcasted_iota(jnp.int32, flat.shape, 1) < HD
+    zero = jnp.zeros_like(flat)
+    return jnp.concatenate([jnp.where(first, flat, zero), jnp.where(first, zero, flat)], axis=0)
+
+
+def attention_kernel(
+    col_ref, x_ref, x1_ref, x2_ref, x3_ref, grad_ref, bias_ref,
+    wq_ref, wk_ref, wv_ref, wg_ref, wo_ref,
+    raw_ref, keep_ref, send_ref,
+    pairs_ref, scores_ref, expo_ref, both_ref, parts_ref,
+):
+    scale = HD ** (-0.5)
+    width = 2 * TILE
+    me = col_ref[0]
+    places = [pl.multiple_of(lax.bitwise_xor(me, bits) * TILE, TILE) for bits in range(4)]
+    x = x_ref[...]
+    for place, ref in zip(places, (x_ref, x1_ref, x2_ref, x3_ref)):
+        pairs_ref[pl.ds(place, TILE), :] = ref[...]
+    out_grad = grad_ref[...]
+    w_q, w_g, w_o = wq_ref[...], wg_ref[...], wo_ref[...]
+    w_kv = jnp.concatenate([wk_ref[...], wv_ref[...]], axis=0)
+    w_qg = jnp.concatenate([w_q, w_g], axis=0)
+
+    query_gate = dot_nt(w_qg, x)
+    query_t = (query_gate[: 2 * HD] * scale).astype(BF16)
+    gate_t = jax.nn.sigmoid(query_gate[2 * HD :])
+    query = (dot_nt(x, w_q) * scale).astype(BF16)
+    gated_grad_t = dot_nt(w_o, out_grad)
+    att_grad_f = (gated_grad_t * gate_t).astype(BF16).astype(F32)
+    att_grad_t = att_grad_f.astype(BF16)
+    att_grad = jnp.transpose(att_grad_f).astype(BF16)
+
+    pairs = pairs_ref[...]
+    key_value = dot_nt(pairs, w_kv).astype(BF16)
+    key_value_t = dot_nt(w_kv, pairs).astype(BF16)
+    zero_wide = jnp.zeros((2 * HD, width), BF16)
+    left = jnp.concatenate(
+        [
+            jnp.concatenate([split_rows(query_t), zero_wide], axis=1),
+            jnp.concatenate([zero_wide, split_rows(att_grad_t)], axis=1),
+        ],
+        axis=0,
+    )
+    top = None
+    for block in range(4):
+        rows = slice(block * TILE, (block + 1) * TILE)
+        product = dot_nn(key_value[rows], left)
+        scores = product[:, :width] + bias_ref[rows, :].astype(F32)
+        scores_ref[rows, :width] = scores
+        scores_ref[rows, width:] = product[:, width:]
+        part = jnp.max(scores.reshape(TILE // 8, 8, width), axis=0)
+        top = part if top is None else jnp.maximum(top, part)
+    top = jnp.max(top, axis=0, keepdims=True)
+    total = jnp.zeros((8, width), F32)
+    for block in range(4):
+        rows = slice(block * TILE, (block + 1) * TILE)
+        expo = jnp.exp(scores_ref[rows, :width] - top)
+        scores_ref[rows, :width] = expo
+        expo_ref[rows, :] = expo.astype(BF16)
+        total = total + jnp.sum(expo.reshape(TILE // 8, 8, width), axis=0)
+    total = jnp.sum(total, axis=0, keepdims=True)
+    inverse = 1.0 / total
+    attended_t = join_rows(dot_nn(key_value_t[2 * HD :], expo_ref[...]) * inverse)
+    gated_t = (gate_t * attended_t).astype(BF16)
+    gate_logit_t = gated_grad_t * attended_t * gate_t * (1.0 - gate_t)
+    products = att_grad_f * attended_t
+    delta = jnp.concatenate(
+        [
+            jnp.sum(products[:HD], axis=0, keepdims=True),
+            jnp.sum(products[HD:], axis=0, keepdims=True),
+        ],
+        axis=1,
+    )
+    for block in range(4):
+        rows = slice(block * TILE, (block + 1) * TILE)
+        prob = scores_ref[rows, :width] * inverse
+        both_ref[rows, :width] = (prob * (scores_ref[rows, width:] - delta)).astype(BF16)
+        both_ref[rows, width:] = prob.astype(BF16)
+    query_grad_t = join_rows(dot_nn(key_value_t[: 2 * HD], both_ref[:, :width])) * scale
+    zero_tall = jnp.zeros((width, 2 * HD), BF16)
+    right = jnp.concatenate(
+        [
+            jnp.concatenate([split_cols(query), zero_tall], axis=1),
+            jnp.concatenate([zero_tall, split_cols(att_grad)], axis=1),
+        ],
+        axis=0,
+    )
+    key_value_grad = dot_nn(both_ref[...], right)
+    local_t = jnp.concatenate([query_grad_t, gate_logit_t], axis=0)
+    local = jnp.transpose(local_t).astype(BF16)
+    parts_ref[...] = dot_nn(key_value_grad.astype(BF16), w_kv)
+    own = pl.ds(places[0], TILE)
+    parts_ref[own, :] = parts_ref[own, :] + dot_nn(local, w_qg)
+    keep_ref[:TILE, :] = parts_ref[own, :].astype(BF16)
+    keep_ref[TILE:, :] = parts_ref[pl.ds(places[1], TILE), :].astype(BF16)
+    send_ref[:TILE, :] = parts_ref[pl.ds(places[2], TILE), :].astype(BF16)
+    send_ref[TILE:, :] = parts_ref[pl.ds(places[3], TILE), :].astype(BF16)
+    raw_ref[: 4 * HD, :] = dot_nn(local_t.astype(BF16), x).astype(BF16)
+    raw_ref[4 * HD : 8 * HD, :] = dot_nn(jnp.transpose(key_value_grad).astype(BF16), pairs).astype(BF16)
+    raw_ref[8 * HD :, :] = dot_nn(gated_t, out_grad).astype(BF16)
+
+
+def attention(col_index, xs, out_grad, bias, weights):
+    spec = pl.BlockSpec(memory_space=pltpu.VMEM)
+    keys = 4 * TILE
+    return pl.pallas_call(
+        attention_kernel,
+        out_shape=(
+            jax.ShapeDtypeStruct((10 * HD, C), BF16),
+            jax.ShapeDtypeStruct((2 * TILE, C), BF16),
+            jax.ShapeDtypeStruct((2 * TILE, C), BF16),
+        ),
+        in_specs=[pl.BlockSpec(memory_space=pltpu.SMEM)] + [spec] * 11,
+        out_specs=(spec, spec, spec),
+        scratch_shapes=[
+            pltpu.VMEM((keys, C), BF16),
+            pltpu.VMEM((keys, 4 * TILE), F32),
+            pltpu.VMEM((keys, 2 * TILE), BF16),
+            pltpu.VMEM((keys, 4 * TILE), BF16),
+            pltpu.VMEM((keys, C), F32),
+        ],
+        name="attention",
+    )(col_index.reshape(1), *xs, out_grad, bias, *weights)
+
+
+def masked_bias(pair_bias, tile_mask, chain_ids, col_index):
+    keys = chain_ids.shape[0]
+    marks = jnp.repeat(lax.dynamic_index_in_dim(tile_mask, col_index, 0, keepdims=False), TILE)
+    own_chain = lax.dynamic_slice_in_dim(chain_ids, col_index * TILE, TILE)
+    allowed = (marks[:, None] == 1) | (chain_ids[:, None] == own_chain[None, :])
+    turned = jnp.transpose(pair_bias, (2, 1, 0))
+    masked = jnp.where(allowed[:, None, :], turned, jnp.asarray(NEG_FILL, BF16))
+    return masked.reshape(keys, 2 * TILE)
+
+
+def four_cols(
+    pair, out_grad, pair_bias, w_query, w_key, w_value, w_gate, w_out, tile_mask, chain_ids
+):
+    col_index = lax.axis_index("col")
+    head_index = lax.axis_index("head")
+    x = pair.reshape(TILE, C)
+    x2 = crossed(x, "col", 2)
+    x1 = crossed(x, "col", 1)
+    x3 = crossed(x2, "col", 1)
+    bias = masked_bias(pair_bias, tile_mask, chain_ids, col_index)
+    raw, keep, send = attention(
+        col_index,
+        (x, x1, x2, x3),
+        out_grad.reshape(TILE, C),
+        bias,
+        (w_query.T, w_key.T, w_value.T, w_gate.T, w_out),
+    )
+    row_raw = crossed(raw, "row", 1)
+    two_parts = keep.astype(F32) + crossed(send, "col", 2).astype(F32)
+    raw = (raw.astype(F32) + row_raw.astype(F32)).astype(BF16)
+    raw = (raw.astype(F32) + crossed(raw, "col", 2).astype(F32)).astype(BF16)
+    one_part = two_parts[:TILE] + crossed(two_parts[TILE:].astype(BF16), "col", 1).astype(F32)
+    raw = raw.astype(F32) + crossed(raw, "col", 1).astype(F32)
+    half = TILE // 2
+    mine = lax.dynamic_slice_in_dim(one_part, head_index * half, half, 0)
+    other = lax.dynamic_slice_in_dim(one_part, (1 - head_index) * half, half, 0)
+    pair_grad = (mine + crossed(other.astype(BF16), "head", 1).astype(F32)).astype(BF16)
+    squares = jnp.sum(raw * raw).reshape(1, 1)
+    squares = squares + crossed(squares, "head", 1)
+    clip = jnp.minimum(1.0, CLIP_NORM / jnp.sqrt(squares + 1e-06))
+    raw = raw * clip
+    width = 2 * HD
+    return (
+        pair_grad.reshape(1, half, C),
+        raw[:width].T,
+        raw[2 * width : 3 * width].T,
+        raw[3 * width : 4 * width].T,
+        raw[width : 2 * width].T,
+        raw[4 * width :],
+    )
+
+
+def per_device(pair, out_grad, pair_bias, *rest):
+    small = lax.axis_size("col") == 4 and lax.axis_size("row") == 2 and lax.axis_size("head") == 2
+    if small and pair.shape == (1, TILE, C) and pair_bias.shape == (TILE, 2, 4 * TILE):
+        return four_cols(pair, out_grad, pair_bias, *rest)
+    return any_cols(pair, out_grad, pair_bias, *rest)
+
+
 def solution(mesh):
     return jax.shard_map(
         per_device,

time: 156 us -> 38.4 us (0.25)
  blocking collectives: 64.2 us -> 0 us
  waiting for transfers between devices: 51.9 us -> 10.7 us
  between operations: 17.7 us -> 2.06 us
  starting transfers between devices: 3.59 us -> 14.7 us
  matrix products: 7.86 us -> 0 us
  Pallas kernels: 0 us -> 3.01 us
  local copies, waits for them, and re-layouts: 5.54 us -> 3.2 us
    psum x2 -> x0, blocking collectives: 38.5 us -> none  [the longest x1 35.6 us: per_device(): summed_four, summed_out = lax.psum((raw_four, raw_out), ('col', 'row'))]
    psum x1 -> x0, waiting for transfers between devices: 32.1 us -> none  [per_device(): summed_four, summed_out = lax.psum((raw_four, raw_out), ('col', 'row'))]
    all_gather x2 -> x0, blocking collectives: 25.7 us -> none  [the longest x1 13.7 us: per_device(): key_piece = lax.all_gather(key_grid, 'col', axis=1, tiled=True)]
    ppermute x8 -> x10, starting transfers between devices: 3.5 us -> 14.7 us  [crossed(): lax.ppermute(value, axis, [(source, source ^ bits) for source in range(co...]
    dot_general x34 -> x0, matrix products: 7.86 us -> none  [the longest x5 1.37 us: allowed_between(): jnp.dot(jnp.dot(query_tiles, tile_mask.astype(jnp.float32)), key_tiles.T)]
    ppermute x8 -> x10, waiting for transfers between devices: 18 us -> 10.7 us  [crossed(): lax.ppermute(value, axis, [(source, source ^ bits) for source in range(co...]
    pallas_call x0 -> x1, Pallas kernels: none -> 3.01 us  [attention(): pl.pallas_call(attention_kernel, out_shape=(jax.ShapeDtypeStruct((10 * HD...]
    unnamed x26 -> x11, local copies, waits for them, and re-layouts: 4.79 us -> 1.97 us
  transfers between devices with their start and end apart: 10 -> 10, of which waited for: 10 -> 6; matrix products, arithmetic and copies ran while one was open for 5% -> 13% of each run, Pallas kernels for 0% -> 0%
where the time goes in v1:
time: 38.4 us; the launch traced here: 38.1 us
  starting transfers between devices  14.7 us (38%)
  waiting for transfers between devices  10.7 us (28%)
  other arithmetic  4.42 us (12%)
  local copies, waits for them, and re-layouts  3.2 us (8%)
  Pallas kernels  3.01 us (8%)
  between operations  2.06 us (5%)
    ppermute x10, starting transfers between devices, crossed(): lax.ppermute(value, axis, [(source, source ^ bits) for source in range(co...  14.7 us
    ppermute x10, waiting for transfers between devices, crossed(): lax.ppermute(value, axis, [(source, source ^ bits) for source in range(co...  10.7 us
    pallas_call x1, Pallas kernels, attention(): pl.pallas_call(attention_kernel, out_shape=(jax.ShapeDtypeStruct((10 * HD...  3.01 us
    unnamed x11, local copies, waits for them, and re-layouts  1.97 us
    select_n x1, other arithmetic, masked_bias(): masked = jnp.where(allowed[:, None, :], turned, jnp.asarray(NEG_FILL, BF16))  1.39 us
    add x1, other arithmetic, four_cols(): two_parts = keep.astype(F32) + crossed(send, 'col', 2).astype(F32)  0.89 us
  transfers between devices with their start and end apart: 10, of which 6 were waited for; matrix products, arithmetic and copies ran while one was open for 13% of the time, Pallas kernels for 0%

profile of v1, /device:TPU:0, one launch (start us, length us, event | category | flops | bytes accessed | tf_op | source)
XLA Modules:
  0.0 38.1 jit_solution(5258175802996929396)
XLA Ops:
  0.6 4.1 %collective-permute-start.1 = (bf16[128,128]{1,0:T(8,128)(2,1)}, bf16[128,128]{1,0:T(8,128)(2,1)S(1)}, u32[]{:S(2)}, u32[]{:S(2)}) collective-permute-start(bf16[128,128]{1,0:T(8,128)(2,1)} %bitcast.31), channel_id=1, source_target_pairs={{0,8},{4,12},{8,0},{12,4},{1,9},{5,13},{9,1},{13,5},{2,10},{6,14},... | collective-permute-start | bytes 98312 | tf_op jit(solution)/shard_map/ppermute | solution.py:185
  4.7 1.6 %collective-permute-start = (bf16[128,128]{1,0:T(8,128)(2,1)}, bf16[128,128]{1,0:T(8,128)(2,1)S(1)}, u32[]{:S(2)}, u32[]{:S(2)}) collective-permute-start(bf16[128,128]{1,0:T(8,128)(2,1)} %bitcast.32), channel_id=1, source_target_pairs={{0,4},{4,0},{8,12},{12,8},{1,5},{5,1},{9,13},{13,9},{2,6},{6,2},{1... | collective-permute-start | bytes 98312 | tf_op jit(solution)/shard_map/ppermute | solution.py:185
  6.3 0.7 %compare_bitcast_fusion = pred[4]{0:T(512)(128)(4,1)S(1)} fusion(s32[4,4]{1,0:T(4,128)} %param.18, s32[]{:T(128)S(6)} %select_n.17), kind=kLoop, calls=%fused_computation.18 | loop fusion | flops 4 | bytes 24 | tf_op jit(solution)/shard_map/eq | solution.py:338
  7.1 0.6 %copy-done.4 = s32[512]{0:T(512)S(1)} copy-done((s32[512]{0:T(512)S(1)}, s32[512]{0:T(512)}, u32[]{:S(2)}) %copy-start.4) | copy-done | bytes 2072
  7.9 0.8 %collective-permute-start.2 = (bf16[128,128]{1,0:T(8,128)(2,1)S(1)}, bf16[128,128]{1,0:T(8,128)(2,1)S(1)}, u32[]{:S(2)}, u32[]{:S(2)}) collective-permute-start(bf16[128,128]{1,0:T(8,128)(2,1)S(1)} %collective-permute-done.1.x2_ref), channel_id=1, source_target_pairs={{0,4},{4,0},{8,12},{12,8},{1,5},{5,1},{9,13},{13,9},{2,6},{6,2},{1... | collective-permute-start | bytes 98312 | tf_op jit(solution)/shard_map/ppermute | solution.py:185
  8.7 1.4 %broadcast_select_fusion = bf16[512,2,128]{0,1,2:T(2,128)(2,1)S(1)} fusion(pred[512,128]{0,1:T(8,128)(4,1)S(1)} %compare_or_fusion, bf16[128,2,512]{2,1,0:T(2,128)(2,1)} %param.12), kind=kLoop, calls=%fused_computation | loop fusion | flops 131072 | bytes 589824 | tf_op jit(solution)/shard_map/jit(_where)/select_n | solution.py:340
  10.2 0.4 %copy.16 = bf16[512,2,128]{2,1,0:T(2,128)(2,1)S(1)} copy(bf16[512,2,128]{0,1,2:T(2,128)(2,1)S(1)} %broadcast_select_fusion) | data formatting | bytes 524288 | tf_op jit(solution)/shard_map/jit(_where)/select_n | solution.py:340
  10.6 0.7 %copy.19 = bf16[64,8,2,128]{3,1,2,0:T(8,128)(2,1)} copy(bf16[64,8,2,128]{3,2,1,0:T(2,128)(2,1)S(1)} %bitcast.30) | data formatting | bytes 524288
  11.3 0.6 %collective-permute-done.2.x3_ref = bf16[128,128]{1,0:T(8,128)(2,1)S(1)} collective-permute-done((bf16[128,128]{1,0:T(8,128)(2,1)S(1)}, bf16[128,128]{1,0:T(8,128)(2,1)S(1)}, u32[]{:S(2)}, u32[]{:S(2)}) %collective-permute-start.2) | collective-permute-done | bytes 32800 | tf_op jit(solution)/shard_map/ppermute | solution.py:185
  11.9 0.6 %copy-done.3 = bf16[128,128]{1,0:T(8,128)(2,1)} copy-done((bf16[128,128]{1,0:T(8,128)(2,1)}, bf16[128,128]{1,0:T(8,128)(2,1)S(1)}, u32[]{:S(2)}) %copy-start.3) | copy-done | bytes 32792
  12.5 3.0 %attention.1 = (bf16[320,128]{1,0:T(8,128)(2,1)}, bf16[256,128]{1,0:T(8,128)(2,1)}, bf16[256,128]{1,0:T(8,128)(2,1)}) custom-call(s32[1]{0:T(128)} %bitcast.col_ref, bf16[128,128]{1,0:T(8,128)(2,1)} %bitcast.33, bf16[128,128]{1,0:T(8,128)(2,1)} %copy-done.2, bf16[128,128]{1,0:T(8,128)(2,1)} %copy-done.1, bf16[128,128]{1,0:T(8,128)(2,1)} %copy-done.3, ...), custom_call_target="tpu_custom_call" | custom-call | tf_op jit(solution)/shard_map/attention/pallas_call | solution.py:314
  15.5 2.3 %collective-permute-start.3 = (bf16[256,128]{1,0:T(8,128)(2,1)}, bf16[256,128]{1,0:T(8,128)(2,1)S(1)}, u32[]{:S(2)}, u32[]{:S(2)}) collective-permute-start(bf16[256,128]{1,0:T(8,128)(2,1)} %get-tuple-element.10), channel_id=1, source_target_pairs={{0,8},{4,12},{8,0},{12,4},{1,9},{5,13},{9,1},{13,5},{2,10},{6,14},... | collective-permute-start | bytes 196616 | tf_op jit(solution)/shard_map/ppermute | solution.py:185
  17.8 1.5 %collective-permute-start.6 = (bf16[320,128]{1,0:T(8,128)(2,1)}, bf16[320,128]{1,0:T(8,128)(2,1)S(1)}, u32[]{:S(2)}, u32[]{:S(2)}) collective-permute-start(bf16[320,128]{1,0:T(8,128)(2,1)} %get-tuple-element.11), channel_id=1, source_target_pairs={{0,2},{2,0},{1,3},{3,1},{4,6},{6,4},{5,7},{7,5},{8,10},{10,8},{9,1... | collective-permute-start | bytes 245768 | tf_op jit(solution)/shard_map/ppermute | solution.py:185
  19.3 2.3 %collective-permute-done.3 = bf16[256,128]{1,0:T(8,128)(2,1)S(1)} collective-permute-done((bf16[256,128]{1,0:T(8,128)(2,1)}, bf16[256,128]{1,0:T(8,128)(2,1)S(1)}, u32[]{:S(2)}, u32[]{:S(2)}) %collective-permute-start.3) | collective-permute-done | bytes 65568 | tf_op jit(solution)/shard_map/ppermute | solution.py:185
  21.6 0.9 %convert_add_fusion.1 = f32[256,128]{1,0:T(8,128)S(1)} fusion(bf16[256,128]{1,0:T(8,128)(2,1)S(1)} %collective-permute-done.3, bf16[256,128]{1,0:T(8,128)(2,1)} %get-tuple-element.9), kind=kLoop, calls=%fused_computation.8 | loop fusion | flops 98304 | bytes 262144 | tf_op jit(solution)/shard_map/add | solution.py:362
  22.5 0.4 %collective-permute-start.4 = (bf16[128,128]{1,0:T(8,128)(2,1)S(1)}, bf16[128,128]{1,0:T(8,128)(2,1)S(1)}, u32[]{:S(2)}, u32[]{:S(2)}) collective-permute-start(bf16[128,128]{1,0:T(8,128)(2,1)S(1)} %slice.42), channel_id=1, source_target_pairs={{0,4},{4,0},{8,12},{12,8},{1,5},{5,1},{9,13},{13,9},{2,6},{6,2},{1... | collective-permute-start | bytes 98312 | tf_op jit(solution)/shard_map/ppermute | solution.py:185
  23.0 3.4 %collective-permute-start.7 = (bf16[320,128]{1,0:T(8,128)(2,1)S(1)}, bf16[320,128]{1,0:T(8,128)(2,1)S(1)}, u32[]{:S(2)}, u32[]{:S(2)}) collective-permute-start(bf16[320,128]{1,0:T(8,128)(2,1)S(1)} %add_convert_fusion.1), channel_id=1, source_target_pairs={{0,8},{4,12},{8,0},{12,4},{1,9},{5,13},{9,1},{13,5},{2,10},{6,14},... | collective-permute-start | bytes 245768 | tf_op jit(solution)/shard_map/ppermute | solution.py:185
  26.6 3.1 %collective-permute-done.7 = bf16[320,128]{1,0:T(8,128)(2,1)S(1)} collective-permute-done((bf16[320,128]{1,0:T(8,128)(2,1)S(1)}, bf16[320,128]{1,0:T(8,128)(2,1)S(1)}, u32[]{:S(2)}, u32[]{:S(2)}) %collective-permute-start.7) | collective-permute-done | bytes 81952 | tf_op jit(solution)/shard_map/ppermute | solution.py:185
  29.7 0.6 %collective-permute-start.8 = (bf16[320,128]{1,0:T(8,128)(2,1)S(1)}, bf16[320,128]{1,0:T(8,128)(2,1)S(1)}, u32[]{:S(2)}, u32[]{:S(2)}) collective-permute-start(bf16[320,128]{1,0:T(8,128)(2,1)S(1)} %add_convert_fusion), channel_id=1, source_target_pairs={{0,4},{4,0},{8,12},{12,8},{1,5},{5,1},{9,13},{13,9},{2,6},{6,2},{1... | collective-permute-start | bytes 245768 | tf_op jit(solution)/shard_map/ppermute | solution.py:185
  30.2 0.6 %fusion.1 = bf16[1,64,128]{2,1,0:T(8,128)(2,1)} fusion(bf16[64,128]{1,0:T(8,128)(2,1)S(1)} %collective-permute-done.5, f32[128,128]{1,0:T(8,128)S(1)} %slice_add_fusion, s32[]{:T(128)S(6)} %select_n.20), kind=kLoop, calls=%fused_computation.17 | loop fusion | flops 24576 | bytes 65540 | tf_op jit(solution)/shard_map/reshape | solution.py:377
  30.9 3.3 %collective-permute-done.8 = bf16[320,128]{1,0:T(8,128)(2,1)S(1)} collective-permute-done((bf16[320,128]{1,0:T(8,128)(2,1)S(1)}, bf16[320,128]{1,0:T(8,128)(2,1)S(1)}, u32[]{:S(2)}, u32[]{:S(2)}) %collective-permute-start.8) | collective-permute-done | bytes 81952 | tf_op jit(solution)/shard_map/ppermute | solution.py:185
  34.2 0.6 %multiply_reduce_fusion = f32[]{:T(128)} fusion(bf16[320,128]{1,0:T(8,128)(2,1)S(1)} %collective-permute-done.8, bf16[320,128]{1,0:T(8,128)(2,1)S(1)} %add_convert_fusion), kind=kLoop, calls=%fused_computation.3 | loop fusion | flops 204799 | bytes 163844 | tf_op jit(solution)/shard_map/reduce_sum | solution.py:371
  34.8 1.2 %collective-permute-done.9 = f32[1,1]{1,0:T(1,128)} collective-permute-done((f32[1,1]{1,0:T(1,128)}, f32[1,1]{1,0:T(1,128)}, u32[]{:S(2)}, u32[]{:S(2)}) %collective-permute-start.9) | collective-permute-done | bytes 36 | tf_op jit(solution)/shard_map/ppermute | solution.py:185
  37.4 0.7 %fusion.2 = (f32[64,128]{1,0:T(8,128)}, f32[128,64]{0,1:T(8,128)}, f32[128,64]{0,1:T(8,128)}, f32[128,64]{0,1:T(8,128)}, f32[128,64]{0,1:T(8,128)}) fusion(f32[320,128]{1,0:T(8,128)S(1)} %fusion), kind=kLoop, calls=%fused_computation.21 | loop fusion | bytes 327680 | tf_op jit(solution)/shard_map/slice | solution.py:382
  (24 shorter events, 0.6 us)
Async XLA Ops:
  0.6 7.2 %collective-permute-start.1 = (bf16[128,128]{1,0:T(8,128)(2,1)}, bf16[128,128]{1,0:T(8,128)(2,1)S(1)}, u32[]{:S(2)}, u32[]{:S(2)}) collective-permute-start(bf16[128,128]{1,0:T(8,128)(2,1)} %bitcast.31), channel_id=1, source_target_pairs={{0,8},{4,12},{8,0},{12,4},{1,9},{5,13},{9,1},{13,5},{2,10},{6,14},... | collective-permute-start | bytes 98312 | tf_op jit(solution)/shard_map/ppermute | solution.py:185
  4.7 6.6 %collective-permute-start = (bf16[128,128]{1,0:T(8,128)(2,1)}, bf16[128,128]{1,0:T(8,128)(2,1)S(1)}, u32[]{:S(2)}, u32[]{:S(2)}) collective-permute-start(bf16[128,128]{1,0:T(8,128)(2,1)} %bitcast.32), channel_id=1, source_target_pairs={{0,4},{4,0},{8,12},{12,8},{1,5},{5,1},{9,13},{13,9},{2,6},{6,2},{1... | collective-permute-start | bytes 98312 | tf_op jit(solution)/shard_map/ppermute | solution.py:185
  7.0 0.7 %copy-start.4 = (s32[512]{0:T(512)S(1)}, s32[512]{0:T(512)}, u32[]{:S(2)}) copy-start(s32[512]{0:T(512)} %param.19) | copy-start | bytes 6148
  7.9 2.3 %copy-start.1 = (bf16[128,128]{1,0:T(8,128)(2,1)}, bf16[128,128]{1,0:T(8,128)(2,1)S(1)}, u32[]{:S(2)}) copy-start(bf16[128,128]{1,0:T(8,128)(2,1)S(1)} %collective-permute-done.1.x2_ref) | copy-start | bytes 98308
  7.9 4.0 %collective-permute-start.2 = (bf16[128,128]{1,0:T(8,128)(2,1)S(1)}, bf16[128,128]{1,0:T(8,128)(2,1)S(1)}, u32[]{:S(2)}, u32[]{:S(2)}) collective-permute-start(bf16[128,128]{1,0:T(8,128)(2,1)S(1)} %collective-permute-done.1.x2_ref), channel_id=1, source_target_pairs={{0,4},{4,0},{8,12},{12,8},{1,5},{5,1},{9,13},{13,9},{2,6},{6,2},{1... | collective-permute-start | bytes 98312 | tf_op jit(solution)/shard_map/ppermute | solution.py:185
  11.3 0.6 %copy-start.2 = (bf16[128,128]{1,0:T(8,128)(2,1)}, bf16[128,128]{1,0:T(8,128)(2,1)S(1)}, u32[]{:S(2)}) copy-start(bf16[128,128]{1,0:T(8,128)(2,1)S(1)} %collective-permute-done.x1_ref) | copy-start | bytes 98308
  11.9 0.6 %copy-start.3 = (bf16[128,128]{1,0:T(8,128)(2,1)}, bf16[128,128]{1,0:T(8,128)(2,1)S(1)}, u32[]{:S(2)}) copy-start(bf16[128,128]{1,0:T(8,128)(2,1)S(1)} %collective-permute-done.2.x3_ref) | copy-start | bytes 98308
  15.5 6.1 %collective-permute-start.3 = (bf16[256,128]{1,0:T(8,128)(2,1)}, bf16[256,128]{1,0:T(8,128)(2,1)S(1)}, u32[]{:S(2)}, u32[]{:S(2)}) collective-permute-start(bf16[256,128]{1,0:T(8,128)(2,1)} %get-tuple-element.10), channel_id=1, source_target_pairs={{0,8},{4,12},{8,0},{12,4},{1,9},{5,13},{9,1},{13,5},{2,10},{6,14},... | collective-permute-start | bytes 196616 | tf_op jit(solution)/shard_map/ppermute | solution.py:185
  17.8 5.2 %collective-permute-start.6 = (bf16[320,128]{1,0:T(8,128)(2,1)}, bf16[320,128]{1,0:T(8,128)(2,1)S(1)}, u32[]{:S(2)}, u32[]{:S(2)}) collective-permute-start(bf16[320,128]{1,0:T(8,128)(2,1)} %get-tuple-element.11), channel_id=1, source_target_pairs={{0,2},{2,0},{1,3},{3,1},{4,6},{6,4},{5,7},{7,5},{8,10},{10,8},{9,1... | collective-permute-start | bytes 245768 | tf_op jit(solution)/shard_map/ppermute | solution.py:185
  21.6 1.3 %copy-start = (bf16[320,128]{1,0:T(8,128)(2,1)S(1)}, bf16[320,128]{1,0:T(8,128)(2,1)}, u32[]{:S(2)}) copy-start(bf16[320,128]{1,0:T(8,128)(2,1)} %get-tuple-element.11) | copy-start | bytes 245764
  22.5 4.0 %collective-permute-start.4 = (bf16[128,128]{1,0:T(8,128)(2,1)S(1)}, bf16[128,128]{1,0:T(8,128)(2,1)S(1)}, u32[]{:S(2)}, u32[]{:S(2)}) collective-permute-start(bf16[128,128]{1,0:T(8,128)(2,1)S(1)} %slice.42), channel_id=1, source_target_pairs={{0,4},{4,0},{8,12},{12,8},{1,5},{5,1},{9,13},{13,9},{2,6},{6,2},{1... | collective-permute-start | bytes 98312 | tf_op jit(solution)/shard_map/ppermute | solution.py:185
  23.0 6.7 %collective-permute-start.7 = (bf16[320,128]{1,0:T(8,128)(2,1)S(1)}, bf16[320,128]{1,0:T(8,128)(2,1)S(1)}, u32[]{:S(2)}, u32[]{:S(2)}) collective-permute-start(bf16[320,128]{1,0:T(8,128)(2,1)S(1)} %add_convert_fusion.1), channel_id=1, source_target_pairs={{0,8},{4,12},{8,0},{12,4},{1,9},{5,13},{9,1},{13,5},{2,10},{6,14},... | collective-permute-start | bytes 245768 | tf_op jit(solution)/shard_map/ppermute | solution.py:185
  26.5 3.7 %collective-permute-start.5 = (bf16[64,128]{1,0:T(8,128)(2,1)S(1)}, bf16[64,128]{1,0:T(8,128)(2,1)S(1)}, u32[]{:S(2)}, u32[]{:S(2)}) collective-permute-start(bf16[64,128]{1,0:T(8,128)(2,1)S(1)} %dynamic-slice_convert_fusion), channel_id=1, source_target_pairs={{0,1},{1,0},{2,3},{3,2},{4,5},{5,4},{6,7},{7,6},{8,9},{9,8},{10,11... | collective-permute-start | bytes 49160 | tf_op jit(solution)/shard_map/ppermute | solution.py:185
  29.7 4.5 %collective-permute-start.8 = (bf16[320,128]{1,0:T(8,128)(2,1)S(1)}, bf16[320,128]{1,0:T(8,128)(2,1)S(1)}, u32[]{:S(2)}, u32[]{:S(2)}) collective-permute-start(bf16[320,128]{1,0:T(8,128)(2,1)S(1)} %add_convert_fusion), channel_id=1, source_target_pairs={{0,4},{4,0},{8,12},{12,8},{1,5},{5,1},{9,13},{13,9},{2,6},{6,2},{1... | collective-permute-start | bytes 245768 | tf_op jit(solution)/shard_map/ppermute | solution.py:185
  34.8 1.2 %collective-permute-start.9 = (f32[1,1]{1,0:T(1,128)}, f32[1,1]{1,0:T(1,128)}, u32[]{:S(2)}, u32[]{:S(2)}) collective-permute-start(f32[1,1]{1,0:T(1,128)} %bitcast.11), channel_id=1, source_target_pairs={{0,1},{1,0},{2,3},{3,2},{4,5},{5,4},{6,7},{7,6},{8,9},{9,8},{10,11... | collective-permute-start | bytes 20 | tf_op jit(solution)/shard_map/ppermute | solution.py:185

commit v2 on v0

--- a/solution.py
+++ b/solution.py
@@ -3,6 +3,8 @@
 import jax
 import jax.numpy as jnp
 from jax import lax
+from jax.experimental import pallas as pl
+from jax.experimental.pallas import tpu as pltpu
 from jax.sharding import PartitionSpec as P
 
 C = 128
@@ -12,6 +14,9 @@
 
 
 NEG_FILL = -1e30
+F32 = jnp.float32
+BF16 = jnp.bfloat16
+CLIP_NORM = 0.5 * math.sqrt(5.0 * C * H * HD)
 
 
 def shifted(value, axis, steps):
@@ -50,7 +55,7 @@
     return (prob.astype(jnp.bfloat16), grad_score)
 
 
-def per_device(
+def any_cols(
     pair, out_grad, pair_bias, w_query, w_key, w_value, w_gate, w_out, tile_mask, chain_ids
 ):
     rows_dev, cols_dev, channels = pair.shape
@@ -176,6 +181,320 @@
     )
 
 
+def exchange(value, partner):
+    cols, rows, heads = lax.axis_size("col"), lax.axis_size("row"), lax.axis_size("head")
+    pairs = []
+    for col in range(cols):
+        for row in range(rows):
+            for head in range(heads):
+                to_col, to_row, to_head = partner(col, row, head)
+                source = (col * rows + row) * heads + head
+                pairs.append((source, (to_col * rows + to_row) * heads + to_head))
+    return lax.ppermute(value, ("col", "row", "head"), pairs)
+
+
+def next_col(col, row, head):
+    return col ^ 1, row, head
+
+
+def far_col(col, row, head):
+    return col ^ 2, row, head
+
+
+def other_row(col, row, head):
+    return col, row ^ 1, head
+
+
+def other_head(col, row, head):
+    return col, row, head ^ 1
+
+
+def staggered(first, second):
+    return lambda col, row, head: (first, second)[head](col, row, head)
+
+
+def dot_nn(left, right):
+    return jnp.dot(left, right, preferred_element_type=F32)
+
+
+def dot_nt(left, right):
+    return lax.dot_general(left, right, (((1,), (1,)), ((), ())), preferred_element_type=F32)
+
+
+def split_rows(flat):
+    first = lax.broadcasted_iota(jnp.int32, flat.shape, 0) < HD
+    zero = jnp.zeros_like(flat)
+    return jnp.concatenate([jnp.where(first, flat, zero), jnp.where(first, zero, flat)], axis=1)
+
+
+def join_rows(wide):
+    count = wide.shape[1] // 2
+    first = lax.broadcasted_iota(jnp.int32, (wide.shape[0], count), 0) < HD
+    return jnp.where(first, wide[:, :count], wide[:, count:])
+
+
+def split_cols(flat):
+    first = lax.broadcasted_iota(jnp.int32, flat.shape, 1) < HD
+    zero = jnp.zeros_like(flat)
+    return jnp.concatenate([jnp.where(first, flat, zero), jnp.where(first, zero, flat)], axis=0)
+
+
+def local_kernel(
+    col_ref, tile_hbm, x_hbm, grad_hbm, bias_hbm, chain_hbm, wq_hbm, wk_hbm, wv_hbm, wg_hbm, wo_hbm,
+    x_ref, grad_ref, w_qg_ref, w_kv_ref, bias_out, left_out, right_out, gate_out, gated_grad_out,
+    att_grad_out, tile_ref, chain_ref, wo_ref, bias_ref, sems,
+):
+    scale = HD ** (-0.5)
+    width = 2 * TILE
+    me = col_ref[0]
+    moves = [
+        (x_hbm, x_ref),
+        (wq_hbm, w_qg_ref.at[: 2 * HD]),
+        (wg_hbm, w_qg_ref.at[2 * HD :]),
+        (grad_hbm, grad_ref),
+        (wo_hbm, wo_ref),
+        (chain_hbm, chain_ref),
+        (tile_hbm, tile_ref),
+        (bias_hbm, bias_ref),
+        (wk_hbm, w_kv_ref.at[: 2 * HD]),
+        (wv_hbm, w_kv_ref.at[2 * HD :]),
+    ]
+    copies = [
+        pltpu.make_async_copy(source, target, sems.at[place])
+        for place, (source, target) in enumerate(moves)
+    ]
+    for copy in copies:
+        copy.start()
+    for copy in copies[:5]:
+        copy.wait()
+    x = x_ref[...]
+    query_gate = dot_nt(w_qg_ref[...], x)
+    gated_grad_t = dot_nt(wo_ref[...], grad_ref[...])
+    query = (dot_nt(x, w_qg_ref[: 2 * HD, :]) * scale).astype(BF16)
+    query_t = (query_gate[: 2 * HD] * scale).astype(BF16)
+    gate_t = jax.nn.sigmoid(query_gate[2 * HD :])
+    att_grad_t = (gated_grad_t * gate_t).astype(BF16)
+    att_grad_f = att_grad_t.astype(F32)
+    att_grad = jnp.transpose(att_grad_f).astype(BF16)
+    zero_wide = jnp.zeros((2 * HD, width), BF16)
+    zero_tall = jnp.zeros((width, 2 * HD), BF16)
+    left_out[: 2 * HD, :] = jnp.concatenate([split_rows(query_t), zero_wide], axis=1)
+    left_out[2 * HD :, :] = jnp.concatenate([zero_wide, split_rows(att_grad_t)], axis=1)
+    right_out[:width, :] = jnp.concatenate([split_cols(query), zero_tall], axis=1)
+    right_out[width:, :] = jnp.concatenate([zero_tall, split_cols(att_grad)], axis=1)
+    gate_out[...] = gate_t
+    gated_grad_out[...] = gated_grad_t
+    att_grad_out[...] = att_grad_f
+    for copy in copies[5:]:
+        copy.wait()
+    chains = chain_ref[...].astype(F32)
+    own_chain = chain_ref[pl.ds(me, 1), :].astype(F32)
+    for block in range(4):
+        rows = slice(block * TILE, (block + 1) * TILE)
+        key_chain = jnp.transpose(jnp.broadcast_to(chains[block : block + 1, :], (TILE, TILE)))
+        apart = jnp.where(tile_ref[me, block] == 1, 0.0, 1.0)
+        banned = jnp.where(key_chain == own_chain, 0.0, apart) > 0.5
+        for head in range(2):
+            bias = bias_ref[:, head, rows].astype(F32)
+            bias_out[rows, head * TILE : (head + 1) * TILE] = jnp.where(
+                banned, NEG_FILL, jnp.transpose(bias)
+            )
+
+
+def attention_kernel(
+    col_ref, x_ref, x1_ref, x2_ref, x3_ref, grad_ref, bias_ref, left_ref, right_ref,
+    gate_ref, gated_grad_ref, att_grad_ref, w_kv_ref,
+    raw_ref, local_ref, key_value_grad_ref,
+    pairs_ref, scores_ref, expo_ref, both_ref,
+):
+    scale = HD ** (-0.5)
+    width = 2 * TILE
+    me = col_ref[0]
+    for bits, ref in enumerate((x_ref, x1_ref, x2_ref, x3_ref)):
+        place = pl.multiple_of(lax.bitwise_xor(me, bits) * TILE, TILE)
+        pairs_ref[pl.ds(place, TILE), :] = ref[...]
+    w_kv = w_kv_ref[...]
+    pairs = pairs_ref[...]
+    key_value = dot_nt(pairs, w_kv).astype(BF16)
+    key_value_t = dot_nt(w_kv, pairs).astype(BF16)
+    left = left_ref[...]
+    top = None
+    for block in range(4):
+        rows = slice(block * TILE, (block + 1) * TILE)
+        product = dot_nn(key_value[rows], left)
+        scores = product[:, :width] + bias_ref[rows, :]
+        scores_ref[rows, :width] = scores
+        scores_ref[rows, width:] = product[:, width:]
+        part = jnp.max(scores.reshape(TILE // 8, 8, width), axis=0)
+        top = part if top is None else jnp.maximum(top, part)
+    top = jnp.max(top, axis=0, keepdims=True)
+    total = jnp.zeros((8, width), F32)
+    for block in range(4):
+        rows = slice(block * TILE, (block + 1) * TILE)
+        expo = jnp.exp(scores_ref[rows, :width] - top)
+        scores_ref[rows, :width] = expo
+        expo_ref[rows, :] = expo.astype(BF16)
+        total = total + jnp.sum(expo.reshape(TILE // 8, 8, width), axis=0)
+    inverse = 1.0 / jnp.sum(total, axis=0, keepdims=True)
+    attended_t = join_rows(dot_nn(key_value_t[2 * HD :], expo_ref[...]) * inverse)
+    gate_t, gated_grad_t = gate_ref[...], gated_grad_ref[...]
+    gated_t = (gate_t * attended_t).astype(BF16)
+    gate_logit_t = gated_grad_t * attended_t * gate_t * (1.0 - gate_t)
+    products = att_grad_ref[...] * attended_t
+    delta = jnp.concatenate(
+        [
+            jnp.sum(products[:HD], axis=0, keepdims=True),
+            jnp.sum(products[HD:], axis=0, keepdims=True),
+        ],
+        axis=1,
+    )
+    for block in range(4):
+        rows = slice(block * TILE, (block + 1) * TILE)
+        prob = scores_ref[rows, :width] * inverse
+        both_ref[rows, :width] = (prob * (scores_ref[rows, width:] - delta)).astype(BF16)
+        both_ref[rows, width:] = prob.astype(BF16)
+    query_grad_t = join_rows(dot_nn(key_value_t[: 2 * HD], both_ref[:, :width])) * scale
+    key_value_grad = dot_nn(both_ref[...], right_ref[...])
+    local_t = jnp.concatenate([query_grad_t, gate_logit_t], axis=0)
+    local_ref[...] = jnp.transpose(local_t).astype(BF16)
+    key_value_grad_ref[...] = key_value_grad.astype(BF16)
+    raw_ref[: 4 * HD, :] = dot_nn(local_t.astype(BF16), x_ref[...]).astype(BF16)
+    raw_ref[4 * HD : 8 * HD, :] = dot_nn(jnp.transpose(key_value_grad).astype(BF16), pairs).astype(BF16)
+    raw_ref[8 * HD :, :] = dot_nn(gated_t, grad_ref[...]).astype(BF16)
+
+
+def parts_kernel(
+    place_ref, key_value_grad_ref, local_ref, w_qg_ref, w_kv_ref, keep_ref, send_ref, parts_ref
+):
+    me, head = place_ref[0], place_ref[1]
+    half = TILE // 2
+    parts_ref[...] = dot_nn(key_value_grad_ref[...], w_kv_ref[...])
+    own = pl.ds(pl.multiple_of(me * TILE, TILE), TILE)
+    parts_ref[own, :] = parts_ref[own, :] + dot_nn(local_ref[...], w_qg_ref[...])
+    for bits in range(4):
+        start = lax.bitwise_xor(me, bits) * TILE
+        mine = pl.multiple_of(start + head * half, half)
+        other = pl.multiple_of(start + (1 - head) * half, half)
+        rows = slice(bits * half, (bits + 1) * half)
+        keep_ref[rows, :] = parts_ref[pl.ds(mine, half), :]
+        send_ref[rows, :] = parts_ref[pl.ds(other, half), :].astype(BF16)
+
+
+def squares_kernel(own_ref, other_ref, total_ref, squares_ref):
+    total = own_ref[...].astype(F32) + other_ref[...].astype(F32)
+    total_ref[...] = total
+    squares_ref[...] = jnp.sum((total * total).reshape(total.shape[0] // 8, 8, C), axis=0)
+
+
+def clip_kernel(total_ref, own_ref, other_ref, query_ref, gate_ref, key_ref, value_ref, out_ref):
+    squares = own_ref[...] + other_ref[...]
+    squares = jnp.sum(jnp.sum(squares, axis=0, keepdims=True), axis=1, keepdims=True)
+    clip = jnp.minimum(1.0, CLIP_NORM / jnp.sqrt(squares + 1e-06))
+    for part, ref in enumerate((query_ref, gate_ref, key_ref, value_ref, out_ref)):
+        ref[...] = total_ref[part * 2 * HD : (part + 1) * 2 * HD, :] * clip
+
+
+VMEM = pl.BlockSpec(memory_space=pltpu.VMEM)
+SMEM = pl.BlockSpec(memory_space=pltpu.SMEM)
+HBM = pl.BlockSpec(memory_space=pltpu.HBM)
+
+
+def on_core(kernel, name, specs, operands, outs, scratch=(), cost=1 << 18):
+    return pl.pallas_call(
+        kernel,
+        out_shape=tuple(jax.ShapeDtypeStruct(shape, dtype) for shape, dtype in outs),
+        in_specs=specs + [VMEM] * (len(operands) - len(specs)),
+        out_specs=(VMEM,) * len(outs),
+        scratch_shapes=scratch,
+        compiler_params=pltpu.CompilerParams(vmem_limit_bytes=16 << 20),
+        cost_estimate=pl.CostEstimate(flops=1 << 20, bytes_accessed=cost, transcendentals=0),
+        name=name,
+    )(
+        *(
+            pltpu.with_memory_space_constraint(operand, pltpu.HBM) if spec is HBM else operand
+            for spec, operand in zip(specs + [VMEM] * len(operands), operands)
+        )
+    )
+
+
+def four_cols(
+    pair, out_grad, pair_bias, w_query, w_key, w_value, w_gate, w_out, tile_mask, chain_ids
+):
+    col_index = lax.axis_index("col")
+    head_index = lax.axis_index("head")
+    col = col_index.reshape(1)
+    width, keys, wide = 2 * HD, 4 * TILE, 2 * TILE
+    x = pair.reshape(TILE, C)
+    x2 = exchange(x, far_col)
+    x1 = exchange(x, next_col)
+    x3 = exchange(x2, next_col)
+    x, grad, w_qg, w_kv, bias, left, right, gate_t, gated_grad_t, att_grad_t = on_core(
+        local_kernel, "local", [SMEM] + [HBM] * 10,
+        (
+            col, tile_mask, x, out_grad.reshape(TILE, C), pair_bias, chain_ids.reshape(4, TILE),
+            w_query.T, w_key.T, w_value.T, w_gate.T, w_out,
+        ),
+        (
+            ((TILE, C), BF16), ((TILE, C), BF16), ((2 * width, C), BF16), ((2 * width, C), BF16),
+            ((keys, wide), F32), ((C, 2 * wide), BF16), ((2 * wide, C), BF16),
+            ((width, TILE), F32), ((width, TILE), F32), ((width, TILE), F32),
+        ),
+        [
+            pltpu.SMEM((4, 4), jnp.int32), pltpu.VMEM((4, TILE), jnp.int32),
+            pltpu.VMEM((width, C), BF16), pltpu.VMEM((TILE, 2, keys), BF16),
+            pltpu.SemaphoreType.DMA((10,)),
+        ],
+    )
+    raw, local, key_value_grad = on_core(
+        attention_kernel, "attention", [SMEM],
+        (col, x, x1, x2, x3, grad, bias, left, right, gate_t, gated_grad_t, att_grad_t, w_kv),
+        (((5 * width, C), BF16), ((TILE, C), BF16), ((keys, C), BF16)),
+        [
+            pltpu.VMEM((keys, C), BF16), pltpu.VMEM((keys, 2 * wide), F32),
+            pltpu.VMEM((keys, wide), BF16), pltpu.VMEM((keys, 2 * wide), BF16),
+        ],
+    )
+
+    def summed(one, two):
+        return (one.astype(F32) + two.astype(F32)).astype(BF16)
+
+    keep, send = on_core(
+        parts_kernel, "parts", [SMEM],
+        (jnp.stack([col_index, head_index]), key_value_grad, local, w_qg, w_kv),
+        (((wide, C), F32), ((wide, C), BF16)), [pltpu.VMEM((keys, C), F32)],
+    )
+    raw = summed(raw, exchange(raw, staggered(other_row, next_col)))
+    raw = summed(raw, exchange(raw, staggered(far_col, other_row)))
+    parts = keep + exchange(send, other_head).astype(F32)
+    parts = parts[:TILE] + exchange(parts[TILE:].astype(BF16), far_col).astype(F32)
+    half = TILE // 2
+    pair_grad = parts[:half] + exchange(parts[half:].astype(BF16), next_col).astype(F32)
+    total, squares = on_core(
+        squares_kernel, "squares", [], (raw, exchange(raw, staggered(next_col, far_col))),
+        (((5 * width, C), F32), ((8, C), F32)),
+    )
+    grads = on_core(
+        clip_kernel, "clip", [], (total, squares, exchange(squares, other_head)),
+        (((width, C), F32),) * 5,
+    )
+    query_grad, gate_grad, key_grad, value_grad, out_weight_grad = grads
+    return (
+        pair_grad.astype(BF16).reshape(1, half, C),
+        query_grad.T,
+        key_grad.T,
+        value_grad.T,
+        gate_grad.T,
+        out_weight_grad,
+    )
+
+
+def per_device(pair, out_grad, pair_bias, *rest):
+    small = lax.axis_size("col") == 4 and lax.axis_size("row") == 2 and lax.axis_size("head") == 2
+    if small and pair.shape == (1, TILE, C) and pair_bias.shape == (TILE, 2, 4 * TILE):
+        return four_cols(pair, out_grad, pair_bias, *rest)
+    return any_cols(pair, out_grad, pair_bias, *rest)
+
+
 def solution(mesh):
     return jax.shard_map(
         per_device,

time: 156 us -> 31.5 us (0.20)
  blocking collectives: 64.2 us -> 0 us
  waiting for transfers between devices: 51.9 us -> 9.05 us
  between operations: 17.7 us -> 0.72 us
  starting transfers between devices: 3.59 us -> 16.1 us
  matrix products: 7.86 us -> 0 us
  local copies, waits for them, and re-layouts: 5.54 us -> 0.01 us
  Pallas kernels: 0 us -> 4.73 us
  other arithmetic: 3.99 us -> 0.76 us
    psum x2 -> x0, blocking collectives: 38.5 us -> none  [the longest x1 35.6 us: per_device(): summed_four, summed_out = lax.psum((raw_four, raw_out), ('col', 'row'))]
    psum x1 -> x0, waiting for transfers between devices: 32.1 us -> none  [per_device(): summed_four, summed_out = lax.psum((raw_four, raw_out), ('col', 'row'))]
    all_gather x2 -> x0, blocking collectives: 25.7 us -> none  [the longest x1 13.7 us: per_device(): key_piece = lax.all_gather(key_grid, 'col', axis=1, tiled=True)]
    ppermute x8 -> x10, starting transfers between devices: 3.5 us -> 16.1 us  [exchange(): return lax.ppermute(value, ('col', 'row', 'head'), pairs)]
    ppermute x8 -> x10, waiting for transfers between devices: 18 us -> 9.05 us  [exchange(): return lax.ppermute(value, ('col', 'row', 'head'), pairs)]
    dot_general x34 -> x0, matrix products: 7.86 us -> none  [the longest x5 1.37 us: allowed_between(): jnp.dot(jnp.dot(query_tiles, tile_mask.astype(jnp.float32)), key_tiles.T)]
    unnamed x26 -> x0, local copies, waits for them, and re-layouts: 4.79 us -> none
    pallas_call x0 -> x5, Pallas kernels: none -> 4.73 us  [on_core(): pl.pallas_call(kernel, out_shape=tuple((jax.ShapeDtypeStruct(shape, dtype...]
  transfers between devices with their start and end apart: 10 -> 10, of which waited for: 10 -> 6; matrix products, arithmetic and copies ran while one was open for 5% -> 2% of each run, Pallas kernels for 0% -> 9%
where the time goes in v2:
time: 31.5 us; the launch traced here: 31.4 us
  starting transfers between devices  16.1 us (51%)
  waiting for transfers between devices  9.05 us (29%)
  Pallas kernels  4.73 us (15%)
  other arithmetic  0.76 us (2%)
  between operations  0.72 us (2%)
    ppermute x10, starting transfers between devices, exchange(): return lax.ppermute(value, ('col', 'row', 'head'), pairs)  16.1 us
    ppermute x10, waiting for transfers between devices, exchange(): return lax.ppermute(value, ('col', 'row', 'head'), pairs)  9.05 us
    pallas_call x5, Pallas kernels, on_core(): pl.pallas_call(kernel, out_shape=tuple((jax.ShapeDtypeStruct(shape, dtype...  4.73 us
  transfers between devices with their start and end apart: 10, of which 6 were waited for; matrix products, arithmetic and copies ran while one was open for 2% of the time, Pallas kernels for 9%

profile of v2, /device:TPU:0, one launch (start us, length us, event | category | flops | bytes accessed | tf_op | source)
XLA Modules:
  0.0 31.4 jit_solution(866324406080031822)
XLA Ops:
  0.6 4.1 %collective-permute-start.1 = (bf16[128,128]{1,0:T(8,128)(2,1)}, bf16[128,128]{1,0:T(8,128)(2,1)S(1)}, u32[]{:S(2)}, u32[]{:S(2)}) collective-permute-start(bf16[128,128]{1,0:T(8,128)(2,1)} %bitcast.16), channel_id=1, source_target_pairs={{0,8},{1,9},{2,10},{3,11},{4,12},{5,13},{6,14},{7,15},{8,0},{9,1},... | collective-permute-start | bytes 98312 | tf_op jit(solution)/shard_map/ppermute | solution.py:193
  4.7 1.6 %collective-permute-start = (bf16[128,128]{1,0:T(8,128)(2,1)}, bf16[128,128]{1,0:T(8,128)(2,1)S(1)}, u32[]{:S(2)}, u32[]{:S(2)}) collective-permute-start(bf16[128,128]{1,0:T(8,128)(2,1)} %bitcast.17), channel_id=1, source_target_pairs={{0,4},{1,5},{2,6},{3,7},{4,0},{5,1},{6,2},{7,3},{8,12},{9,13},{10,... | collective-permute-start | bytes 98312 | tf_op jit(solution)/shard_map/ppermute | solution.py:193
  6.3 1.0 %collective-permute-done.1.x2_ref = bf16[128,128]{1,0:T(8,128)(2,1)S(1)} collective-permute-done((bf16[128,128]{1,0:T(8,128)(2,1)}, bf16[128,128]{1,0:T(8,128)(2,1)S(1)}, u32[]{:S(2)}, u32[]{:S(2)}) %collective-permute-start.1) | collective-permute-done | bytes 32800 | tf_op jit(solution)/shard_map/ppermute | solution.py:193
  7.3 1.5 %collective-permute-start.2 = (bf16[128,128]{1,0:T(8,128)(2,1)S(1)}, bf16[128,128]{1,0:T(8,128)(2,1)S(1)}, u32[]{:S(2)}, u32[]{:S(2)}) collective-permute-start(bf16[128,128]{1,0:T(8,128)(2,1)S(1)} %collective-permute-done.1.x2_ref), channel_id=1, source_target_pairs={{0,4},{1,5},{2,6},{3,7},{4,0},{5,1},{6,2},{7,3},{8,12},{9,13},{10,... | collective-permute-start | bytes 98312 | tf_op jit(solution)/shard_map/ppermute | solution.py:193
  8.8 1.9 %local.1 = (bf16[128,128]{1,0:T(8,128)(2,1)S(1)}, bf16[128,128]{1,0:T(8,128)(2,1)S(1)}, bf16[128,128]{1,0:T(8,128)(2,1)S(1)}, bf16[128,128]{1,0:T(8,128)(2,1)S(1...) custom-call(s32[1]{0:T(128)} %bitcast.col_ref, ...), custom_call_target="tpu_custom_call" | custom-call | flops 1048576 | bytes 262144 | tf_op jit(solution)/shard_map/local/pallas_call | solution.py:403
  10.7 0.6 %collective-permute-done.2.x3_ref = bf16[128,128]{1,0:T(8,128)(2,1)S(1)} collective-permute-done((bf16[128,128]{1,0:T(8,128)(2,1)S(1)}, bf16[128,128]{1,0:T(8,128)(2,1)S(1)}, u32[]{:S(2)}, u32[]{:S(2)}) %collective-permute-start.2) | collective-permute-done | bytes 32800 | tf_op jit(solution)/shard_map/ppermute | solution.py:193
  11.2 1.3 %attention.1 = (bf16[320,128]{1,0:T(8,128)(2,1)S(1)}, bf16[128,128]{1,0:T(8,128)(2,1)S(1)}, bf16[512,128]{1,0:T(8,128)(2,1)S(1)}) custom-call(s32[1]{0:T(128)} %bitcast.col_ref, bf16[128,128]{1,0:T(8,128)(2,1)S(1)} %get-tuple-element.28.x_ref, bf16[128,128]{1,0:T(8,128)(2,1)S(1)} %collective-permute-done.x1_ref, ...), custom_call_target="tpu_custom_call" | custom-call | flops 1048576 | bytes 262144 | tf_op jit(solution)/shard_map/attention/pallas_call | solution.py:403
  12.5 1.7 %collective-permute-start.6 = (bf16[320,128]{1,0:T(8,128)(2,1)S(1)}, bf16[320,128]{1,0:T(8,128)(2,1)S(1)}, u32[]{:S(2)}, u32[]{:S(2)}) collective-permute-start(bf16[320,128]{1,0:T(8,128)(2,1)S(1)} %get-tuple-element.42), channel_id=1, source_target_pairs={{0,2},{1,5},{2,0},{3,7},{4,6},{5,1},{6,4},{7,3},{8,10},{9,13},{10,... | collective-permute-start | bytes 245768 | tf_op jit(solution)/shard_map/ppermute | solution.py:193
  14.2 0.1 pad_add_fusion.place_ref
  14.3 0.8 %parts.1 = (f32[256,128]{1,0:T(8,128)S(1)}, bf16[256,128]{1,0:T(8,128)(2,1)S(1)}) custom-call(s32[2]{0:T(128)S(1)} %pad_add_fusion.place_ref, bf16[512,128]{1,0:T(8,128)(2,1)S(1)} %get-tuple-element.37.key_value_grad_ref, bf16[128,128]{1,0:T(8,128)(2,1)S(1)} %get-tuple-element.38.local_ref, bf16[128,128]{1,0:T(8,128)(2,1)S(1)} %get-tuple-element.39.w_qg_ref, ...), custom_call_target="tpu_custom_call" | custom-call | flops 1048576 | bytes 262144 | tf_op jit(solution)/shard_map/parts/pallas_call | solution.py:403
  15.0 0.1 collective-permute-start.3
  15.1 1.9 %collective-permute-done.6 = bf16[320,128]{1,0:T(8,128)(2,1)S(1)} collective-permute-done((bf16[320,128]{1,0:T(8,128)(2,1)S(1)}, bf16[320,128]{1,0:T(8,128)(2,1)S(1)}, u32[]{:S(2)}, u32[]{:S(2)}) %collective-permute-start.6) | collective-permute-done | bytes 81952 | tf_op jit(solution)/shard_map/ppermute | solution.py:193
  17.0 2.7 %collective-permute-start.7 = (bf16[320,128]{1,0:T(8,128)(2,1)S(1)}, bf16[320,128]{1,0:T(8,128)(2,1)S(1)}, u32[]{:S(2)}, u32[]{:S(2)}) collective-permute-start(bf16[320,128]{1,0:T(8,128)(2,1)S(1)} %add_convert_fusion.1), channel_id=1, source_target_pairs={{0,8},{1,3},{2,10},{3,1},{4,12},{5,7},{6,14},{7,5},{8,0},{9,11},{1... | collective-permute-start | bytes 245768 | tf_op jit(solution)/shard_map/ppermute | solution.py:193
  19.8 0.0 collective-permute-done.3
  19.8 0.3 %collective-permute-start.4 = (bf16[128,128]{1,0:T(8,128)(2,1)S(1)}, bf16[128,128]{1,0:T(8,128)(2,1)S(1)}, u32[]{:S(2)}, u32[]{:S(2)}) collective-permute-start(bf16[128,128]{1,0:T(8,128)(2,1)S(1)} %slice.30), channel_id=1, source_target_pairs={{0,8},{1,9},{2,10},{3,11},{4,12},{5,13},{6,14},{7,15},{8,0},{9,1},... | collective-permute-start | bytes 98312 | tf_op jit(solution)/shard_map/ppermute | solution.py:193
  20.1 2.3 %collective-permute-done.7 = bf16[320,128]{1,0:T(8,128)(2,1)S(1)} collective-permute-done((bf16[320,128]{1,0:T(8,128)(2,1)S(1)}, bf16[320,128]{1,0:T(8,128)(2,1)S(1)}, u32[]{:S(2)}, u32[]{:S(2)}) %collective-permute-start.7) | collective-permute-done | bytes 81952 | tf_op jit(solution)/shard_map/ppermute | solution.py:193
  22.5 3.7 %collective-permute-start.8 = (bf16[320,128]{1,0:T(8,128)(2,1)S(1)}, bf16[320,128]{1,0:T(8,128)(2,1)S(1)}, u32[]{:S(2)}, u32[]{:S(2)}) collective-permute-start(bf16[320,128]{1,0:T(8,128)(2,1)S(1)} %add_convert_fusion.own_ref), channel_id=1, source_target_pairs={{0,4},{1,9},{2,6},{3,11},{4,0},{5,13},{6,2},{7,15},{8,12},{9,1},{1... | collective-permute-start | bytes 245768 | tf_op jit(solution)/shard_map/ppermute | solution.py:193
  26.2 0.0 collective-permute-done.4
  26.2 0.4 %collective-permute-start.5 = (bf16[64,128]{1,0:T(8,128)(2,1)S(1)}, bf16[64,128]{1,0:T(8,128)(2,1)S(1)}, u32[]{:S(2)}, u32[]{:S(2)}) collective-permute-start(bf16[64,128]{1,0:T(8,128)(2,1)S(1)} %slice.31), channel_id=1, source_target_pairs={{0,4},{1,5},{2,6},{3,7},{4,0},{5,1},{6,2},{7,3},{8,12},{9,13},{10,... | collective-permute-start | bytes 49160 | tf_op jit(solution)/shard_map/ppermute | solution.py:193
  26.6 2.0 %collective-permute-done.8.other_ref = bf16[320,128]{1,0:T(8,128)(2,1)S(1)} collective-permute-done((bf16[320,128]{1,0:T(8,128)(2,1)S(1)}, bf16[320,128]{1,0:T(8,128)(2,1)S(1)}, u32[]{:S(2)}, u32[]{:S(2)}) %collective-permute-start.8) | collective-permute-done | bytes 81952 | tf_op jit(solution)/shard_map/ppermute | solution.py:193
  28.6 0.1 collective-permute-start.9
  28.7 1.3 %collective-permute-done.5 = bf16[64,128]{1,0:T(8,128)(2,1)S(1)} collective-permute-done((bf16[64,128]{1,0:T(8,128)(2,1)S(1)}, bf16[64,128]{1,0:T(8,128)(2,1)S(1)}, u32[]{:S(2)}, u32[]{:S(2)}) %collective-permute-start.5) | collective-permute-done | bytes 16416 | tf_op jit(solution)/shard_map/ppermute | solution.py:193
  30.0 0.6 %fusion.1 = bf16[1,64,128]{2,1,0:T(8,128)(2,1)} fusion(bf16[64,128]{1,0:T(8,128)(2,1)S(1)} %collective-permute-done.5, f32[128,128]{1,0:T(8,128)S(1)} %slice_add_fusion), kind=kLoop, calls=%fused_computation.8 | loop fusion | flops 24576 | bytes 65536 | tf_op jit(solution)/shard_map/reshape | solution.py:482
  30.6 0.8 %clip.1 = (f32[64,128]{1,0:T(8,128)}, f32[64,128]{1,0:T(8,128)}, f32[64,128]{1,0:T(8,128)}, f32[64,128]{1,0:T(8,128)}, f32[64,128]{1,0:T(8,128)}) custom-call(f32[320,128]{1,0:T(8,128)S(1)} %get-tuple-element.43.total_ref, f32[8,128]{1,0:T(8,128)S(1)} %get-tuple-element.44.own_ref, f32[8,128]{1,0:T(8,128)S(1)} %collective-permute-done.9.other_ref), custom_call_target="tpu_custom_call" | custom-call | flops 1048576 | bytes 262144 | tf_op jit(solution)/shard_map/clip/pallas_call | solution.py:403
  (9 shorter events, 0.1 us)
Async XLA Ops:
  0.6 6.7 %collective-permute-start.1 = (bf16[128,128]{1,0:T(8,128)(2,1)}, bf16[128,128]{1,0:T(8,128)(2,1)S(1)}, u32[]{:S(2)}, u32[]{:S(2)}) collective-permute-start(bf16[128,128]{1,0:T(8,128)(2,1)} %bitcast.16), channel_id=1, source_target_pairs={{0,8},{1,9},{2,10},{3,11},{4,12},{5,13},{6,14},{7,15},{8,0},{9,1},... | collective-permute-start | bytes 98312 | tf_op jit(solution)/shard_map/ppermute | solution.py:193
  4.7 5.9 %collective-permute-start = (bf16[128,128]{1,0:T(8,128)(2,1)}, bf16[128,128]{1,0:T(8,128)(2,1)S(1)}, u32[]{:S(2)}, u32[]{:S(2)}) collective-permute-start(bf16[128,128]{1,0:T(8,128)(2,1)} %bitcast.17), channel_id=1, source_target_pairs={{0,4},{1,5},{2,6},{3,7},{4,0},{5,1},{6,2},{7,3},{8,12},{9,13},{10,... | collective-permute-start | bytes 98312 | tf_op jit(solution)/shard_map/ppermute | solution.py:193
  7.3 3.9 %collective-permute-start.2 = (bf16[128,128]{1,0:T(8,128)(2,1)S(1)}, bf16[128,128]{1,0:T(8,128)(2,1)S(1)}, u32[]{:S(2)}, u32[]{:S(2)}) collective-permute-start(bf16[128,128]{1,0:T(8,128)(2,1)S(1)} %collective-permute-done.1.x2_ref), channel_id=1, source_target_pairs={{0,4},{1,5},{2,6},{3,7},{4,0},{5,1},{6,2},{7,3},{8,12},{9,13},{10,... | collective-permute-start | bytes 98312 | tf_op jit(solution)/shard_map/ppermute | solution.py:193
  12.5 4.5 %collective-permute-start.6 = (bf16[320,128]{1,0:T(8,128)(2,1)S(1)}, bf16[320,128]{1,0:T(8,128)(2,1)S(1)}, u32[]{:S(2)}, u32[]{:S(2)}) collective-permute-start(bf16[320,128]{1,0:T(8,128)(2,1)S(1)} %get-tuple-element.42), channel_id=1, source_target_pairs={{0,2},{1,5},{2,0},{3,7},{4,6},{5,1},{6,4},{7,3},{8,10},{9,13},{10,... | collective-permute-start | bytes 245768 | tf_op jit(solution)/shard_map/ppermute | solution.py:193
  15.0 4.7 %collective-permute-start.3 = (bf16[256,128]{1,0:T(8,128)(2,1)S(1)}, bf16[256,128]{1,0:T(8,128)(2,1)S(1)}, u32[]{:S(2)}, u32[]{:S(2)}) collective-permute-start(bf16[256,128]{1,0:T(8,128)(2,1)S(1)} %get-tuple-element.41), channel_id=1, source_target_pairs={{0,1},{1,0},{2,3},{3,2},{4,5},{5,4},{6,7},{7,6},{8,9},{9,8},{10,11... | collective-permute-start | bytes 196616 | tf_op jit(solution)/shard_map/ppermute | solution.py:193
  17.0 5.4 %collective-permute-start.7 = (bf16[320,128]{1,0:T(8,128)(2,1)S(1)}, bf16[320,128]{1,0:T(8,128)(2,1)S(1)}, u32[]{:S(2)}, u32[]{:S(2)}) collective-permute-start(bf16[320,128]{1,0:T(8,128)(2,1)S(1)} %add_convert_fusion.1), channel_id=1, source_target_pairs={{0,8},{1,3},{2,10},{3,1},{4,12},{5,7},{6,14},{7,5},{8,0},{9,11},{1... | collective-permute-start | bytes 245768 | tf_op jit(solution)/shard_map/ppermute | solution.py:193
  19.8 6.4 %collective-permute-start.4 = (bf16[128,128]{1,0:T(8,128)(2,1)S(1)}, bf16[128,128]{1,0:T(8,128)(2,1)S(1)}, u32[]{:S(2)}, u32[]{:S(2)}) collective-permute-start(bf16[128,128]{1,0:T(8,128)(2,1)S(1)} %slice.30), channel_id=1, source_target_pairs={{0,8},{1,9},{2,10},{3,11},{4,12},{5,13},{6,14},{7,15},{8,0},{9,1},... | collective-permute-start | bytes 98312 | tf_op jit(solution)/shard_map/ppermute | solution.py:193
  22.5 6.1 %collective-permute-start.8 = (bf16[320,128]{1,0:T(8,128)(2,1)S(1)}, bf16[320,128]{1,0:T(8,128)(2,1)S(1)}, u32[]{:S(2)}, u32[]{:S(2)}) collective-permute-start(bf16[320,128]{1,0:T(8,128)(2,1)S(1)} %add_convert_fusion.own_ref), channel_id=1, source_target_pairs={{0,4},{1,9},{2,6},{3,11},{4,0},{5,13},{6,2},{7,15},{8,12},{9,1},{1... | collective-permute-start | bytes 245768 | tf_op jit(solution)/shard_map/ppermute | solution.py:193
  26.2 3.8 %collective-permute-start.5 = (bf16[64,128]{1,0:T(8,128)(2,1)S(1)}, bf16[64,128]{1,0:T(8,128)(2,1)S(1)}, u32[]{:S(2)}, u32[]{:S(2)}) collective-permute-start(bf16[64,128]{1,0:T(8,128)(2,1)S(1)} %slice.31), channel_id=1, source_target_pairs={{0,4},{1,5},{2,6},{3,7},{4,0},{5,1},{6,2},{7,3},{8,12},{9,13},{10,... | collective-permute-start | bytes 49160 | tf_op jit(solution)/shard_map/ppermute | solution.py:193
  28.6 2.0 %collective-permute-start.9 = (f32[8,128]{1,0:T(8,128)S(1)}, f32[8,128]{1,0:T(8,128)S(1)}, u32[]{:S(2)}, u32[]{:S(2)}) collective-permute-start(f32[8,128]{1,0:T(8,128)S(1)} %get-tuple-element.44.own_ref), channel_id=1, source_target_pairs={{0,1},{1,0},{2,3},{3,2},{4,5},{5,4},{6,7},{7,6},{8,9},{9,8},{10,11... | collective-permute-start | bytes 12296 | tf_op jit(solution)/shard_map/ppermute | solution.py:193

commit v3 on v2

--- a/solution.py
+++ b/solution.py
@@ -199,6 +199,10 @@
 
 def far_col(col, row, head):
     return col ^ 2, row, head
+
+
+def end_col(col, row, head):
+    return col ^ 3, row, head
 
 
 def other_row(col, row, head):
@@ -302,15 +306,15 @@
 
 
 def attention_kernel(
-    col_ref, x_ref, x1_ref, x2_ref, x3_ref, grad_ref, bias_ref, left_ref, right_ref,
+    col_ref, head_ref, x_ref, next_ref, direct_ref, crossed_ref, grad_ref, bias_ref, left_ref, right_ref,
     gate_ref, gated_grad_ref, att_grad_ref, w_kv_ref,
     raw_ref, local_ref, key_value_grad_ref,
     pairs_ref, scores_ref, expo_ref, both_ref,
 ):
     scale = HD ** (-0.5)
     width = 2 * TILE
-    me = col_ref[0]
-    for bits, ref in enumerate((x_ref, x1_ref, x2_ref, x3_ref)):
+    me, head = col_ref[0], head_ref[0]
+    for bits, ref in ((0, x_ref), (1, next_ref), (2 + head, direct_ref), (3 - head, crossed_ref)):
         place = pl.multiple_of(lax.bitwise_xor(me, bits) * TILE, TILE)
         pairs_ref[pl.ds(place, TILE), :] = ref[...]
     w_kv = w_kv_ref[...]
@@ -364,9 +368,9 @@
 
 
 def parts_kernel(
-    place_ref, key_value_grad_ref, local_ref, w_qg_ref, w_kv_ref, keep_ref, send_ref, parts_ref
+    col_ref, head_ref, key_value_grad_ref, local_ref, w_qg_ref, w_kv_ref, keep_ref, send_ref, parts_ref
 ):
-    me, head = place_ref[0], place_ref[1]
+    me, head = col_ref[0], head_ref[0]
     half = TILE // 2
     parts_ref[...] = dot_nn(key_value_grad_ref[...], w_kv_ref[...])
     own = pl.ds(pl.multiple_of(me * TILE, TILE), TILE)
@@ -425,9 +429,9 @@
     col = col_index.reshape(1)
     width, keys, wide = 2 * HD, 4 * TILE, 2 * TILE
     x = pair.reshape(TILE, C)
-    x2 = exchange(x, far_col)
-    x1 = exchange(x, next_col)
-    x3 = exchange(x2, next_col)
+    head = head_index.reshape(1)
+    x_direct = exchange(x, staggered(far_col, end_col))
+    x_next = exchange(x, next_col)
     x, grad, w_qg, w_kv, bias, left, right, gate_t, gated_grad_t, att_grad_t = on_core(
         local_kernel, "local", [SMEM] + [HBM] * 10,
         (
@@ -445,9 +449,11 @@
             pltpu.SemaphoreType.DMA((10,)),
         ],
     )
+    x_direct, w_kv = lax.optimization_barrier((x_direct, w_kv))
+    x_crossed = exchange(x_direct, other_head)
     raw, local, key_value_grad = on_core(
-        attention_kernel, "attention", [SMEM],
-        (col, x, x1, x2, x3, grad, bias, left, right, gate_t, gated_grad_t, att_grad_t, w_kv),
+        attention_kernel, "attention", [SMEM, SMEM],
+        (col, head, x, x_next, x_direct, x_crossed, grad, bias, left, right, gate_t, gated_grad_t, att_grad_t, w_kv),
         (((5 * width, C), BF16), ((TILE, C), BF16), ((keys, C), BF16)),
         [
             pltpu.VMEM((keys, C), BF16), pltpu.VMEM((keys, 2 * wide), F32),
@@ -459,19 +465,23 @@
         return (one.astype(F32) + two.astype(F32)).astype(BF16)
 
     keep, send = on_core(
-        parts_kernel, "parts", [SMEM],
-        (jnp.stack([col_index, head_index]), key_value_grad, local, w_qg, w_kv),
+        parts_kernel, "parts", [SMEM, SMEM], (col, head, key_value_grad, local, w_qg, w_kv),
         (((wide, C), F32), ((wide, C), BF16)), [pltpu.VMEM((keys, C), F32)],
     )
+    half = TILE // 2
     raw = summed(raw, exchange(raw, staggered(other_row, next_col)))
+    parts = keep + exchange(send, other_head).astype(F32)
+    kept, sent = parts[:TILE], parts[TILE:].astype(BF16)
+    raw, kept = lax.optimization_barrier((raw, kept))
+    parts = kept + exchange(sent, far_col).astype(F32)
     raw = summed(raw, exchange(raw, staggered(far_col, other_row)))
-    parts = keep + exchange(send, other_head).astype(F32)
-    parts = parts[:TILE] + exchange(parts[TILE:].astype(BF16), far_col).astype(F32)
-    half = TILE // 2
-    pair_grad = parts[:half] + exchange(parts[half:].astype(BF16), next_col).astype(F32)
+    kept, sent = parts[:half], parts[half:].astype(BF16)
+    raw, kept = lax.optimization_barrier((raw, kept))
+    pair_grad = (kept + exchange(sent, next_col).astype(F32)).astype(BF16)
+    last = exchange(raw, staggered(next_col, far_col))
+    last, pair_grad = lax.optimization_barrier((last, pair_grad))
     total, squares = on_core(
-        squares_kernel, "squares", [], (raw, exchange(raw, staggered(next_col, far_col))),
-        (((5 * width, C), F32), ((8, C), F32)),
+        squares_kernel, "squares", [], (raw, last), (((5 * width, C), F32), ((8, C), F32)),
     )
     grads = on_core(
         clip_kernel, "clip", [], (total, squares, exchange(squares, other_head)),
@@ -479,7 +489,7 @@
     )
     query_grad, gate_grad, key_grad, value_grad, out_weight_grad = grads
     return (
-        pair_grad.astype(BF16).reshape(1, half, C),
+        pair_grad.reshape(1, half, C),
         query_grad.T,
         key_grad.T,
         value_grad.T,

time: 31.5 us -> 28.7 us (0.911)
  starting transfers between devices: 16.1 us -> 12.9 us
  local copies, waits for them, and re-layouts: 0.01 us -> 1.24 us
  Pallas kernels: 4.73 us -> 4.19 us
    ppermute x10, starting transfers between devices: 16.1 us -> 12.9 us  [exchange(): return lax.ppermute(value, ('col', 'row', 'head'), pairs)]
    unnamed x0 -> x4, local copies, waits for them, and re-layouts: none -> 1.22 us
    convert_element_type x0 -> x1, other arithmetic: none -> 0.61 us  [four_cols(): pair_grad = (kept + exchange(sent, next_col).astype(F32)).astype(BF16)]
    reshape x1 -> x0, other arithmetic: 0.61 us -> none  [four_cols(): pair_grad.astype(BF16).reshape(1, half, C)]
    pallas_call x5, Pallas kernels: 4.73 us -> 4.19 us  [on_core(): pl.pallas_call(kernel, out_shape=tuple((jax.ShapeDtypeStruct(shape, dtype...]
  transfers between devices with their start and end apart: 10 -> 10, of which waited for: 6 -> 8; matrix products, arithmetic and copies ran while one was open for 2% -> 2% of each run, Pallas kernels for 9% -> 7%
where the time goes in v3:
time: 28.7 us; the launch traced here: 28.6 us
  starting transfers between devices  12.9 us (45%)
  waiting for transfers between devices  8.86 us (31%)
  Pallas kernels  4.19 us (15%)
  local copies, waits for them, and re-layouts  1.24 us (4%)
  between operations  0.74 us (3%)
  other arithmetic  0.69 us (2%)
    ppermute x10, starting transfers between devices, exchange(): return lax.ppermute(value, ('col', 'row', 'head'), pairs)  12.9 us
    ppermute x10, waiting for transfers between devices, exchange(): return lax.ppermute(value, ('col', 'row', 'head'), pairs)  8.86 us
    pallas_call x5, Pallas kernels, on_core(): pl.pallas_call(kernel, out_shape=tuple((jax.ShapeDtypeStruct(shape, dtype...  4.19 us
    unnamed x4, local copies, waits for them, and re-layouts  1.22 us
    convert_element_type x1, other arithmetic, four_cols(): pair_grad = (kept + exchange(sent, next_col).astype(F32)).astype(BF16)  0.61 us
  transfers between devices with their start and end apart: 10, of which 8 were waited for; matrix products, arithmetic and copies ran while one was open for 2% of the time, Pallas kernels for 7%

profile of v3, /device:TPU:0, one launch (start us, length us, event | category | flops | bytes accessed | tf_op | source)
XLA Modules:
  0.0 28.6 jit_solution(12497818781090286887)
XLA Ops:
  0.6 4.1 %collective-permute-start.1 = (bf16[128,128]{1,0:T(8,128)(2,1)}, bf16[128,128]{1,0:T(8,128)(2,1)S(1)}, u32[]{:S(2)}, u32[]{:S(2)}) collective-permute-start(bf16[128,128]{1,0:T(8,128)(2,1)} %bitcast.15), channel_id=1, source_target_pairs={{0,8},{1,13},{2,10},{3,15},{4,12},{5,9},{6,14},{7,11},{8,0},{9,5},... | collective-permute-start | bytes 98312 | tf_op jit(solution)/shard_map/ppermute | solution.py:193
  4.7 1.6 %collective-permute-start = (bf16[128,128]{1,0:T(8,128)(2,1)}, bf16[128,128]{1,0:T(8,128)(2,1)S(1)}, u32[]{:S(2)}, u32[]{:S(2)}) collective-permute-start(bf16[128,128]{1,0:T(8,128)(2,1)} %bitcast.16), channel_id=1, source_target_pairs={{0,4},{1,5},{2,6},{3,7},{4,0},{5,1},{6,2},{7,3},{8,12},{9,13},{10,... | collective-permute-start | bytes 98312 | tf_op jit(solution)/shard_map/ppermute | solution.py:193
  6.3 1.9 %local.1 = (bf16[128,128]{1,0:T(8,128)(2,1)S(1)}, bf16[128,128]{1,0:T(8,128)(2,1)S(1)}, bf16[128,128]{1,0:T(8,128)(2,1)S(1)}, bf16[128,128]{1,0:T(8,128)(2,1)S(1...) custom-call(s32[1]{0:T(128)} %bitcast.col_ref, ...), custom_call_target="tpu_custom_call" | custom-call | flops 1048576 | bytes 262144 | tf_op jit(solution)/shard_map/local/pallas_call | solution.py:407
  8.2 0.1 collective-permute-start.2
  8.3 0.6 %collective-permute-done.next_ref = bf16[128,128]{1,0:T(8,128)(2,1)S(1)} collective-permute-done((bf16[128,128]{1,0:T(8,128)(2,1)}, bf16[128,128]{1,0:T(8,128)(2,1)S(1)}, u32[]{:S(2)}, u32[]{:S(2)}) %collective-permute-start) | collective-permute-done | bytes 32800 | tf_op jit(solution)/shard_map/ppermute | solution.py:193
  8.9 0.6 %collective-permute-done.2.crossed_ref = bf16[128,128]{1,0:T(8,128)(2,1)S(1)} collective-permute-done((bf16[128,128]{1,0:T(8,128)(2,1)S(1)}, bf16[128,128]{1,0:T(8,128)(2,1)S(1)}, u32[]{:S(2)}, u32[]{:S(2)}) %collective-permute-start.2) | collective-permute-done | bytes 32800 | tf_op jit(solution)/shard_map/ppermute | solution.py:193
  9.5 1.3 %attention.1 = (bf16[320,128]{1,0:T(8,128)(2,1)S(1)}, bf16[128,128]{1,0:T(8,128)(2,1)S(1)}, bf16[512,128]{1,0:T(8,128)(2,1)S(1)}) custom-call(s32[1]{0:T(128)} %bitcast.col_ref, s32[1]{0:T(128)} %bitcast.1.head_ref, bf16[128,128]{1,0:T(8,128)(2,1)S(1)} %get-tuple-element.36.x_ref, bf16[128,128]{1,0:T(8,128)(2,1)S(1)} %collective-permute-done.next_ref, ...), custom_call_target="tpu_custom_call" | custom-call | flops 1048576 | bytes 262144 | tf_op jit(solution)/shard_map/attention/pallas_call | solution.py:407
  10.8 0.2 parts.1
  11.0 0.2 collective-permute-start.4
  11.2 1.5 %collective-permute-start.3 = (bf16[320,128]{1,0:T(8,128)(2,1)S(1)}, bf16[320,128]{1,0:T(8,128)(2,1)S(1)}, u32[]{:S(2)}, u32[]{:S(2)}) collective-permute-start(bf16[320,128]{1,0:T(8,128)(2,1)S(1)} %get-tuple-element.47), channel_id=1, source_target_pairs={{0,2},{1,5},{2,0},{3,7},{4,6},{5,1},{6,4},{7,3},{8,10},{9,13},{10,... | collective-permute-start | bytes 245768 | tf_op jit(solution)/shard_map/ppermute | solution.py:193
  12.8 0.6 %copy-done = f32[256,128]{1,0:T(8,128)} copy-done((f32[256,128]{1,0:T(8,128)}, f32[256,128]{1,0:T(8,128)S(1)}, u32[]{:S(2)}) %copy-start) | copy-done | bytes 131096
  13.4 1.8 %collective-permute-start.6 = (bf16[128,128]{1,0:T(8,128)(2,1)S(1)}, bf16[128,128]{1,0:T(8,128)(2,1)S(1)}, u32[]{:S(2)}, u32[]{:S(2)}) collective-permute-start(bf16[128,128]{1,0:T(8,128)(2,1)S(1)} %slice.24), channel_id=1, source_target_pairs={{0,8},{1,9},{2,10},{3,11},{4,12},{5,13},{6,14},{7,15},{8,0},{9,1},... | collective-permute-start | bytes 98312 | tf_op jit(solution)/shard_map/ppermute | solution.py:193
  15.2 0.5 %collective-permute-done.3 = bf16[320,128]{1,0:T(8,128)(2,1)S(1)} collective-permute-done((bf16[320,128]{1,0:T(8,128)(2,1)S(1)}, bf16[320,128]{1,0:T(8,128)(2,1)S(1)}, u32[]{:S(2)}, u32[]{:S(2)}) %collective-permute-start.3) | collective-permute-done | bytes 81952 | tf_op jit(solution)/shard_map/ppermute | solution.py:193
  15.7 1.9 %collective-permute-start.5 = (bf16[320,128]{1,0:T(8,128)(2,1)S(1)}, bf16[320,128]{1,0:T(8,128)(2,1)S(1)}, u32[]{:S(2)}, u32[]{:S(2)}) collective-permute-start(bf16[320,128]{1,0:T(8,128)(2,1)S(1)} %add_convert_fusion.1), channel_id=1, source_target_pairs={{0,8},{1,3},{2,10},{3,1},{4,12},{5,7},{6,14},{7,5},{8,0},{9,11},{1... | collective-permute-start | bytes 245768 | tf_op jit(solution)/shard_map/ppermute | solution.py:193
  17.6 0.6 %collective-permute-done.6 = bf16[128,128]{1,0:T(8,128)(2,1)S(1)} collective-permute-done((bf16[128,128]{1,0:T(8,128)(2,1)S(1)}, bf16[128,128]{1,0:T(8,128)(2,1)S(1)}, u32[]{:S(2)}, u32[]{:S(2)}) %collective-permute-start.6) | collective-permute-done | bytes 32800 | tf_op jit(solution)/shard_map/ppermute | solution.py:193
  18.3 0.6 %copy-done.1 = f32[128,128]{1,0:T(8,128)} copy-done((f32[128,128]{1,0:T(8,128)}, f32[128,128]{1,0:T(8,128)S(1)}, u32[]{:S(2)}) %copy-start.1) | copy-done | bytes 65560
  18.9 1.1 %collective-permute-start.8 = (bf16[64,128]{1,0:T(8,128)(2,1)S(1)}, bf16[64,128]{1,0:T(8,128)(2,1)S(1)}, u32[]{:S(2)}, u32[]{:S(2)}) collective-permute-start(bf16[64,128]{1,0:T(8,128)(2,1)S(1)} %slice.25), channel_id=1, source_target_pairs={{0,4},{1,5},{2,6},{3,7},{4,0},{5,1},{6,2},{7,3},{8,12},{9,13},{10,... | collective-permute-start | bytes 49160 | tf_op jit(solution)/shard_map/ppermute | solution.py:193
  19.9 2.1 %collective-permute-done.5 = bf16[320,128]{1,0:T(8,128)(2,1)S(1)} collective-permute-done((bf16[320,128]{1,0:T(8,128)(2,1)S(1)}, bf16[320,128]{1,0:T(8,128)(2,1)S(1)}, u32[]{:S(2)}, u32[]{:S(2)}) %collective-permute-start.5) | collective-permute-done | bytes 81952 | tf_op jit(solution)/shard_map/ppermute | solution.py:193
  22.0 0.5 %collective-permute-start.7 = (bf16[320,128]{1,0:T(8,128)(2,1)S(1)}, bf16[320,128]{1,0:T(8,128)(2,1)S(1)}, u32[]{:S(2)}, u32[]{:S(2)}) collective-permute-start(bf16[320,128]{1,0:T(8,128)(2,1)S(1)} %add_convert_fusion.own_ref), channel_id=1, source_target_pairs={{0,4},{1,9},{2,6},{3,11},{4,0},{5,13},{6,2},{7,15},{8,12},{9,1},{1... | collective-permute-start | bytes 245768 | tf_op jit(solution)/shard_map/ppermute | solution.py:193
  22.6 0.5 %collective-permute-done.8 = bf16[64,128]{1,0:T(8,128)(2,1)S(1)} collective-permute-done((bf16[64,128]{1,0:T(8,128)(2,1)S(1)}, bf16[64,128]{1,0:T(8,128)(2,1)S(1)}, u32[]{:S(2)}, u32[]{:S(2)}) %collective-permute-start.8) | collective-permute-done | bytes 16416 | tf_op jit(solution)/shard_map/ppermute | solution.py:193
  23.1 0.6 %add_convert_fusion.2 = bf16[64,128]{1,0:T(8,128)(2,1)} fusion(f32[64,128]{1,0:T(8,128)S(1)} %slice-done.1, bf16[64,128]{1,0:T(8,128)(2,1)S(1)} %collective-permute-done.8), kind=kLoop, calls=%fused_computation.6 | loop fusion | flops 24576 | bytes 65536 | tf_op jit(solution)/shard_map/convert_element_type | solution.py:480
  23.7 2.8 %collective-permute-done.7.other_ref = bf16[320,128]{1,0:T(8,128)(2,1)S(1)} collective-permute-done((bf16[320,128]{1,0:T(8,128)(2,1)S(1)}, bf16[320,128]{1,0:T(8,128)(2,1)S(1)}, u32[]{:S(2)}, u32[]{:S(2)}) %collective-permute-start.7) | collective-permute-done | bytes 81952 | tf_op jit(solution)/shard_map/ppermute | solution.py:193
  26.7 1.2 %collective-permute-done.9.other_ref = f32[8,128]{1,0:T(8,128)S(1)} collective-permute-done((f32[8,128]{1,0:T(8,128)S(1)}, f32[8,128]{1,0:T(8,128)S(1)}, u32[]{:S(2)}, u32[]{:S(2)}) %collective-permute-start.9) | collective-permute-done | bytes 4128 | tf_op jit(solution)/shard_map/ppermute | solution.py:193
  27.8 0.8 %clip.1 = (f32[64,128]{1,0:T(8,128)}, f32[64,128]{1,0:T(8,128)}, f32[64,128]{1,0:T(8,128)}, f32[64,128]{1,0:T(8,128)}, f32[64,128]{1,0:T(8,128)}) custom-call(f32[320,128]{1,0:T(8,128)S(1)} %get-tuple-element.59.total_ref, f32[8,128]{1,0:T(8,128)S(1)} %get-tuple-element.60.own_ref, f32[8,128]{1,0:T(8,128)S(1)} %collective-permute-done.9.other_ref), custom_call_target="tpu_custom_call" | custom-call | flops 1048576 | bytes 262144 | tf_op jit(solution)/shard_map/clip/pallas_call | solution.py:407
  (16 shorter events, 0.2 us)
Async XLA Ops:
  0.6 7.6 %collective-permute-start.1 = (bf16[128,128]{1,0:T(8,128)(2,1)}, bf16[128,128]{1,0:T(8,128)(2,1)S(1)}, u32[]{:S(2)}, u32[]{:S(2)}) collective-permute-start(bf16[128,128]{1,0:T(8,128)(2,1)} %bitcast.15), channel_id=1, source_target_pairs={{0,8},{1,13},{2,10},{3,15},{4,12},{5,9},{6,14},{7,11},{8,0},{9,5},... | collective-permute-start | bytes 98312 | tf_op jit(solution)/shard_map/ppermute | solution.py:193
  4.7 4.1 %collective-permute-start = (bf16[128,128]{1,0:T(8,128)(2,1)}, bf16[128,128]{1,0:T(8,128)(2,1)S(1)}, u32[]{:S(2)}, u32[]{:S(2)}) collective-permute-start(bf16[128,128]{1,0:T(8,128)(2,1)} %bitcast.16), channel_id=1, source_target_pairs={{0,4},{1,5},{2,6},{3,7},{4,0},{5,1},{6,2},{7,3},{8,12},{9,13},{10,... | collective-permute-start | bytes 98312 | tf_op jit(solution)/shard_map/ppermute | solution.py:193
  8.2 1.3 %collective-permute-start.2 = (bf16[128,128]{1,0:T(8,128)(2,1)S(1)}, bf16[128,128]{1,0:T(8,128)(2,1)S(1)}, u32[]{:S(2)}, u32[]{:S(2)}) collective-permute-start(bf16[128,128]{1,0:T(8,128)(2,1)S(1)} %collective-permute-done.1.direct_ref), channel_id=1, source_target_pairs={{0,1},{1,0},{2,3},{3,2},{4,5},{5,4},{6,7},{7,6},{8,9},{9,8},{10,11... | collective-permute-start | bytes 98312 | tf_op jit(solution)/shard_map/ppermute | solution.py:193
  11.0 1.7 %collective-permute-start.4 = (bf16[256,128]{1,0:T(8,128)(2,1)S(1)}, bf16[256,128]{1,0:T(8,128)(2,1)S(1)}, u32[]{:S(2)}, u32[]{:S(2)}) collective-permute-start(bf16[256,128]{1,0:T(8,128)(2,1)S(1)} %get-tuple-element.52), channel_id=1, source_target_pairs={{0,1},{1,0},{2,3},{3,2},{4,5},{5,4},{6,7},{7,6},{8,9},{9,8},{10,11... | collective-permute-start | bytes 196616 | tf_op jit(solution)/shard_map/ppermute | solution.py:193
  11.2 4.4 %collective-permute-start.3 = (bf16[320,128]{1,0:T(8,128)(2,1)S(1)}, bf16[320,128]{1,0:T(8,128)(2,1)S(1)}, u32[]{:S(2)}, u32[]{:S(2)}) collective-permute-start(bf16[320,128]{1,0:T(8,128)(2,1)S(1)} %get-tuple-element.47), channel_id=1, source_target_pairs={{0,2},{1,5},{2,0},{3,7},{4,6},{5,1},{6,4},{7,3},{8,10},{9,13},{10,... | collective-permute-start | bytes 245768 | tf_op jit(solution)/shard_map/ppermute | solution.py:193
  12.7 0.6 %copy-start = (f32[256,128]{1,0:T(8,128)}, f32[256,128]{1,0:T(8,128)S(1)}, u32[]{:S(2)}) copy-start(f32[256,128]{1,0:T(8,128)S(1)} %convert_add_fusion) | copy-start | bytes 393220
  13.4 4.8 %collective-permute-start.6 = (bf16[128,128]{1,0:T(8,128)(2,1)S(1)}, bf16[128,128]{1,0:T(8,128)(2,1)S(1)}, u32[]{:S(2)}, u32[]{:S(2)}) collective-permute-start(bf16[128,128]{1,0:T(8,128)(2,1)S(1)} %slice.24), channel_id=1, source_target_pairs={{0,8},{1,9},{2,10},{3,11},{4,12},{5,13},{6,14},{7,15},{8,0},{9,1},... | collective-permute-start | bytes 98312 | tf_op jit(solution)/shard_map/ppermute | solution.py:193
  15.2 3.0 %slice-start = ((f32[256,128]{1,0:T(8,128)}), f32[128,128]{1,0:T(8,128)S(1)}, s32[]{:S(2)}) async-start(f32[256,128]{1,0:T(8,128)} %copy-done), calls=%async_computation | async-start | bytes 131072 | tf_op jit(solution)/shard_map/slice | solution.py:474
  15.7 6.3 %collective-permute-start.5 = (bf16[320,128]{1,0:T(8,128)(2,1)S(1)}, bf16[320,128]{1,0:T(8,128)(2,1)S(1)}, u32[]{:S(2)}, u32[]{:S(2)}) collective-permute-start(bf16[320,128]{1,0:T(8,128)(2,1)S(1)} %add_convert_fusion.1), channel_id=1, source_target_pairs={{0,8},{1,3},{2,10},{3,1},{4,12},{5,7},{6,14},{7,5},{8,0},{9,11},{1... | collective-permute-start | bytes 245768 | tf_op jit(solution)/shard_map/ppermute | solution.py:193
  18.2 0.6 %copy-start.1 = (f32[128,128]{1,0:T(8,128)}, f32[128,128]{1,0:T(8,128)S(1)}, u32[]{:S(2)}) copy-start(f32[128,128]{1,0:T(8,128)S(1)} %convert_add_fusion.1) | copy-start | bytes 196612
  18.9 4.3 %collective-permute-start.8 = (bf16[64,128]{1,0:T(8,128)(2,1)S(1)}, bf16[64,128]{1,0:T(8,128)(2,1)S(1)}, u32[]{:S(2)}, u32[]{:S(2)}) collective-permute-start(bf16[64,128]{1,0:T(8,128)(2,1)S(1)} %slice.25), channel_id=1, source_target_pairs={{0,4},{1,5},{2,6},{3,7},{4,0},{5,1},{6,2},{7,3},{8,12},{9,13},{10,... | collective-permute-start | bytes 49160 | tf_op jit(solution)/shard_map/ppermute | solution.py:193
  19.9 3.2 %slice-start.1 = ((f32[128,128]{1,0:T(8,128)}), f32[64,128]{1,0:T(8,128)S(1)}, s32[]{:S(2)}) async-start(f32[128,128]{1,0:T(8,128)} %copy-done.1), calls=%async_computation.1 | async-start | bytes 65536 | tf_op jit(solution)/shard_map/slice | solution.py:478
  22.0 4.5 %collective-permute-start.7 = (bf16[320,128]{1,0:T(8,128)(2,1)S(1)}, bf16[320,128]{1,0:T(8,128)(2,1)S(1)}, u32[]{:S(2)}, u32[]{:S(2)}) collective-permute-start(bf16[320,128]{1,0:T(8,128)(2,1)S(1)} %add_convert_fusion.own_ref), channel_id=1, source_target_pairs={{0,4},{1,9},{2,6},{3,11},{4,0},{5,13},{6,2},{7,15},{8,12},{9,1},{1... | collective-permute-start | bytes 245768 | tf_op jit(solution)/shard_map/ppermute | solution.py:193
  26.6 1.2 %collective-permute-start.9 = (f32[8,128]{1,0:T(8,128)S(1)}, f32[8,128]{1,0:T(8,128)S(1)}, u32[]{:S(2)}, u32[]{:S(2)}) collective-permute-start(f32[8,128]{1,0:T(8,128)S(1)} %get-tuple-element.60.own_ref), channel_id=1, source_target_pairs={{0,1},{1,0},{2,3},{3,2},{4,5},{5,4},{6,7},{7,6},{8,9},{9,8},{10,11... | collective-permute-start | bytes 12296 | tf_op jit(solution)/shard_map/ppermute | solution.py:193

commit v4 on v3

--- a/solution.py
+++ b/solution.py
@@ -375,13 +375,24 @@
     parts_ref[...] = dot_nn(key_value_grad_ref[...], w_kv_ref[...])
     own = pl.ds(pl.multiple_of(me * TILE, TILE), TILE)
     parts_ref[own, :] = parts_ref[own, :] + dot_nn(local_ref[...], w_qg_ref[...])
-    for bits in range(4):
+    for place, bits in enumerate((0, 2, 1, 3)):
         start = lax.bitwise_xor(me, bits) * TILE
         mine = pl.multiple_of(start + head * half, half)
         other = pl.multiple_of(start + (1 - head) * half, half)
-        rows = slice(bits * half, (bits + 1) * half)
+        rows = slice(place * half, (place + 1) * half)
         keep_ref[rows, :] = parts_ref[pl.ds(mine, half), :]
         send_ref[rows, :] = parts_ref[pl.ds(other, half), :].astype(BF16)
+
+
+def fold_kernel(own_ref, other_ref, keep_ref, send_ref):
+    half = keep_ref.shape[0]
+    keep_ref[...] = own_ref[:half, :] + other_ref[:half, :].astype(F32)
+    send_ref[...] = (own_ref[half:, :] + other_ref[half:, :].astype(F32)).astype(BF16)
+
+
+def add_kernel(own_ref, other_ref, send_ref):
+    half = send_ref.shape[0]
+    send_ref[...] = (own_ref[half:, :] + other_ref[half:, :].astype(F32)).astype(BF16)
 
 
 def squares_kernel(own_ref, other_ref, total_ref, squares_ref):
@@ -390,12 +401,16 @@
     squares_ref[...] = jnp.sum((total * total).reshape(total.shape[0] // 8, 8, C), axis=0)
 
 
-def clip_kernel(total_ref, own_ref, other_ref, query_ref, gate_ref, key_ref, value_ref, out_ref):
+def clip_kernel(
+    total_ref, own_ref, other_ref, pair_own_ref, pair_other_ref,
+    query_ref, gate_ref, key_ref, value_ref, out_ref, pair_ref,
+):
     squares = own_ref[...] + other_ref[...]
     squares = jnp.sum(jnp.sum(squares, axis=0, keepdims=True), axis=1, keepdims=True)
     clip = jnp.minimum(1.0, CLIP_NORM / jnp.sqrt(squares + 1e-06))
     for part, ref in enumerate((query_ref, gate_ref, key_ref, value_ref, out_ref)):
         ref[...] = total_ref[part * 2 * HD : (part + 1) * 2 * HD, :] * clip
+    pair_ref[...] = (pair_own_ref[...] + pair_other_ref[...].astype(F32)).astype(BF16)
 
 
 VMEM = pl.BlockSpec(memory_space=pltpu.VMEM)
@@ -470,24 +485,27 @@
     )
     half = TILE // 2
     raw = summed(raw, exchange(raw, staggered(other_row, next_col)))
-    parts = keep + exchange(send, other_head).astype(F32)
-    kept, sent = parts[:TILE], parts[TILE:].astype(BF16)
-    raw, kept = lax.optimization_barrier((raw, kept))
-    parts = kept + exchange(sent, far_col).astype(F32)
+    given = exchange(send, other_head)
+    keep, send = on_core(
+        fold_kernel, "fold_heads", [], (keep, given), (((TILE, C), F32), ((TILE, C), BF16)),
+    )
+    raw, keep = lax.optimization_barrier((raw, keep))
+    given = exchange(send, next_col)
+    send = (keep[half:] + given[half:].astype(F32)).astype(BF16)
+    keep, early = keep[:half], given[:half]
     raw = summed(raw, exchange(raw, staggered(far_col, other_row)))
-    kept, sent = parts[:half], parts[half:].astype(BF16)
-    raw, kept = lax.optimization_barrier((raw, kept))
-    pair_grad = (kept + exchange(sent, next_col).astype(F32)).astype(BF16)
+    raw, keep = lax.optimization_barrier((raw, keep))
+    given = exchange(send, far_col)
+    keep = keep + early.astype(F32)
     last = exchange(raw, staggered(next_col, far_col))
-    last, pair_grad = lax.optimization_barrier((last, pair_grad))
     total, squares = on_core(
         squares_kernel, "squares", [], (raw, last), (((5 * width, C), F32), ((8, C), F32)),
     )
     grads = on_core(
-        clip_kernel, "clip", [], (total, squares, exchange(squares, other_head)),
-        (((width, C), F32),) * 5,
-    )
-    query_grad, gate_grad, key_grad, value_grad, out_weight_grad = grads
+        clip_kernel, "clip", [], (total, squares, exchange(squares, other_head), keep, given),
+        (((width, C), F32),) * 5 + (((half, C), BF16),),
+    )
+    query_grad, gate_grad, key_grad, value_grad, out_weight_grad, pair_grad = grads
     return (
         pair_grad.reshape(1, half, C),
         query_grad.T,

time: 28.7 us -> 28.3 us (0.986)
  starting transfers between devices: 12.9 us -> 14.3 us
  local copies, waits for them, and re-layouts: 1.24 us -> 0 us
  other arithmetic: 0.69 us -> 0.07 us
    ppermute x10, starting transfers between devices: 12.9 us -> 14.3 us  [exchange(): return lax.ppermute(value, ('col', 'row', 'head'), pairs)]
    unnamed x4 -> x0, local copies, waits for them, and re-layouts: 1.22 us -> none
    convert_element_type x1, other arithmetic: 0.61 us -> 0.01 us  [four_cols(): send = (keep[half:] + given[half:].astype(F32)).astype(BF16)]
    pallas_call x5 -> x6, Pallas kernels: 4.19 us -> 4.2 us  [on_core(): pl.pallas_call(kernel, out_shape=tuple((jax.ShapeDtypeStruct(shape, dtype...]
  transfers between devices with their start and end apart: 10 -> 10, of which waited for: 8 -> 9; matrix products, arithmetic and copies ran while one was open for 2% -> 0% of each run, Pallas kernels for 7% -> 8%
where the time goes in v4:
time: 28.3 us; the launch traced here: 28.2 us
  starting transfers between devices  14.3 us (51%)
  waiting for transfers between devices  8.87 us (31%)
  Pallas kernels  4.2 us (15%)
  between operations  0.72 us (3%)
    ppermute x10, starting transfers between devices, exchange(): return lax.ppermute(value, ('col', 'row', 'head'), pairs)  14.3 us
    ppermute x10, waiting for transfers between devices, exchange(): return lax.ppermute(value, ('col', 'row', 'head'), pairs)  8.87 us
    pallas_call x6, Pallas kernels, on_core(): pl.pallas_call(kernel, out_shape=tuple((jax.ShapeDtypeStruct(shape, dtype...  4.2 us
  transfers between devices with their start and end apart: 10, of which 9 were waited for; matrix products, arithmetic and copies ran while one was open for 0% of the time, Pallas kernels for 8%

profile of v4, /device:TPU:0, one launch (start us, length us, event | category | flops | bytes accessed | tf_op | source)
XLA Modules:
  0.0 28.2 jit_solution(878507836544408554)
XLA Ops:
  0.6 4.1 %collective-permute-start.1 = (bf16[128,128]{1,0:T(8,128)(2,1)}, bf16[128,128]{1,0:T(8,128)(2,1)S(1)}, u32[]{:S(2)}, u32[]{:S(2)}) collective-permute-start(bf16[128,128]{1,0:T(8,128)(2,1)} %bitcast.15), channel_id=1, source_target_pairs={{0,8},{1,13},{2,10},{3,15},{4,12},{5,9},{6,14},{7,11},{8,0},{9,5},... | collective-permute-start | bytes 98312 | tf_op jit(solution)/shard_map/ppermute | solution.py:193
  4.7 1.6 %collective-permute-start = (bf16[128,128]{1,0:T(8,128)(2,1)}, bf16[128,128]{1,0:T(8,128)(2,1)S(1)}, u32[]{:S(2)}, u32[]{:S(2)}) collective-permute-start(bf16[128,128]{1,0:T(8,128)(2,1)} %bitcast.16), channel_id=1, source_target_pairs={{0,4},{1,5},{2,6},{3,7},{4,0},{5,1},{6,2},{7,3},{8,12},{9,13},{10,... | collective-permute-start | bytes 98312 | tf_op jit(solution)/shard_map/ppermute | solution.py:193
  6.3 1.9 %local.1 = (bf16[128,128]{1,0:T(8,128)(2,1)S(1)}, bf16[128,128]{1,0:T(8,128)(2,1)S(1)}, bf16[128,128]{1,0:T(8,128)(2,1)S(1)}, bf16[128,128]{1,0:T(8,128)(2,1)S(1...) custom-call(s32[1]{0:T(128)} %bitcast.col_ref, ...), custom_call_target="tpu_custom_call" | custom-call | flops 1048576 | bytes 262144 | tf_op jit(solution)/shard_map/local/pallas_call | solution.py:422
  8.2 0.0 collective-permute-done.1.direct_ref
  8.2 0.1 collective-permute-start.2
  8.3 0.6 %collective-permute-done.next_ref = bf16[128,128]{1,0:T(8,128)(2,1)S(1)} collective-permute-done((bf16[128,128]{1,0:T(8,128)(2,1)}, bf16[128,128]{1,0:T(8,128)(2,1)S(1)}, u32[]{:S(2)}, u32[]{:S(2)}) %collective-permute-start) | collective-permute-done | bytes 32800 | tf_op jit(solution)/shard_map/ppermute | solution.py:193
  8.9 0.6 %collective-permute-done.2.crossed_ref = bf16[128,128]{1,0:T(8,128)(2,1)S(1)} collective-permute-done((bf16[128,128]{1,0:T(8,128)(2,1)S(1)}, bf16[128,128]{1,0:T(8,128)(2,1)S(1)}, u32[]{:S(2)}, u32[]{:S(2)}) %collective-permute-start.2) | collective-permute-done | bytes 32800 | tf_op jit(solution)/shard_map/ppermute | solution.py:193
  9.5 1.3 %attention.1 = (bf16[320,128]{1,0:T(8,128)(2,1)S(1)}, bf16[128,128]{1,0:T(8,128)(2,1)S(1)}, bf16[512,128]{1,0:T(8,128)(2,1)S(1)}) custom-call(s32[1]{0:T(128)} %bitcast.col_ref, s32[1]{0:T(128)} %bitcast.1.head_ref, bf16[128,128]{1,0:T(8,128)(2,1)S(1)} %get-tuple-element.37.x_ref, bf16[128,128]{1,0:T(8,128)(2,1)S(1)} %collective-permute-done.next_ref, ...), custom_call_target="tpu_custom_call" | custom-call | flops 1048576 | bytes 262144 | tf_op jit(solution)/shard_map/attention/pallas_call | solution.py:422
  10.8 1.6 %collective-permute-start.3 = (bf16[320,128]{1,0:T(8,128)(2,1)S(1)}, bf16[320,128]{1,0:T(8,128)(2,1)S(1)}, u32[]{:S(2)}, u32[]{:S(2)}) collective-permute-start(bf16[320,128]{1,0:T(8,128)(2,1)S(1)} %get-tuple-element.48), channel_id=1, source_target_pairs={{0,2},{1,5},{2,0},{3,7},{4,6},{5,1},{6,4},{7,3},{8,10},{9,13},{10,... | collective-permute-start | bytes 245768 | tf_op jit(solution)/shard_map/ppermute | solution.py:193
  12.3 0.2 parts.1
  12.6 0.1 collective-permute-start.4
  12.6 1.2 %collective-permute-done.4.other_ref = bf16[256,128]{1,0:T(8,128)(2,1)S(1)} collective-permute-done((bf16[256,128]{1,0:T(8,128)(2,1)S(1)}, bf16[256,128]{1,0:T(8,128)(2,1)S(1)}, u32[]{:S(2)}, u32[]{:S(2)}) %collective-permute-start.4) | collective-permute-done | bytes 65568 | tf_op jit(solution)/shard_map/ppermute | solution.py:193
  13.9 1.0 %collective-permute-start.8 = (bf16[128,128]{1,0:T(8,128)(2,1)S(1)}, bf16[128,128]{1,0:T(8,128)(2,1)S(1)}, u32[]{:S(2)}, u32[]{:S(2)}) collective-permute-start(bf16[128,128]{1,0:T(8,128)(2,1)S(1)} %get-tuple-element.61), channel_id=1, source_target_pairs={{0,4},{1,5},{2,6},{3,7},{4,0},{5,1},{6,2},{7,3},{8,12},{9,13},{10,... | collective-permute-start | bytes 98312 | tf_op jit(solution)/shard_map/ppermute | solution.py:193
  14.9 0.4 %collective-permute-done.3 = bf16[320,128]{1,0:T(8,128)(2,1)S(1)} collective-permute-done((bf16[320,128]{1,0:T(8,128)(2,1)S(1)}, bf16[320,128]{1,0:T(8,128)(2,1)S(1)}, u32[]{:S(2)}, u32[]{:S(2)}) %collective-permute-start.3) | collective-permute-done | bytes 81952 | tf_op jit(solution)/shard_map/ppermute | solution.py:193
  15.3 2.3 %collective-permute-start.5 = (bf16[320,128]{1,0:T(8,128)(2,1)S(1)}, bf16[320,128]{1,0:T(8,128)(2,1)S(1)}, u32[]{:S(2)}, u32[]{:S(2)}) collective-permute-start(bf16[320,128]{1,0:T(8,128)(2,1)S(1)} %add_convert_fusion.1), channel_id=1, source_target_pairs={{0,8},{1,3},{2,10},{3,1},{4,12},{5,7},{6,14},{7,5},{8,0},{9,11},{1... | collective-permute-start | bytes 245768 | tf_op jit(solution)/shard_map/ppermute | solution.py:193
  17.6 0.3 %collective-permute-done.8 = bf16[128,128]{1,0:T(8,128)(2,1)S(1)} collective-permute-done((bf16[128,128]{1,0:T(8,128)(2,1)S(1)}, bf16[128,128]{1,0:T(8,128)(2,1)S(1)}, u32[]{:S(2)}, u32[]{:S(2)}) %collective-permute-start.8) | collective-permute-done | bytes 32800 | tf_op jit(solution)/shard_map/ppermute | solution.py:193
  17.9 3.7 %collective-permute-done.5 = bf16[320,128]{1,0:T(8,128)(2,1)S(1)} collective-permute-done((bf16[320,128]{1,0:T(8,128)(2,1)S(1)}, bf16[320,128]{1,0:T(8,128)(2,1)S(1)}, u32[]{:S(2)}, u32[]{:S(2)}) %collective-permute-start.5) | collective-permute-done | bytes 81952 | tf_op jit(solution)/shard_map/ppermute | solution.py:193
  21.6 0.3 collective-permute-start.6
  21.9 3.3 %collective-permute-start.9 = (bf16[64,128]{1,0:T(8,128)(2,1)S(1)}, bf16[64,128]{1,0:T(8,128)(2,1)S(1)}, u32[]{:S(2)}, u32[]{:S(2)}) collective-permute-start(bf16[64,128]{1,0:T(8,128)(2,1)S(1)} %get-tuple-element.68), channel_id=1, source_target_pairs={{0,8},{1,9},{2,10},{3,11},{4,12},{5,13},{6,14},{7,15},{8,0},{9,1},... | collective-permute-start | bytes 49160 | tf_op jit(solution)/shard_map/ppermute | solution.py:193
  25.2 0.9 %collective-permute-done.6.other_ref = bf16[320,128]{1,0:T(8,128)(2,1)S(1)} collective-permute-done((bf16[320,128]{1,0:T(8,128)(2,1)S(1)}, bf16[320,128]{1,0:T(8,128)(2,1)S(1)}, u32[]{:S(2)}, u32[]{:S(2)}) %collective-permute-start.6) | collective-permute-done | bytes 81952 | tf_op jit(solution)/shard_map/ppermute | solution.py:193
  26.2 0.1 collective-permute-start.7
  26.3 0.7 %collective-permute-done.9.pair_other_ref = bf16[64,128]{1,0:T(8,128)(2,1)S(1)} collective-permute-done((bf16[64,128]{1,0:T(8,128)(2,1)S(1)}, bf16[64,128]{1,0:T(8,128)(2,1)S(1)}, u32[]{:S(2)}, u32[]{:S(2)}) %collective-permute-start.9) | collective-permute-done | bytes 16416 | tf_op jit(solution)/shard_map/ppermute | solution.py:193
  26.9 0.5 %collective-permute-done.7.other_ref = f32[8,128]{1,0:T(8,128)S(1)} collective-permute-done((f32[8,128]{1,0:T(8,128)S(1)}, f32[8,128]{1,0:T(8,128)S(1)}, u32[]{:S(2)}, u32[]{:S(2)}) %collective-permute-start.7) | collective-permute-done | bytes 4128 | tf_op jit(solution)/shard_map/ppermute | solution.py:193
  27.4 0.8 %clip.1 = (f32[64,128]{1,0:T(8,128)}, f32[64,128]{1,0:T(8,128)}, f32[64,128]{1,0:T(8,128)}, f32[64,128]{1,0:T(8,128)}, f32[64,128]{1,0:T(8,128)}, /*index=5*/bf16[64,128]{1,0:T(8,128)(2,1)}) custom-call(f32[320,128]{1,0:T(8,128)S(1)} %get-tuple-element.58.total_ref, f32[8,128]{1,0:T(8,128)S(1)} %get-tuple-element.59.own_ref, ...), custom_call_target="tpu_custom_call" | custom-call | flops 1048576 | bytes 262144 | tf_op jit(solution)/shard_map/clip/pallas_call | solution.py:422
  (6 shorter events, 0.1 us)
Async XLA Ops:
  0.6 7.6 %collective-permute-start.1 = (bf16[128,128]{1,0:T(8,128)(2,1)}, bf16[128,128]{1,0:T(8,128)(2,1)S(1)}, u32[]{:S(2)}, u32[]{:S(2)}) collective-permute-start(bf16[128,128]{1,0:T(8,128)(2,1)} %bitcast.15), channel_id=1, source_target_pairs={{0,8},{1,13},{2,10},{3,15},{4,12},{5,9},{6,14},{7,11},{8,0},{9,5},... | collective-permute-start | bytes 98312 | tf_op jit(solution)/shard_map/ppermute | solution.py:193
  4.7 4.1 %collective-permute-start = (bf16[128,128]{1,0:T(8,128)(2,1)}, bf16[128,128]{1,0:T(8,128)(2,1)S(1)}, u32[]{:S(2)}, u32[]{:S(2)}) collective-permute-start(bf16[128,128]{1,0:T(8,128)(2,1)} %bitcast.16), channel_id=1, source_target_pairs={{0,4},{1,5},{2,6},{3,7},{4,0},{5,1},{6,2},{7,3},{8,12},{9,13},{10,... | collective-permute-start | bytes 98312 | tf_op jit(solution)/shard_map/ppermute | solution.py:193
  8.2 1.3 %collective-permute-start.2 = (bf16[128,128]{1,0:T(8,128)(2,1)S(1)}, bf16[128,128]{1,0:T(8,128)(2,1)S(1)}, u32[]{:S(2)}, u32[]{:S(2)}) collective-permute-start(bf16[128,128]{1,0:T(8,128)(2,1)S(1)} %collective-permute-done.1.direct_ref), channel_id=1, source_target_pairs={{0,1},{1,0},{2,3},{3,2},{4,5},{5,4},{6,7},{7,6},{8,9},{9,8},{10,11... | collective-permute-start | bytes 98312 | tf_op jit(solution)/shard_map/ppermute | solution.py:193
  10.8 4.5 %collective-permute-start.3 = (bf16[320,128]{1,0:T(8,128)(2,1)S(1)}, bf16[320,128]{1,0:T(8,128)(2,1)S(1)}, u32[]{:S(2)}, u32[]{:S(2)}) collective-permute-start(bf16[320,128]{1,0:T(8,128)(2,1)S(1)} %get-tuple-element.48), channel_id=1, source_target_pairs={{0,2},{1,5},{2,0},{3,7},{4,6},{5,1},{6,4},{7,3},{8,10},{9,13},{10,... | collective-permute-start | bytes 245768 | tf_op jit(solution)/shard_map/ppermute | solution.py:193
  12.6 1.3 %collective-permute-start.4 = (bf16[256,128]{1,0:T(8,128)(2,1)S(1)}, bf16[256,128]{1,0:T(8,128)(2,1)S(1)}, u32[]{:S(2)}, u32[]{:S(2)}) collective-permute-start(bf16[256,128]{1,0:T(8,128)(2,1)S(1)} %get-tuple-element.53), channel_id=1, source_target_pairs={{0,1},{1,0},{2,3},{3,2},{4,5},{5,4},{6,7},{7,6},{8,9},{9,8},{10,11... | collective-permute-start | bytes 196616 | tf_op jit(solution)/shard_map/ppermute | solution.py:193
  13.9 4.0 %collective-permute-start.8 = (bf16[128,128]{1,0:T(8,128)(2,1)S(1)}, bf16[128,128]{1,0:T(8,128)(2,1)S(1)}, u32[]{:S(2)}, u32[]{:S(2)}) collective-permute-start(bf16[128,128]{1,0:T(8,128)(2,1)S(1)} %get-tuple-element.61), channel_id=1, source_target_pairs={{0,4},{1,5},{2,6},{3,7},{4,0},{5,1},{6,2},{7,3},{8,12},{9,13},{10,... | collective-permute-start | bytes 98312 | tf_op jit(solution)/shard_map/ppermute | solution.py:193
  15.3 6.3 %collective-permute-start.5 = (bf16[320,128]{1,0:T(8,128)(2,1)S(1)}, bf16[320,128]{1,0:T(8,128)(2,1)S(1)}, u32[]{:S(2)}, u32[]{:S(2)}) collective-permute-start(bf16[320,128]{1,0:T(8,128)(2,1)S(1)} %add_convert_fusion.1), channel_id=1, source_target_pairs={{0,8},{1,3},{2,10},{3,1},{4,12},{5,7},{6,14},{7,5},{8,0},{9,11},{1... | collective-permute-start | bytes 245768 | tf_op jit(solution)/shard_map/ppermute | solution.py:193
  21.6 4.5 %collective-permute-start.6 = (bf16[320,128]{1,0:T(8,128)(2,1)S(1)}, bf16[320,128]{1,0:T(8,128)(2,1)S(1)}, u32[]{:S(2)}, u32[]{:S(2)}) collective-permute-start(bf16[320,128]{1,0:T(8,128)(2,1)S(1)} %add_convert_fusion.own_ref), channel_id=1, source_target_pairs={{0,4},{1,9},{2,6},{3,11},{4,0},{5,13},{6,2},{7,15},{8,12},{9,1},{1... | collective-permute-start | bytes 245768 | tf_op jit(solution)/shard_map/ppermute | solution.py:193
  21.9 5.0 %collective-permute-start.9 = (bf16[64,128]{1,0:T(8,128)(2,1)S(1)}, bf16[64,128]{1,0:T(8,128)(2,1)S(1)}, u32[]{:S(2)}, u32[]{:S(2)}) collective-permute-start(bf16[64,128]{1,0:T(8,128)(2,1)S(1)} %get-tuple-element.68), channel_id=1, source_target_pairs={{0,8},{1,9},{2,10},{3,11},{4,12},{5,13},{6,14},{7,15},{8,0},{9,1},... | collective-permute-start | bytes 49160 | tf_op jit(solution)/shard_map/ppermute | solution.py:193
  26.2 1.2 %collective-permute-start.7 = (f32[8,128]{1,0:T(8,128)S(1)}, f32[8,128]{1,0:T(8,128)S(1)}, u32[]{:S(2)}, u32[]{:S(2)}) collective-permute-start(f32[8,128]{1,0:T(8,128)S(1)} %get-tuple-element.59.own_ref), channel_id=1, source_target_pairs={{0,1},{1,0},{2,3},{3,2},{4,5},{5,4},{6,7},{7,6},{8,9},{9,8},{10,11... | collective-permute-start | bytes 12296 | tf_op jit(solution)/shard_map/ppermute | solution.py:193

commit v5 on v4

--- a/solution.py
+++ b/solution.py
@@ -390,11 +390,6 @@
     send_ref[...] = (own_ref[half:, :] + other_ref[half:, :].astype(F32)).astype(BF16)
 
 
-def add_kernel(own_ref, other_ref, send_ref):
-    half = send_ref.shape[0]
-    send_ref[...] = (own_ref[half:, :] + other_ref[half:, :].astype(F32)).astype(BF16)
-
-
 def squares_kernel(own_ref, other_ref, total_ref, squares_ref):
     total = own_ref[...].astype(F32) + other_ref[...].astype(F32)
     total_ref[...] = total
@@ -484,7 +479,7 @@
         (((wide, C), F32), ((wide, C), BF16)), [pltpu.VMEM((keys, C), F32)],
     )
     half = TILE // 2
-    raw = summed(raw, exchange(raw, staggered(other_row, next_col)))
+    raw = summed(raw, exchange(raw, staggered(next_col, far_col)))
     given = exchange(send, other_head)
     keep, send = on_core(
         fold_kernel, "fold_heads", [], (keep, given), (((TILE, C), F32), ((TILE, C), BF16)),
@@ -497,7 +492,7 @@
     raw, keep = lax.optimization_barrier((raw, keep))
     given = exchange(send, far_col)
     keep = keep + early.astype(F32)
-    last = exchange(raw, staggered(next_col, far_col))
+    last = exchange(raw, staggered(other_row, next_col))
     total, squares = on_core(
         squares_kernel, "squares", [], (raw, last), (((5 * width, C), F32), ((8, C), F32)),
     )

time: 28.3 us -> 28.3 us (level)
  starting transfers between devices: 14.3 us -> 13.9 us
  waiting for transfers between devices: 8.87 us -> 9.25 us
    ppermute x10, starting transfers between devices: 14.3 us -> 13.9 us  [exchange(): return lax.ppermute(value, ('col', 'row', 'head'), pairs)]
    ppermute x10, waiting for transfers between devices: 8.87 us -> 9.25 us  [exchange(): return lax.ppermute(value, ('col', 'row', 'head'), pairs)]
  transfers between devices with their start and end apart: 10 -> 10, of which waited for: 9 -> 8; matrix products, arithmetic and copies ran while one was open for 0% -> 0% of each run, Pallas kernels for 8% -> 8%
where the time goes in v5:
time: 28.3 us; the launch traced here: 28.1 us
  starting transfers between devices  13.9 us (49%)
  waiting for transfers between devices  9.25 us (33%)
  Pallas kernels  4.2 us (15%)
  between operations  0.71 us (3%)
    ppermute x10, starting transfers between devices, exchange(): return lax.ppermute(value, ('col', 'row', 'head'), pairs)  13.9 us
    ppermute x10, waiting for transfers between devices, exchange(): return lax.ppermute(value, ('col', 'row', 'head'), pairs)  9.25 us
    pallas_call x6, Pallas kernels, on_core(): pl.pallas_call(kernel, out_shape=tuple((jax.ShapeDtypeStruct(shape, dtype...  4.2 us
  transfers between devices with their start and end apart: 10, of which 8 were waited for; matrix products, arithmetic and copies ran while one was open for 0% of the time, Pallas kernels for 8%

profile of v5, /device:TPU:0, one launch (start us, length us, event | category | flops | bytes accessed | tf_op | source)
XLA Modules:
  0.0 28.1 jit_solution(2712758055672893991)
XLA Ops:
  0.6 4.1 %collective-permute-start.1 = (bf16[128,128]{1,0:T(8,128)(2,1)}, bf16[128,128]{1,0:T(8,128)(2,1)S(1)}, u32[]{:S(2)}, u32[]{:S(2)}) collective-permute-start(bf16[128,128]{1,0:T(8,128)(2,1)} %bitcast.15), channel_id=1, source_target_pairs={{0,8},{1,13},{2,10},{3,15},{4,12},{5,9},{6,14},{7,11},{8,0},{9,5},... | collective-permute-start | bytes 98312 | tf_op jit(solution)/shard_map/ppermute | solution.py:193
  4.7 1.6 %collective-permute-start = (bf16[128,128]{1,0:T(8,128)(2,1)}, bf16[128,128]{1,0:T(8,128)(2,1)S(1)}, u32[]{:S(2)}, u32[]{:S(2)}) collective-permute-start(bf16[128,128]{1,0:T(8,128)(2,1)} %bitcast.16), channel_id=1, source_target_pairs={{0,4},{1,5},{2,6},{3,7},{4,0},{5,1},{6,2},{7,3},{8,12},{9,13},{10,... | collective-permute-start | bytes 98312 | tf_op jit(solution)/shard_map/ppermute | solution.py:193
  6.3 1.9 %local.1 = (bf16[128,128]{1,0:T(8,128)(2,1)S(1)}, bf16[128,128]{1,0:T(8,128)(2,1)S(1)}, bf16[128,128]{1,0:T(8,128)(2,1)S(1)}, bf16[128,128]{1,0:T(8,128)(2,1)S(1...) custom-call(s32[1]{0:T(128)} %bitcast.col_ref, ...), custom_call_target="tpu_custom_call" | custom-call | flops 1048576 | bytes 262144 | tf_op jit(solution)/shard_map/local/pallas_call | solution.py:417
  8.2 0.0 collective-permute-done.1.direct_ref
  8.2 0.1 collective-permute-start.2
  8.3 0.6 %collective-permute-done.next_ref = bf16[128,128]{1,0:T(8,128)(2,1)S(1)} collective-permute-done((bf16[128,128]{1,0:T(8,128)(2,1)}, bf16[128,128]{1,0:T(8,128)(2,1)S(1)}, u32[]{:S(2)}, u32[]{:S(2)}) %collective-permute-start) | collective-permute-done | bytes 32800 | tf_op jit(solution)/shard_map/ppermute | solution.py:193
  8.9 0.6 %collective-permute-done.2.crossed_ref = bf16[128,128]{1,0:T(8,128)(2,1)S(1)} collective-permute-done((bf16[128,128]{1,0:T(8,128)(2,1)S(1)}, bf16[128,128]{1,0:T(8,128)(2,1)S(1)}, u32[]{:S(2)}, u32[]{:S(2)}) %collective-permute-start.2) | collective-permute-done | bytes 32800 | tf_op jit(solution)/shard_map/ppermute | solution.py:193
  9.5 1.3 %attention.1 = (bf16[320,128]{1,0:T(8,128)(2,1)S(1)}, bf16[128,128]{1,0:T(8,128)(2,1)S(1)}, bf16[512,128]{1,0:T(8,128)(2,1)S(1)}) custom-call(s32[1]{0:T(128)} %bitcast.col_ref, s32[1]{0:T(128)} %bitcast.1.head_ref, bf16[128,128]{1,0:T(8,128)(2,1)S(1)} %get-tuple-element.37.x_ref, bf16[128,128]{1,0:T(8,128)(2,1)S(1)} %collective-permute-done.next_ref, ...), custom_call_target="tpu_custom_call" | custom-call | flops 1048576 | bytes 262144 | tf_op jit(solution)/shard_map/attention/pallas_call | solution.py:417
  10.8 1.0 %collective-permute-start.3 = (bf16[320,128]{1,0:T(8,128)(2,1)S(1)}, bf16[320,128]{1,0:T(8,128)(2,1)S(1)}, u32[]{:S(2)}, u32[]{:S(2)}) collective-permute-start(bf16[320,128]{1,0:T(8,128)(2,1)S(1)} %get-tuple-element.48), channel_id=1, source_target_pairs={{0,4},{1,9},{2,6},{3,11},{4,0},{5,13},{6,2},{7,15},{8,12},{9,1},{1... | collective-permute-start | bytes 245768 | tf_op jit(solution)/shard_map/ppermute | solution.py:193
  11.8 0.2 parts.1
  12.0 0.8 %collective-permute-start.4 = (bf16[256,128]{1,0:T(8,128)(2,1)S(1)}, bf16[256,128]{1,0:T(8,128)(2,1)S(1)}, u32[]{:S(2)}, u32[]{:S(2)}) collective-permute-start(bf16[256,128]{1,0:T(8,128)(2,1)S(1)} %get-tuple-element.53), channel_id=1, source_target_pairs={{0,1},{1,0},{2,3},{3,2},{4,5},{5,4},{6,7},{7,6},{8,9},{9,8},{10,11... | collective-permute-start | bytes 196616 | tf_op jit(solution)/shard_map/ppermute | solution.py:193
  12.8 0.9 %collective-permute-done.4.other_ref = bf16[256,128]{1,0:T(8,128)(2,1)S(1)} collective-permute-done((bf16[256,128]{1,0:T(8,128)(2,1)S(1)}, bf16[256,128]{1,0:T(8,128)(2,1)S(1)}, u32[]{:S(2)}, u32[]{:S(2)}) %collective-permute-start.4) | collective-permute-done | bytes 65568 | tf_op jit(solution)/shard_map/ppermute | solution.py:193
  13.8 1.8 %collective-permute-start.8 = (bf16[128,128]{1,0:T(8,128)(2,1)S(1)}, bf16[128,128]{1,0:T(8,128)(2,1)S(1)}, u32[]{:S(2)}, u32[]{:S(2)}) collective-permute-start(bf16[128,128]{1,0:T(8,128)(2,1)S(1)} %get-tuple-element.61), channel_id=1, source_target_pairs={{0,4},{1,5},{2,6},{3,7},{4,0},{5,1},{6,2},{7,3},{8,12},{9,13},{10,... | collective-permute-start | bytes 98312 | tf_op jit(solution)/shard_map/ppermute | solution.py:193
  15.5 0.2 collective-permute-done.3
  15.7 1.5 %collective-permute-start.5 = (bf16[320,128]{1,0:T(8,128)(2,1)S(1)}, bf16[320,128]{1,0:T(8,128)(2,1)S(1)}, u32[]{:S(2)}, u32[]{:S(2)}) collective-permute-start(bf16[320,128]{1,0:T(8,128)(2,1)S(1)} %add_convert_fusion.1), channel_id=1, source_target_pairs={{0,8},{1,3},{2,10},{3,1},{4,12},{5,7},{6,14},{7,5},{8,0},{9,11},{1... | collective-permute-start | bytes 245768 | tf_op jit(solution)/shard_map/ppermute | solution.py:193
  17.2 0.5 %collective-permute-done.8 = bf16[128,128]{1,0:T(8,128)(2,1)S(1)} collective-permute-done((bf16[128,128]{1,0:T(8,128)(2,1)S(1)}, bf16[128,128]{1,0:T(8,128)(2,1)S(1)}, u32[]{:S(2)}, u32[]{:S(2)}) %collective-permute-start.8) | collective-permute-done | bytes 32800 | tf_op jit(solution)/shard_map/ppermute | solution.py:193
  17.8 3.4 %collective-permute-done.5 = bf16[320,128]{1,0:T(8,128)(2,1)S(1)} collective-permute-done((bf16[320,128]{1,0:T(8,128)(2,1)S(1)}, bf16[320,128]{1,0:T(8,128)(2,1)S(1)}, u32[]{:S(2)}, u32[]{:S(2)}) %collective-permute-start.5) | collective-permute-done | bytes 81952 | tf_op jit(solution)/shard_map/ppermute | solution.py:193
  21.2 1.6 %collective-permute-start.6 = (bf16[320,128]{1,0:T(8,128)(2,1)S(1)}, bf16[320,128]{1,0:T(8,128)(2,1)S(1)}, u32[]{:S(2)}, u32[]{:S(2)}) collective-permute-start(bf16[320,128]{1,0:T(8,128)(2,1)S(1)} %add_convert_fusion.own_ref), channel_id=1, source_target_pairs={{0,2},{1,5},{2,0},{3,7},{4,6},{5,1},{6,4},{7,3},{8,10},{9,13},{10,... | collective-permute-start | bytes 245768 | tf_op jit(solution)/shard_map/ppermute | solution.py:193
  22.7 1.4 %collective-permute-start.9 = (bf16[64,128]{1,0:T(8,128)(2,1)S(1)}, bf16[64,128]{1,0:T(8,128)(2,1)S(1)}, u32[]{:S(2)}, u32[]{:S(2)}) collective-permute-start(bf16[64,128]{1,0:T(8,128)(2,1)S(1)} %get-tuple-element.68), channel_id=1, source_target_pairs={{0,8},{1,9},{2,10},{3,11},{4,12},{5,13},{6,14},{7,15},{8,0},{9,1},... | collective-permute-start | bytes 49160 | tf_op jit(solution)/shard_map/ppermute | solution.py:193
  24.2 1.5 %collective-permute-done.6.other_ref = bf16[320,128]{1,0:T(8,128)(2,1)S(1)} collective-permute-done((bf16[320,128]{1,0:T(8,128)(2,1)S(1)}, bf16[320,128]{1,0:T(8,128)(2,1)S(1)}, u32[]{:S(2)}, u32[]{:S(2)}) %collective-permute-start.6) | collective-permute-done | bytes 81952 | tf_op jit(solution)/shard_map/ppermute | solution.py:193
  25.7 0.1 collective-permute-start.7
  25.8 1.6 %collective-permute-done.9.pair_other_ref = bf16[64,128]{1,0:T(8,128)(2,1)S(1)} collective-permute-done((bf16[64,128]{1,0:T(8,128)(2,1)S(1)}, bf16[64,128]{1,0:T(8,128)(2,1)S(1)}, u32[]{:S(2)}, u32[]{:S(2)}) %collective-permute-start.9) | collective-permute-done | bytes 16416 | tf_op jit(solution)/shard_map/ppermute | solution.py:193
  27.4 0.0 collective-permute-done.7.other_ref
  27.4 0.8 %clip.1 = (f32[64,128]{1,0:T(8,128)}, f32[64,128]{1,0:T(8,128)}, f32[64,128]{1,0:T(8,128)}, f32[64,128]{1,0:T(8,128)}, f32[64,128]{1,0:T(8,128)}, /*index=5*/bf16[64,128]{1,0:T(8,128)(2,1)}) custom-call(f32[320,128]{1,0:T(8,128)S(1)} %get-tuple-element.58.total_ref, f32[8,128]{1,0:T(8,128)S(1)} %get-tuple-element.59.own_ref, ...), custom_call_target="tpu_custom_call" | custom-call | flops 1048576 | bytes 262144 | tf_op jit(solution)/shard_map/clip/pallas_call | solution.py:417
  (6 shorter events, 0.1 us)
Async XLA Ops:
  0.6 7.6 %collective-permute-start.1 = (bf16[128,128]{1,0:T(8,128)(2,1)}, bf16[128,128]{1,0:T(8,128)(2,1)S(1)}, u32[]{:S(2)}, u32[]{:S(2)}) collective-permute-start(bf16[128,128]{1,0:T(8,128)(2,1)} %bitcast.15), channel_id=1, source_target_pairs={{0,8},{1,13},{2,10},{3,15},{4,12},{5,9},{6,14},{7,11},{8,0},{9,5},... | collective-permute-start | bytes 98312 | tf_op jit(solution)/shard_map/ppermute | solution.py:193
  4.7 4.1 %collective-permute-start = (bf16[128,128]{1,0:T(8,128)(2,1)}, bf16[128,128]{1,0:T(8,128)(2,1)S(1)}, u32[]{:S(2)}, u32[]{:S(2)}) collective-permute-start(bf16[128,128]{1,0:T(8,128)(2,1)} %bitcast.16), channel_id=1, source_target_pairs={{0,4},{1,5},{2,6},{3,7},{4,0},{5,1},{6,2},{7,3},{8,12},{9,13},{10,... | collective-permute-start | bytes 98312 | tf_op jit(solution)/shard_map/ppermute | solution.py:193
  8.2 1.3 %collective-permute-start.2 = (bf16[128,128]{1,0:T(8,128)(2,1)S(1)}, bf16[128,128]{1,0:T(8,128)(2,1)S(1)}, u32[]{:S(2)}, u32[]{:S(2)}) collective-permute-start(bf16[128,128]{1,0:T(8,128)(2,1)S(1)} %collective-permute-done.1.direct_ref), channel_id=1, source_target_pairs={{0,1},{1,0},{2,3},{3,2},{4,5},{5,4},{6,7},{7,6},{8,9},{9,8},{10,11... | collective-permute-start | bytes 98312 | tf_op jit(solution)/shard_map/ppermute | solution.py:193
  10.8 4.9 %collective-permute-start.3 = (bf16[320,128]{1,0:T(8,128)(2,1)S(1)}, bf16[320,128]{1,0:T(8,128)(2,1)S(1)}, u32[]{:S(2)}, u32[]{:S(2)}) collective-permute-start(bf16[320,128]{1,0:T(8,128)(2,1)S(1)} %get-tuple-element.48), channel_id=1, source_target_pairs={{0,4},{1,9},{2,6},{3,11},{4,0},{5,13},{6,2},{7,15},{8,12},{9,1},{1... | collective-permute-start | bytes 245768 | tf_op jit(solution)/shard_map/ppermute | solution.py:193
  12.0 1.7 %collective-permute-start.4 = (bf16[256,128]{1,0:T(8,128)(2,1)S(1)}, bf16[256,128]{1,0:T(8,128)(2,1)S(1)}, u32[]{:S(2)}, u32[]{:S(2)}) collective-permute-start(bf16[256,128]{1,0:T(8,128)(2,1)S(1)} %get-tuple-element.53), channel_id=1, source_target_pairs={{0,1},{1,0},{2,3},{3,2},{4,5},{5,4},{6,7},{7,6},{8,9},{9,8},{10,11... | collective-permute-start | bytes 196616 | tf_op jit(solution)/shard_map/ppermute | solution.py:193
  13.8 4.0 %collective-permute-start.8 = (bf16[128,128]{1,0:T(8,128)(2,1)S(1)}, bf16[128,128]{1,0:T(8,128)(2,1)S(1)}, u32[]{:S(2)}, u32[]{:S(2)}) collective-permute-start(bf16[128,128]{1,0:T(8,128)(2,1)S(1)} %get-tuple-element.61), channel_id=1, source_target_pairs={{0,4},{1,5},{2,6},{3,7},{4,0},{5,1},{6,2},{7,3},{8,12},{9,13},{10,... | collective-permute-start | bytes 98312 | tf_op jit(solution)/shard_map/ppermute | solution.py:193
  15.7 5.4 %collective-permute-start.5 = (bf16[320,128]{1,0:T(8,128)(2,1)S(1)}, bf16[320,128]{1,0:T(8,128)(2,1)S(1)}, u32[]{:S(2)}, u32[]{:S(2)}) collective-permute-start(bf16[320,128]{1,0:T(8,128)(2,1)S(1)} %add_convert_fusion.1), channel_id=1, source_target_pairs={{0,8},{1,3},{2,10},{3,1},{4,12},{5,7},{6,14},{7,5},{8,0},{9,11},{1... | collective-permute-start | bytes 245768 | tf_op jit(solution)/shard_map/ppermute | solution.py:193
  21.2 4.5 %collective-permute-start.6 = (bf16[320,128]{1,0:T(8,128)(2,1)S(1)}, bf16[320,128]{1,0:T(8,128)(2,1)S(1)}, u32[]{:S(2)}, u32[]{:S(2)}) collective-permute-start(bf16[320,128]{1,0:T(8,128)(2,1)S(1)} %add_convert_fusion.own_ref), channel_id=1, source_target_pairs={{0,2},{1,5},{2,0},{3,7},{4,6},{5,1},{6,4},{7,3},{8,10},{9,13},{10,... | collective-permute-start | bytes 245768 | tf_op jit(solution)/shard_map/ppermute | solution.py:193
  22.7 4.6 %collective-permute-start.9 = (bf16[64,128]{1,0:T(8,128)(2,1)S(1)}, bf16[64,128]{1,0:T(8,128)(2,1)S(1)}, u32[]{:S(2)}, u32[]{:S(2)}) collective-permute-start(bf16[64,128]{1,0:T(8,128)(2,1)S(1)} %get-tuple-element.68), channel_id=1, source_target_pairs={{0,8},{1,9},{2,10},{3,11},{4,12},{5,13},{6,14},{7,15},{8,0},{9,1},... | collective-permute-start | bytes 49160 | tf_op jit(solution)/shard_map/ppermute | solution.py:193
  25.7 1.6 %collective-permute-start.7 = (f32[8,128]{1,0:T(8,128)S(1)}, f32[8,128]{1,0:T(8,128)S(1)}, u32[]{:S(2)}, u32[]{:S(2)}) collective-permute-start(f32[8,128]{1,0:T(8,128)S(1)} %get-tuple-element.59.own_ref), channel_id=1, source_target_pairs={{0,1},{1,0},{2,3},{3,2},{4,5},{5,4},{6,7},{7,6},{8,9},{9,8},{10,11... | collective-permute-start | bytes 12296 | tf_op jit(solution)/shard_map/ppermute | solution.py:193

commit v6 on v5

--- a/solution.py
+++ b/solution.py
@@ -246,7 +246,7 @@
 def local_kernel(
     col_ref, tile_hbm, x_hbm, grad_hbm, bias_hbm, chain_hbm, wq_hbm, wk_hbm, wv_hbm, wg_hbm, wo_hbm,
     x_ref, grad_ref, w_qg_ref, w_kv_ref, bias_out, left_out, right_out, gate_out, gated_grad_out,
-    att_grad_out, tile_ref, chain_ref, wo_ref, bias_ref, sems,
+    tile_ref, chain_ref, wo_ref, bias_ref, sems,
 ):
     scale = HD ** (-0.5)
     width = 2 * TILE
@@ -288,7 +288,6 @@
     right_out[width:, :] = jnp.concatenate([zero_tall, split_cols(att_grad)], axis=1)
     gate_out[...] = gate_t
     gated_grad_out[...] = gated_grad_t
-    att_grad_out[...] = att_grad_f
     for copy in copies[5:]:
         copy.wait()
     chains = chain_ref[...].astype(F32)
@@ -307,7 +306,7 @@
 
 def attention_kernel(
     col_ref, head_ref, x_ref, next_ref, direct_ref, crossed_ref, grad_ref, bias_ref, left_ref, right_ref,
-    gate_ref, gated_grad_ref, att_grad_ref, w_kv_ref,
+    gate_ref, gated_grad_ref, w_kv_ref,
     raw_ref, local_ref, key_value_grad_ref,
     pairs_ref, scores_ref, expo_ref, both_ref,
 ):
@@ -333,25 +332,21 @@
         top = part if top is None else jnp.maximum(top, part)
     top = jnp.max(top, axis=0, keepdims=True)
     total = jnp.zeros((8, width), F32)
+    weighted = jnp.zeros((8, width), F32)
     for block in range(4):
         rows = slice(block * TILE, (block + 1) * TILE)
         expo = jnp.exp(scores_ref[rows, :width] - top)
         scores_ref[rows, :width] = expo
         expo_ref[rows, :] = expo.astype(BF16)
         total = total + jnp.sum(expo.reshape(TILE // 8, 8, width), axis=0)
+        products = expo * scores_ref[rows, width:]
+        weighted = weighted + jnp.sum(products.reshape(TILE // 8, 8, width), axis=0)
     inverse = 1.0 / jnp.sum(total, axis=0, keepdims=True)
+    delta = jnp.sum(weighted, axis=0, keepdims=True) * inverse
     attended_t = join_rows(dot_nn(key_value_t[2 * HD :], expo_ref[...]) * inverse)
     gate_t, gated_grad_t = gate_ref[...], gated_grad_ref[...]
     gated_t = (gate_t * attended_t).astype(BF16)
     gate_logit_t = gated_grad_t * attended_t * gate_t * (1.0 - gate_t)
-    products = att_grad_ref[...] * attended_t
-    delta = jnp.concatenate(
-        [
-            jnp.sum(products[:HD], axis=0, keepdims=True),
-            jnp.sum(products[HD:], axis=0, keepdims=True),
-        ],
-        axis=1,
-    )
     for block in range(4):
         rows = slice(block * TILE, (block + 1) * TILE)
         prob = scores_ref[rows, :width] * inverse
@@ -442,7 +437,7 @@
     head = head_index.reshape(1)
     x_direct = exchange(x, staggered(far_col, end_col))
     x_next = exchange(x, next_col)
-    x, grad, w_qg, w_kv, bias, left, right, gate_t, gated_grad_t, att_grad_t = on_core(
+    x, grad, w_qg, w_kv, bias, left, right, gate_t, gated_grad_t = on_core(
         local_kernel, "local", [SMEM] + [HBM] * 10,
         (
             col, tile_mask, x, out_grad.reshape(TILE, C), pair_bias, chain_ids.reshape(4, TILE),
@@ -451,7 +446,7 @@
         (
             ((TILE, C), BF16), ((TILE, C), BF16), ((2 * width, C), BF16), ((2 * width, C), BF16),
             ((keys, wide), F32), ((C, 2 * wide), BF16), ((2 * wide, C), BF16),
-            ((width, TILE), F32), ((width, TILE), F32), ((width, TILE), F32),
+            ((width, TILE), F32), ((width, TILE), F32),
         ),
         [
             pltpu.SMEM((4, 4), jnp.int32), pltpu.VMEM((4, TILE), jnp.int32),
@@ -463,7 +458,7 @@
     x_crossed = exchange(x_direct, other_head)
     raw, local, key_value_grad = on_core(
         attention_kernel, "attention", [SMEM, SMEM],
-        (col, head, x, x_next, x_direct, x_crossed, grad, bias, left, right, gate_t, gated_grad_t, att_grad_t, w_kv),
+        (col, head, x, x_next, x_direct, x_crossed, grad, bias, left, right, gate_t, gated_grad_t, w_kv),
         (((5 * width, C), BF16), ((TILE, C), BF16), ((keys, C), BF16)),
         [
             pltpu.VMEM((keys, C), BF16), pltpu.VMEM((keys, 2 * wide), F32),

time: 28.3 us -> 28.7 us (1.014)
  waiting for transfers between devices: 9.25 us -> 10.6 us
  starting transfers between devices: 13.9 us -> 13 us
    ppermute x10, waiting for transfers between devices: 9.25 us -> 10.6 us  [exchange(): return lax.ppermute(value, ('col', 'row', 'head'), pairs)]
    ppermute x10, starting transfers between devices: 13.9 us -> 13 us  [exchange(): return lax.ppermute(value, ('col', 'row', 'head'), pairs)]
  transfers between devices with their start and end apart: 10 -> 10, of which waited for: 8 -> 9; matrix products, arithmetic and copies ran while one was open for 0% -> 0% of each run, Pallas kernels for 8% -> 8%
where the time goes in v6:
time: 28.7 us; the launch traced here: 28.5 us
  starting transfers between devices  13 us (45%)
  waiting for transfers between devices  10.6 us (37%)
  Pallas kernels  4.15 us (14%)
  between operations  0.71 us (2%)
    ppermute x10, starting transfers between devices, exchange(): return lax.ppermute(value, ('col', 'row', 'head'), pairs)  13 us
    ppermute x10, waiting for transfers between devices, exchange(): return lax.ppermute(value, ('col', 'row', 'head'), pairs)  10.6 us
    pallas_call x6, Pallas kernels, on_core(): pl.pallas_call(kernel, out_shape=tuple((jax.ShapeDtypeStruct(shape, dtype...  4.15 us
  transfers between devices with their start and end apart: 10, of which 9 were waited for; matrix products, arithmetic and copies ran while one was open for 0% of the time, Pallas kernels for 8%

profile of v6, /device:TPU:0, one launch (start us, length us, event | category | flops | bytes accessed | tf_op | source)
XLA Modules:
  0.0 28.5 jit_solution(16247178277657361348)
XLA Ops:
  0.6 4.1 %collective-permute-start.1 = (bf16[128,128]{1,0:T(8,128)(2,1)}, bf16[128,128]{1,0:T(8,128)(2,1)S(1)}, u32[]{:S(2)}, u32[]{:S(2)}) collective-permute-start(bf16[128,128]{1,0:T(8,128)(2,1)} %bitcast.15), channel_id=1, source_target_pairs={{0,8},{1,13},{2,10},{3,15},{4,12},{5,9},{6,14},{7,11},{8,0},{9,5},... | collective-permute-start | bytes 98312 | tf_op jit(solution)/shard_map/ppermute | solution.py:193
  4.7 1.6 %collective-permute-start = (bf16[128,128]{1,0:T(8,128)(2,1)}, bf16[128,128]{1,0:T(8,128)(2,1)S(1)}, u32[]{:S(2)}, u32[]{:S(2)}) collective-permute-start(bf16[128,128]{1,0:T(8,128)(2,1)} %bitcast.16), channel_id=1, source_target_pairs={{0,4},{1,5},{2,6},{3,7},{4,0},{5,1},{6,2},{7,3},{8,12},{9,13},{10,... | collective-permute-start | bytes 98312 | tf_op jit(solution)/shard_map/ppermute | solution.py:193
  6.3 1.9 %local.1 = (bf16[128,128]{1,0:T(8,128)(2,1)S(1)}, bf16[128,128]{1,0:T(8,128)(2,1)S(1)}, bf16[128,128]{1,0:T(8,128)(2,1)S(1)}, bf16[128,128]{1,0:T(8,128)(2,1)S(1...) custom-call(s32[1]{0:T(128)} %bitcast.col_ref, ...), custom_call_target="tpu_custom_call" | custom-call | flops 1048576 | bytes 262144 | tf_op jit(solution)/shard_map/local/pallas_call | solution.py:412
  8.2 0.0 collective-permute-done.1.direct_ref
  8.2 0.1 collective-permute-start.2
  8.3 0.6 %collective-permute-done.next_ref = bf16[128,128]{1,0:T(8,128)(2,1)S(1)} collective-permute-done((bf16[128,128]{1,0:T(8,128)(2,1)}, bf16[128,128]{1,0:T(8,128)(2,1)S(1)}, u32[]{:S(2)}, u32[]{:S(2)}) %collective-permute-start) | collective-permute-done | bytes 32800 | tf_op jit(solution)/shard_map/ppermute | solution.py:193
  8.9 0.6 %collective-permute-done.2.crossed_ref = bf16[128,128]{1,0:T(8,128)(2,1)S(1)} collective-permute-done((bf16[128,128]{1,0:T(8,128)(2,1)S(1)}, bf16[128,128]{1,0:T(8,128)(2,1)S(1)}, u32[]{:S(2)}, u32[]{:S(2)}) %collective-permute-start.2) | collective-permute-done | bytes 32800 | tf_op jit(solution)/shard_map/ppermute | solution.py:193
  9.5 1.2 %attention.1 = (bf16[320,128]{1,0:T(8,128)(2,1)S(1)}, bf16[128,128]{1,0:T(8,128)(2,1)S(1)}, bf16[512,128]{1,0:T(8,128)(2,1)S(1)}) custom-call(s32[1]{0:T(128)} %bitcast.col_ref, s32[1]{0:T(128)} %bitcast.1.head_ref, bf16[128,128]{1,0:T(8,128)(2,1)S(1)} %get-tuple-element.36.x_ref, bf16[128,128]{1,0:T(8,128)(2,1)S(1)} %collective-permute-done.next_ref, ...), custom_call_target="tpu_custom_call" | custom-call | flops 1048576 | bytes 262144 | tf_op jit(solution)/shard_map/attention/pallas_call | solution.py:412
  10.7 1.0 %collective-permute-start.3 = (bf16[320,128]{1,0:T(8,128)(2,1)S(1)}, bf16[320,128]{1,0:T(8,128)(2,1)S(1)}, u32[]{:S(2)}, u32[]{:S(2)}) collective-permute-start(bf16[320,128]{1,0:T(8,128)(2,1)S(1)} %get-tuple-element.46), channel_id=1, source_target_pairs={{0,4},{1,9},{2,6},{3,11},{4,0},{5,13},{6,2},{7,15},{8,12},{9,1},{1... | collective-permute-start | bytes 245768 | tf_op jit(solution)/shard_map/ppermute | solution.py:193
  11.7 0.2 parts.1
  12.0 0.8 %collective-permute-start.4 = (bf16[256,128]{1,0:T(8,128)(2,1)S(1)}, bf16[256,128]{1,0:T(8,128)(2,1)S(1)}, u32[]{:S(2)}, u32[]{:S(2)}) collective-permute-start(bf16[256,128]{1,0:T(8,128)(2,1)S(1)} %get-tuple-element.51), channel_id=1, source_target_pairs={{0,1},{1,0},{2,3},{3,2},{4,5},{5,4},{6,7},{7,6},{8,9},{9,8},{10,11... | collective-permute-start | bytes 196616 | tf_op jit(solution)/shard_map/ppermute | solution.py:193
  12.8 0.9 %collective-permute-done.4.other_ref = bf16[256,128]{1,0:T(8,128)(2,1)S(1)} collective-permute-done((bf16[256,128]{1,0:T(8,128)(2,1)S(1)}, bf16[256,128]{1,0:T(8,128)(2,1)S(1)}, u32[]{:S(2)}, u32[]{:S(2)}) %collective-permute-start.4) | collective-permute-done | bytes 65568 | tf_op jit(solution)/shard_map/ppermute | solution.py:193
  13.7 1.8 %collective-permute-start.8 = (bf16[128,128]{1,0:T(8,128)(2,1)S(1)}, bf16[128,128]{1,0:T(8,128)(2,1)S(1)}, u32[]{:S(2)}, u32[]{:S(2)}) collective-permute-start(bf16[128,128]{1,0:T(8,128)(2,1)S(1)} %get-tuple-element.59), channel_id=1, source_target_pairs={{0,4},{1,5},{2,6},{3,7},{4,0},{5,1},{6,2},{7,3},{8,12},{9,13},{10,... | collective-permute-start | bytes 98312 | tf_op jit(solution)/shard_map/ppermute | solution.py:193
  15.5 0.2 collective-permute-done.3
  15.7 1.5 %collective-permute-start.5 = (bf16[320,128]{1,0:T(8,128)(2,1)S(1)}, bf16[320,128]{1,0:T(8,128)(2,1)S(1)}, u32[]{:S(2)}, u32[]{:S(2)}) collective-permute-start(bf16[320,128]{1,0:T(8,128)(2,1)S(1)} %add_convert_fusion.1), channel_id=1, source_target_pairs={{0,8},{1,3},{2,10},{3,1},{4,12},{5,7},{6,14},{7,5},{8,0},{9,11},{1... | collective-permute-start | bytes 245768 | tf_op jit(solution)/shard_map/ppermute | solution.py:193
  17.2 0.5 %collective-permute-done.8 = bf16[128,128]{1,0:T(8,128)(2,1)S(1)} collective-permute-done((bf16[128,128]{1,0:T(8,128)(2,1)S(1)}, bf16[128,128]{1,0:T(8,128)(2,1)S(1)}, u32[]{:S(2)}, u32[]{:S(2)}) %collective-permute-start.8) | collective-permute-done | bytes 32800 | tf_op jit(solution)/shard_map/ppermute | solution.py:193
  17.7 4.3 %collective-permute-done.5 = bf16[320,128]{1,0:T(8,128)(2,1)S(1)} collective-permute-done((bf16[320,128]{1,0:T(8,128)(2,1)S(1)}, bf16[320,128]{1,0:T(8,128)(2,1)S(1)}, u32[]{:S(2)}, u32[]{:S(2)}) %collective-permute-start.5) | collective-permute-done | bytes 81952 | tf_op jit(solution)/shard_map/ppermute | solution.py:193
  22.0 0.7 %collective-permute-start.6 = (bf16[320,128]{1,0:T(8,128)(2,1)S(1)}, bf16[320,128]{1,0:T(8,128)(2,1)S(1)}, u32[]{:S(2)}, u32[]{:S(2)}) collective-permute-start(bf16[320,128]{1,0:T(8,128)(2,1)S(1)} %add_convert_fusion.own_ref), channel_id=1, source_target_pairs={{0,2},{1,5},{2,0},{3,7},{4,6},{5,1},{6,4},{7,3},{8,10},{9,13},{10,... | collective-permute-start | bytes 245768 | tf_op jit(solution)/shard_map/ppermute | solution.py:193
  22.7 1.4 %collective-permute-start.9 = (bf16[64,128]{1,0:T(8,128)(2,1)S(1)}, bf16[64,128]{1,0:T(8,128)(2,1)S(1)}, u32[]{:S(2)}, u32[]{:S(2)}) collective-permute-start(bf16[64,128]{1,0:T(8,128)(2,1)S(1)} %get-tuple-element.66), channel_id=1, source_target_pairs={{0,8},{1,9},{2,10},{3,11},{4,12},{5,13},{6,14},{7,15},{8,0},{9,1},... | collective-permute-start | bytes 49160 | tf_op jit(solution)/shard_map/ppermute | solution.py:193
  24.1 2.4 %collective-permute-done.6.other_ref = bf16[320,128]{1,0:T(8,128)(2,1)S(1)} collective-permute-done((bf16[320,128]{1,0:T(8,128)(2,1)S(1)}, bf16[320,128]{1,0:T(8,128)(2,1)S(1)}, u32[]{:S(2)}, u32[]{:S(2)}) %collective-permute-start.6) | collective-permute-done | bytes 81952 | tf_op jit(solution)/shard_map/ppermute | solution.py:193
  26.6 0.1 collective-permute-start.7
  26.6 0.7 %collective-permute-done.9.pair_other_ref = bf16[64,128]{1,0:T(8,128)(2,1)S(1)} collective-permute-done((bf16[64,128]{1,0:T(8,128)(2,1)S(1)}, bf16[64,128]{1,0:T(8,128)(2,1)S(1)}, u32[]{:S(2)}, u32[]{:S(2)}) %collective-permute-start.9) | collective-permute-done | bytes 16416 | tf_op jit(solution)/shard_map/ppermute | solution.py:193
  27.3 0.5 %collective-permute-done.7.other_ref = f32[8,128]{1,0:T(8,128)S(1)} collective-permute-done((f32[8,128]{1,0:T(8,128)S(1)}, f32[8,128]{1,0:T(8,128)S(1)}, u32[]{:S(2)}, u32[]{:S(2)}) %collective-permute-start.7) | collective-permute-done | bytes 4128 | tf_op jit(solution)/shard_map/ppermute | solution.py:193
  27.8 0.8 %clip.1 = (f32[64,128]{1,0:T(8,128)}, f32[64,128]{1,0:T(8,128)}, f32[64,128]{1,0:T(8,128)}, f32[64,128]{1,0:T(8,128)}, f32[64,128]{1,0:T(8,128)}, /*index=5*/bf16[64,128]{1,0:T(8,128)(2,1)}) custom-call(f32[320,128]{1,0:T(8,128)S(1)} %get-tuple-element.56.total_ref, f32[8,128]{1,0:T(8,128)S(1)} %get-tuple-element.57.own_ref, ...), custom_call_target="tpu_custom_call" | custom-call | flops 1048576 | bytes 262144 | tf_op jit(solution)/shard_map/clip/pallas_call | solution.py:412
  (6 shorter events, 0.1 us)
Async XLA Ops:
  0.6 7.6 %collective-permute-start.1 = (bf16[128,128]{1,0:T(8,128)(2,1)}, bf16[128,128]{1,0:T(8,128)(2,1)S(1)}, u32[]{:S(2)}, u32[]{:S(2)}) collective-permute-start(bf16[128,128]{1,0:T(8,128)(2,1)} %bitcast.15), channel_id=1, source_target_pairs={{0,8},{1,13},{2,10},{3,15},{4,12},{5,9},{6,14},{7,11},{8,0},{9,5},... | collective-permute-start | bytes 98312 | tf_op jit(solution)/shard_map/ppermute | solution.py:193
  4.7 4.1 %collective-permute-start = (bf16[128,128]{1,0:T(8,128)(2,1)}, bf16[128,128]{1,0:T(8,128)(2,1)S(1)}, u32[]{:S(2)}, u32[]{:S(2)}) collective-permute-start(bf16[128,128]{1,0:T(8,128)(2,1)} %bitcast.16), channel_id=1, source_target_pairs={{0,4},{1,5},{2,6},{3,7},{4,0},{5,1},{6,2},{7,3},{8,12},{9,13},{10,... | collective-permute-start | bytes 98312 | tf_op jit(solution)/shard_map/ppermute | solution.py:193
  8.2 1.3 %collective-permute-start.2 = (bf16[128,128]{1,0:T(8,128)(2,1)S(1)}, bf16[128,128]{1,0:T(8,128)(2,1)S(1)}, u32[]{:S(2)}, u32[]{:S(2)}) collective-permute-start(bf16[128,128]{1,0:T(8,128)(2,1)S(1)} %collective-permute-done.1.direct_ref), channel_id=1, source_target_pairs={{0,1},{1,0},{2,3},{3,2},{4,5},{5,4},{6,7},{7,6},{8,9},{9,8},{10,11... | collective-permute-start | bytes 98312 | tf_op jit(solution)/shard_map/ppermute | solution.py:193
  10.7 4.9 %collective-permute-start.3 = (bf16[320,128]{1,0:T(8,128)(2,1)S(1)}, bf16[320,128]{1,0:T(8,128)(2,1)S(1)}, u32[]{:S(2)}, u32[]{:S(2)}) collective-permute-start(bf16[320,128]{1,0:T(8,128)(2,1)S(1)} %get-tuple-element.46), channel_id=1, source_target_pairs={{0,4},{1,9},{2,6},{3,11},{4,0},{5,13},{6,2},{7,15},{8,12},{9,1},{1... | collective-permute-start | bytes 245768 | tf_op jit(solution)/shard_map/ppermute | solution.py:193
  12.0 1.7 %collective-permute-start.4 = (bf16[256,128]{1,0:T(8,128)(2,1)S(1)}, bf16[256,128]{1,0:T(8,128)(2,1)S(1)}, u32[]{:S(2)}, u32[]{:S(2)}) collective-permute-start(bf16[256,128]{1,0:T(8,128)(2,1)S(1)} %get-tuple-element.51), channel_id=1, source_target_pairs={{0,1},{1,0},{2,3},{3,2},{4,5},{5,4},{6,7},{7,6},{8,9},{9,8},{10,11... | collective-permute-start | bytes 196616 | tf_op jit(solution)/shard_map/ppermute | solution.py:193
  13.7 4.0 %collective-permute-start.8 = (bf16[128,128]{1,0:T(8,128)(2,1)S(1)}, bf16[128,128]{1,0:T(8,128)(2,1)S(1)}, u32[]{:S(2)}, u32[]{:S(2)}) collective-permute-start(bf16[128,128]{1,0:T(8,128)(2,1)S(1)} %get-tuple-element.59), channel_id=1, source_target_pairs={{0,4},{1,5},{2,6},{3,7},{4,0},{5,1},{6,2},{7,3},{8,12},{9,13},{10,... | collective-permute-start | bytes 98312 | tf_op jit(solution)/shard_map/ppermute | solution.py:193
  15.7 6.3 %collective-permute-start.5 = (bf16[320,128]{1,0:T(8,128)(2,1)S(1)}, bf16[320,128]{1,0:T(8,128)(2,1)S(1)}, u32[]{:S(2)}, u32[]{:S(2)}) collective-permute-start(bf16[320,128]{1,0:T(8,128)(2,1)S(1)} %add_convert_fusion.1), channel_id=1, source_target_pairs={{0,8},{1,3},{2,10},{3,1},{4,12},{5,7},{6,14},{7,5},{8,0},{9,11},{1... | collective-permute-start | bytes 245768 | tf_op jit(solution)/shard_map/ppermute | solution.py:193
  22.0 4.5 %collective-permute-start.6 = (bf16[320,128]{1,0:T(8,128)(2,1)S(1)}, bf16[320,128]{1,0:T(8,128)(2,1)S(1)}, u32[]{:S(2)}, u32[]{:S(2)}) collective-permute-start(bf16[320,128]{1,0:T(8,128)(2,1)S(1)} %add_convert_fusion.own_ref), channel_id=1, source_target_pairs={{0,2},{1,5},{2,0},{3,7},{4,6},{5,1},{6,4},{7,3},{8,10},{9,13},{10,... | collective-permute-start | bytes 245768 | tf_op jit(solution)/shard_map/ppermute | solution.py:193
  22.7 4.6 %collective-permute-start.9 = (bf16[64,128]{1,0:T(8,128)(2,1)S(1)}, bf16[64,128]{1,0:T(8,128)(2,1)S(1)}, u32[]{:S(2)}, u32[]{:S(2)}) collective-permute-start(bf16[64,128]{1,0:T(8,128)(2,1)S(1)} %get-tuple-element.66), channel_id=1, source_target_pairs={{0,8},{1,9},{2,10},{3,11},{4,12},{5,13},{6,14},{7,15},{8,0},{9,1},... | collective-permute-start | bytes 49160 | tf_op jit(solution)/shard_map/ppermute | solution.py:193
  26.6 1.2 %collective-permute-start.7 = (f32[8,128]{1,0:T(8,128)S(1)}, f32[8,128]{1,0:T(8,128)S(1)}, u32[]{:S(2)}, u32[]{:S(2)}) collective-permute-start(f32[8,128]{1,0:T(8,128)S(1)} %get-tuple-element.57.own_ref), channel_id=1, source_target_pairs={{0,1},{1,0},{2,3},{3,2},{4,5},{5,4},{6,7},{7,6},{8,9},{9,8},{10,11... | collective-permute-start | bytes 12296 | tf_op jit(solution)/shard_map/ppermute | solution.py:193

commit v7 on v6

--- a/solution.py
+++ b/solution.py
@@ -474,7 +474,7 @@
         (((wide, C), F32), ((wide, C), BF16)), [pltpu.VMEM((keys, C), F32)],
     )
     half = TILE // 2
-    raw = summed(raw, exchange(raw, staggered(next_col, far_col)))
+    raw = summed(raw, exchange(raw, staggered(other_row, next_col)))
     given = exchange(send, other_head)
     keep, send = on_core(
         fold_kernel, "fold_heads", [], (keep, given), (((TILE, C), F32), ((TILE, C), BF16)),
@@ -487,7 +487,7 @@
     raw, keep = lax.optimization_barrier((raw, keep))
     given = exchange(send, far_col)
     keep = keep + early.astype(F32)
-    last = exchange(raw, staggered(other_row, next_col))
+    last = exchange(raw, staggered(next_col, far_col))
     total, squares = on_core(
         squares_kernel, "squares", [], (raw, last), (((5 * width, C), F32), ((8, C), F32)),
     )

time: 28.7 us -> 28.3 us (0.986)
  waiting for transfers between devices: 10.6 us -> 8.88 us
  starting transfers between devices: 13 us -> 14.3 us
    ppermute x10, waiting for transfers between devices: 10.6 us -> 8.88 us  [exchange(): return lax.ppermute(value, ('col', 'row', 'head'), pairs)]
    ppermute x10, starting transfers between devices: 13 us -> 14.3 us  [exchange(): return lax.ppermute(value, ('col', 'row', 'head'), pairs)]
where the time goes in v7:
time: 28.3 us; the launch traced here: 28.1 us
  starting transfers between devices  14.3 us (51%)
  waiting for transfers between devices  8.88 us (31%)
  Pallas kernels  4.15 us (15%)
  between operations  0.72 us (3%)
    ppermute x10, starting transfers between devices, exchange(): return lax.ppermute(value, ('col', 'row', 'head'), pairs)  14.3 us
    ppermute x10, waiting for transfers between devices, exchange(): return lax.ppermute(value, ('col', 'row', 'head'), pairs)  8.88 us
    pallas_call x6, Pallas kernels, on_core(): pl.pallas_call(kernel, out_shape=tuple((jax.ShapeDtypeStruct(shape, dtype...  4.15 us
  transfers between devices with their start and end apart: 10, of which 9 were waited for; matrix products, arithmetic and copies ran while one was open for 0% of the time, Pallas kernels for 8%

profile of v7, /device:TPU:0, one launch (start us, length us, event | category | flops | bytes accessed | tf_op | source)
XLA Modules:
  0.0 28.1 jit_solution(2811586662530431517)
XLA Ops:
  0.6 4.1 %collective-permute-start.1 = (bf16[128,128]{1,0:T(8,128)(2,1)}, bf16[128,128]{1,0:T(8,128)(2,1)S(1)}, u32[]{:S(2)}, u32[]{:S(2)}) collective-permute-start(bf16[128,128]{1,0:T(8,128)(2,1)} %bitcast.15), channel_id=1, source_target_pairs={{0,8},{1,13},{2,10},{3,15},{4,12},{5,9},{6,14},{7,11},{8,0},{9,5},... | collective-permute-start | bytes 98312 | tf_op jit(solution)/shard_map/ppermute | solution.py:193
  4.7 1.6 %collective-permute-start = (bf16[128,128]{1,0:T(8,128)(2,1)}, bf16[128,128]{1,0:T(8,128)(2,1)S(1)}, u32[]{:S(2)}, u32[]{:S(2)}) collective-permute-start(bf16[128,128]{1,0:T(8,128)(2,1)} %bitcast.16), channel_id=1, source_target_pairs={{0,4},{1,5},{2,6},{3,7},{4,0},{5,1},{6,2},{7,3},{8,12},{9,13},{10,... | collective-permute-start | bytes 98312 | tf_op jit(solution)/shard_map/ppermute | solution.py:193
  6.3 1.9 %local.1 = (bf16[128,128]{1,0:T(8,128)(2,1)S(1)}, bf16[128,128]{1,0:T(8,128)(2,1)S(1)}, bf16[128,128]{1,0:T(8,128)(2,1)S(1)}, bf16[128,128]{1,0:T(8,128)(2,1)S(1...) custom-call(s32[1]{0:T(128)} %bitcast.col_ref, ...), custom_call_target="tpu_custom_call" | custom-call | flops 1048576 | bytes 262144 | tf_op jit(solution)/shard_map/local/pallas_call | solution.py:412
  8.2 0.0 collective-permute-done.1.direct_ref
  8.2 0.1 collective-permute-start.2
  8.3 0.6 %collective-permute-done.next_ref = bf16[128,128]{1,0:T(8,128)(2,1)S(1)} collective-permute-done((bf16[128,128]{1,0:T(8,128)(2,1)}, bf16[128,128]{1,0:T(8,128)(2,1)S(1)}, u32[]{:S(2)}, u32[]{:S(2)}) %collective-permute-start) | collective-permute-done | bytes 32800 | tf_op jit(solution)/shard_map/ppermute | solution.py:193
  8.9 0.6 %collective-permute-done.2.crossed_ref = bf16[128,128]{1,0:T(8,128)(2,1)S(1)} collective-permute-done((bf16[128,128]{1,0:T(8,128)(2,1)S(1)}, bf16[128,128]{1,0:T(8,128)(2,1)S(1)}, u32[]{:S(2)}, u32[]{:S(2)}) %collective-permute-start.2) | collective-permute-done | bytes 32800 | tf_op jit(solution)/shard_map/ppermute | solution.py:193
  9.5 1.2 %attention.1 = (bf16[320,128]{1,0:T(8,128)(2,1)S(1)}, bf16[128,128]{1,0:T(8,128)(2,1)S(1)}, bf16[512,128]{1,0:T(8,128)(2,1)S(1)}) custom-call(s32[1]{0:T(128)} %bitcast.col_ref, s32[1]{0:T(128)} %bitcast.1.head_ref, bf16[128,128]{1,0:T(8,128)(2,1)S(1)} %get-tuple-element.36.x_ref, bf16[128,128]{1,0:T(8,128)(2,1)S(1)} %collective-permute-done.next_ref, ...), custom_call_target="tpu_custom_call" | custom-call | flops 1048576 | bytes 262144 | tf_op jit(solution)/shard_map/attention/pallas_call | solution.py:412
  10.7 1.6 %collective-permute-start.3 = (bf16[320,128]{1,0:T(8,128)(2,1)S(1)}, bf16[320,128]{1,0:T(8,128)(2,1)S(1)}, u32[]{:S(2)}, u32[]{:S(2)}) collective-permute-start(bf16[320,128]{1,0:T(8,128)(2,1)S(1)} %get-tuple-element.46), channel_id=1, source_target_pairs={{0,2},{1,5},{2,0},{3,7},{4,6},{5,1},{6,4},{7,3},{8,10},{9,13},{10,... | collective-permute-start | bytes 245768 | tf_op jit(solution)/shard_map/ppermute | solution.py:193
  12.3 0.2 parts.1
  12.5 0.1 collective-permute-start.4
  12.6 1.2 %collective-permute-done.4.other_ref = bf16[256,128]{1,0:T(8,128)(2,1)S(1)} collective-permute-done((bf16[256,128]{1,0:T(8,128)(2,1)S(1)}, bf16[256,128]{1,0:T(8,128)(2,1)S(1)}, u32[]{:S(2)}, u32[]{:S(2)}) %collective-permute-start.4) | collective-permute-done | bytes 65568 | tf_op jit(solution)/shard_map/ppermute | solution.py:193
  13.8 1.0 %collective-permute-start.8 = (bf16[128,128]{1,0:T(8,128)(2,1)S(1)}, bf16[128,128]{1,0:T(8,128)(2,1)S(1)}, u32[]{:S(2)}, u32[]{:S(2)}) collective-permute-start(bf16[128,128]{1,0:T(8,128)(2,1)S(1)} %get-tuple-element.59), channel_id=1, source_target_pairs={{0,4},{1,5},{2,6},{3,7},{4,0},{5,1},{6,2},{7,3},{8,12},{9,13},{10,... | collective-permute-start | bytes 98312 | tf_op jit(solution)/shard_map/ppermute | solution.py:193
  14.9 0.4 %collective-permute-done.3 = bf16[320,128]{1,0:T(8,128)(2,1)S(1)} collective-permute-done((bf16[320,128]{1,0:T(8,128)(2,1)S(1)}, bf16[320,128]{1,0:T(8,128)(2,1)S(1)}, u32[]{:S(2)}, u32[]{:S(2)}) %collective-permute-start.3) | collective-permute-done | bytes 81952 | tf_op jit(solution)/shard_map/ppermute | solution.py:193
  15.3 2.3 %collective-permute-start.5 = (bf16[320,128]{1,0:T(8,128)(2,1)S(1)}, bf16[320,128]{1,0:T(8,128)(2,1)S(1)}, u32[]{:S(2)}, u32[]{:S(2)}) collective-permute-start(bf16[320,128]{1,0:T(8,128)(2,1)S(1)} %add_convert_fusion.1), channel_id=1, source_target_pairs={{0,8},{1,3},{2,10},{3,1},{4,12},{5,7},{6,14},{7,5},{8,0},{9,11},{1... | collective-permute-start | bytes 245768 | tf_op jit(solution)/shard_map/ppermute | solution.py:193
  17.5 0.3 %collective-permute-done.8 = bf16[128,128]{1,0:T(8,128)(2,1)S(1)} collective-permute-done((bf16[128,128]{1,0:T(8,128)(2,1)S(1)}, bf16[128,128]{1,0:T(8,128)(2,1)S(1)}, u32[]{:S(2)}, u32[]{:S(2)}) %collective-permute-start.8) | collective-permute-done | bytes 32800 | tf_op jit(solution)/shard_map/ppermute | solution.py:193
  17.8 3.7 %collective-permute-done.5 = bf16[320,128]{1,0:T(8,128)(2,1)S(1)} collective-permute-done((bf16[320,128]{1,0:T(8,128)(2,1)S(1)}, bf16[320,128]{1,0:T(8,128)(2,1)S(1)}, u32[]{:S(2)}, u32[]{:S(2)}) %collective-permute-start.5) | collective-permute-done | bytes 81952 | tf_op jit(solution)/shard_map/ppermute | solution.py:193
  21.6 0.2 collective-permute-start.6
  21.8 3.3 %collective-permute-start.9 = (bf16[64,128]{1,0:T(8,128)(2,1)S(1)}, bf16[64,128]{1,0:T(8,128)(2,1)S(1)}, u32[]{:S(2)}, u32[]{:S(2)}) collective-permute-start(bf16[64,128]{1,0:T(8,128)(2,1)S(1)} %get-tuple-element.66), channel_id=1, source_target_pairs={{0,8},{1,9},{2,10},{3,11},{4,12},{5,13},{6,14},{7,15},{8,0},{9,1},... | collective-permute-start | bytes 49160 | tf_op jit(solution)/shard_map/ppermute | solution.py:193
  25.2 0.9 %collective-permute-done.6.other_ref = bf16[320,128]{1,0:T(8,128)(2,1)S(1)} collective-permute-done((bf16[320,128]{1,0:T(8,128)(2,1)S(1)}, bf16[320,128]{1,0:T(8,128)(2,1)S(1)}, u32[]{:S(2)}, u32[]{:S(2)}) %collective-permute-start.6) | collective-permute-done | bytes 81952 | tf_op jit(solution)/shard_map/ppermute | solution.py:193
  26.1 0.1 collective-permute-start.7
  26.2 0.7 %collective-permute-done.9.pair_other_ref = bf16[64,128]{1,0:T(8,128)(2,1)S(1)} collective-permute-done((bf16[64,128]{1,0:T(8,128)(2,1)S(1)}, bf16[64,128]{1,0:T(8,128)(2,1)S(1)}, u32[]{:S(2)}, u32[]{:S(2)}) %collective-permute-start.9) | collective-permute-done | bytes 16416 | tf_op jit(solution)/shard_map/ppermute | solution.py:193
  26.9 0.5 %collective-permute-done.7.other_ref = f32[8,128]{1,0:T(8,128)S(1)} collective-permute-done((f32[8,128]{1,0:T(8,128)S(1)}, f32[8,128]{1,0:T(8,128)S(1)}, u32[]{:S(2)}, u32[]{:S(2)}) %collective-permute-start.7) | collective-permute-done | bytes 4128 | tf_op jit(solution)/shard_map/ppermute | solution.py:193
  27.4 0.8 %clip.1 = (f32[64,128]{1,0:T(8,128)}, f32[64,128]{1,0:T(8,128)}, f32[64,128]{1,0:T(8,128)}, f32[64,128]{1,0:T(8,128)}, f32[64,128]{1,0:T(8,128)}, /*index=5*/bf16[64,128]{1,0:T(8,128)(2,1)}) custom-call(f32[320,128]{1,0:T(8,128)S(1)} %get-tuple-element.56.total_ref, f32[8,128]{1,0:T(8,128)S(1)} %get-tuple-element.57.own_ref, ...), custom_call_target="tpu_custom_call" | custom-call | flops 1048576 | bytes 262144 | tf_op jit(solution)/shard_map/clip/pallas_call | solution.py:412
  (6 shorter events, 0.1 us)
Async XLA Ops:
  0.6 7.6 %collective-permute-start.1 = (bf16[128,128]{1,0:T(8,128)(2,1)}, bf16[128,128]{1,0:T(8,128)(2,1)S(1)}, u32[]{:S(2)}, u32[]{:S(2)}) collective-permute-start(bf16[128,128]{1,0:T(8,128)(2,1)} %bitcast.15), channel_id=1, source_target_pairs={{0,8},{1,13},{2,10},{3,15},{4,12},{5,9},{6,14},{7,11},{8,0},{9,5},... | collective-permute-start | bytes 98312 | tf_op jit(solution)/shard_map/ppermute | solution.py:193
  4.7 4.1 %collective-permute-start = (bf16[128,128]{1,0:T(8,128)(2,1)}, bf16[128,128]{1,0:T(8,128)(2,1)S(1)}, u32[]{:S(2)}, u32[]{:S(2)}) collective-permute-start(bf16[128,128]{1,0:T(8,128)(2,1)} %bitcast.16), channel_id=1, source_target_pairs={{0,4},{1,5},{2,6},{3,7},{4,0},{5,1},{6,2},{7,3},{8,12},{9,13},{10,... | collective-permute-start | bytes 98312 | tf_op jit(solution)/shard_map/ppermute | solution.py:193
  8.2 1.3 %collective-permute-start.2 = (bf16[128,128]{1,0:T(8,128)(2,1)S(1)}, bf16[128,128]{1,0:T(8,128)(2,1)S(1)}, u32[]{:S(2)}, u32[]{:S(2)}) collective-permute-start(bf16[128,128]{1,0:T(8,128)(2,1)S(1)} %collective-permute-done.1.direct_ref), channel_id=1, source_target_pairs={{0,1},{1,0},{2,3},{3,2},{4,5},{5,4},{6,7},{7,6},{8,9},{9,8},{10,11... | collective-permute-start | bytes 98312 | tf_op jit(solution)/shard_map/ppermute | solution.py:193
  10.7 4.5 %collective-permute-start.3 = (bf16[320,128]{1,0:T(8,128)(2,1)S(1)}, bf16[320,128]{1,0:T(8,128)(2,1)S(1)}, u32[]{:S(2)}, u32[]{:S(2)}) collective-permute-start(bf16[320,128]{1,0:T(8,128)(2,1)S(1)} %get-tuple-element.46), channel_id=1, source_target_pairs={{0,2},{1,5},{2,0},{3,7},{4,6},{5,1},{6,4},{7,3},{8,10},{9,13},{10,... | collective-permute-start | bytes 245768 | tf_op jit(solution)/shard_map/ppermute | solution.py:193
  12.5 1.3 %collective-permute-start.4 = (bf16[256,128]{1,0:T(8,128)(2,1)S(1)}, bf16[256,128]{1,0:T(8,128)(2,1)S(1)}, u32[]{:S(2)}, u32[]{:S(2)}) collective-permute-start(bf16[256,128]{1,0:T(8,128)(2,1)S(1)} %get-tuple-element.51), channel_id=1, source_target_pairs={{0,1},{1,0},{2,3},{3,2},{4,5},{5,4},{6,7},{7,6},{8,9},{9,8},{10,11... | collective-permute-start | bytes 196616 | tf_op jit(solution)/shard_map/ppermute | solution.py:193
  13.8 4.0 %collective-permute-start.8 = (bf16[128,128]{1,0:T(8,128)(2,1)S(1)}, bf16[128,128]{1,0:T(8,128)(2,1)S(1)}, u32[]{:S(2)}, u32[]{:S(2)}) collective-permute-start(bf16[128,128]{1,0:T(8,128)(2,1)S(1)} %get-tuple-element.59), channel_id=1, source_target_pairs={{0,4},{1,5},{2,6},{3,7},{4,0},{5,1},{6,2},{7,3},{8,12},{9,13},{10,... | collective-permute-start | bytes 98312 | tf_op jit(solution)/shard_map/ppermute | solution.py:193
  15.3 6.3 %collective-permute-start.5 = (bf16[320,128]{1,0:T(8,128)(2,1)S(1)}, bf16[320,128]{1,0:T(8,128)(2,1)S(1)}, u32[]{:S(2)}, u32[]{:S(2)}) collective-permute-start(bf16[320,128]{1,0:T(8,128)(2,1)S(1)} %add_convert_fusion.1), channel_id=1, source_target_pairs={{0,8},{1,3},{2,10},{3,1},{4,12},{5,7},{6,14},{7,5},{8,0},{9,11},{1... | collective-permute-start | bytes 245768 | tf_op jit(solution)/shard_map/ppermute | solution.py:193
  21.6 4.5 %collective-permute-start.6 = (bf16[320,128]{1,0:T(8,128)(2,1)S(1)}, bf16[320,128]{1,0:T(8,128)(2,1)S(1)}, u32[]{:S(2)}, u32[]{:S(2)}) collective-permute-start(bf16[320,128]{1,0:T(8,128)(2,1)S(1)} %add_convert_fusion.own_ref), channel_id=1, source_target_pairs={{0,4},{1,9},{2,6},{3,11},{4,0},{5,13},{6,2},{7,15},{8,12},{9,1},{1... | collective-permute-start | bytes 245768 | tf_op jit(solution)/shard_map/ppermute | solution.py:193
  21.8 5.1 %collective-permute-start.9 = (bf16[64,128]{1,0:T(8,128)(2,1)S(1)}, bf16[64,128]{1,0:T(8,128)(2,1)S(1)}, u32[]{:S(2)}, u32[]{:S(2)}) collective-permute-start(bf16[64,128]{1,0:T(8,128)(2,1)S(1)} %get-tuple-element.66), channel_id=1, source_target_pairs={{0,8},{1,9},{2,10},{3,11},{4,12},{5,13},{6,14},{7,15},{8,0},{9,1},... | collective-permute-start | bytes 49160 | tf_op jit(solution)/shard_map/ppermute | solution.py:193
  26.1 1.2 %collective-permute-start.7 = (f32[8,128]{1,0:T(8,128)S(1)}, f32[8,128]{1,0:T(8,128)S(1)}, u32[]{:S(2)}, u32[]{:S(2)}) collective-permute-start(f32[8,128]{1,0:T(8,128)S(1)} %get-tuple-element.57.own_ref), channel_id=1, source_target_pairs={{0,1},{1,0},{2,3},{3,2},{4,5},{5,4},{6,7},{7,6},{8,9},{9,8},{10,11... | collective-permute-start | bytes 12296 | tf_op jit(solution)/shard_map/ppermute | solution.py:193
